TPU v7x, 32 devices: a whole 2x2x4 slice. The times are simulated.
32 devices in a mesh: fsdp: 4 (over z), ctx: 2 (over x), tp: 4 (over y, core).
Axes of the slice: x: 2, y: 2, z: 4, core: 2. Of those that a mesh axis runs over, the one named last changes fastest.
Arguments:
- tokens: bfloat16 [12288, 1024], P(('fsdp', 'ctx')), may hold values from -6 to 6
- out_grad: bfloat16 [12288, 1024], P(('fsdp', 'ctx')), may hold values from -6 to 6
- doc_ids: int32 [12288], P('fsdp'), may hold values from 0 to 23, never falling along the last dimension, each value on 1 to 1024 neighbouring positions
- block_ids: int32 [12288], P('fsdp'), may hold values from 0 to 63, never falling along the last dimension, each value on 1 to 256 neighbouring positions
- expert_ids: int32 [12288, 8], P(('fsdp', 'ctx')), may hold values from 0 to 31, all different within a row; in each aligned block of 1536 rows (0 to 1535, 1536 to 3071, ...) at most 576 rows name the same one
- norm1_gain: bfloat16 [1024], P('fsdp'), may hold values from 0.5 to 1.5
- w_query: bfloat16 [1024, 1024], P('fsdp', 'tp'), may hold values from -0.1875 to 0.1875
- w_key: bfloat16 [1024, 512], P('fsdp', 'tp'), may hold values from -0.1875 to 0.1875
- w_value: bfloat16 [1024, 512], P('fsdp', 'tp'), may hold values from -0.1875 to 0.1875
- w_out: bfloat16 [1024, 1024], P('tp', 'fsdp'), may hold values from -2 to 2
- norm2_gain: bfloat16 [1024], P('fsdp'), may hold values from 0.5 to 1.5
- w_router: bfloat16 [1024, 32], P('fsdp'), may hold values from -0.09375 to 0.09375
- w_gate: bfloat16 [32, 1024, 512], P(None, 'fsdp', 'tp'), may hold values from -0.1875 to 0.1875
- w_up: bfloat16 [32, 1024, 512], P(None, 'fsdp', 'tp'), may hold values from -0.1875 to 0.1875
- w_down: bfloat16 [32, 512, 1024], P(None, 'tp', 'fsdp'), may hold values from -1 to 1
Outputs:
- block_out: bfloat16 [12288, 1024], P(('fsdp', 'ctx'))
- input_grad: bfloat16 [12288, 1024], P(('fsdp', 'ctx'))
- grad_norm1: float32 [1024], P('fsdp')
- grad_query: float32 [1024, 1024], P('fsdp', 'tp')
- grad_key: float32 [1024, 512], P('fsdp', 'tp')
- grad_value: float32 [1024, 512], P('fsdp', 'tp')
- grad_out: float32 [1024, 1024], P('tp', 'fsdp')
- grad_norm2: float32 [1024], P('fsdp')
- grad_router: float32 [1024, 32], P('fsdp')
- grad_gate: float32 [32, 1024, 512], P(None, 'fsdp', 'tp')
- grad_up: float32 [32, 1024, 512], P(None, 'fsdp', 'tp')
- grad_down: float32 [32, 512, 1024], P(None, 'tp', 'fsdp')
Inputs may be any that keep to these rules, and one draw needn't show every extreme that they name: `doc_ids`: never falls along the tokens; each document holds 1 to 1024 consecutive tokens. `block_ids`: never falls along the tokens; each block holds 1 to 256 consecutive tokens. `expert_ids`: the 8 experts of a token differ; in each aligned block of 1536 tokens (the tokens of one device) no expert is named more than 576 times, a bound that some block reaches.
All inputs are finite; a program needn't handle non-finite values.
Results may differ from a plain program's by a relative error of at most 0.017.
Values may be sent and summed in bfloat16 or wider, within the bound.
A program may use at most 448 MiB of HBM per device.

v0:
```python
import jax
import jax.numpy as jnp
from jax import lax
from jax.sharding import PartitionSpec as P

HD = 64
CAP = 576


epsilon = 1e-06
rope_base = 10000.0
masked_score = -1e30


def rope_angles(positions, head_size):
    half_size = head_size // 2
    frequency = rope_base ** (-2.0 * jnp.arange(half_size, dtype=jnp.float32) / head_size)
    angles = positions.astype(jnp.float32)[:, None] * frequency[None, :]
    return (jnp.cos(angles), jnp.sin(angles))


def rotate(values, cosine, sine_table, head_size):
    row_count = values.shape[0]
    shaped = values.reshape(row_count, -1, head_size)
    half_size = head_size // 2
    first_half = shaped[:, :, :half_size]
    second_half = shaped[:, :, half_size:]
    cos_rows = cosine[:, None, :]
    sin_rows = sine_table[:, None, :]
    turned = jnp.concatenate(
        [
            first_half * cos_rows - second_half * sin_rows,
            second_half * cos_rows + first_half * sin_rows,
        ],
        axis=2,
    )
    return turned.reshape(row_count, -1)


def inner_rows(left_mat, right_mat):
    return lax.dot_general(
        left_mat, right_mat, (((0,), (0,)), ((), ())), preferred_element_type=jnp.float32
    )


def outer_cols(left_mat, right_mat):
    return lax.dot_general(
        left_mat, right_mat, (((1,), (1,)), ((), ())), preferred_element_type=jnp.float32
    )


def per_device(
    tokens,
    out_grad,
    doc_ids,
    block_ids,
    expert_ids,
    norm1_gain,
    w_query,
    w_key,
    w_value,
    w_out,
    norm2_gain,
    w_router,
    w_gate,
    w_up,
    w_down,
):
    attn_full = (
        lax.all_gather(w_query, "fsdp", axis=0, tiled=True),
        lax.all_gather(w_key, "fsdp", axis=0, tiled=True),
        lax.all_gather(w_value, "fsdp", axis=0, tiled=True),
        lax.all_gather(w_out, "fsdp", axis=1, tiled=True),
        lax.all_gather(norm1_gain, "fsdp", axis=0, tiled=True),
        lax.all_gather(norm2_gain, "fsdp", axis=0, tiled=True),
    )
    moe_full = (
        lax.all_gather(w_router, "fsdp", axis=0, tiled=True),
        lax.all_gather(w_gate, "fsdp", axis=1, tiled=True),
        lax.all_gather(w_up, "fsdp", axis=1, tiled=True),
        lax.all_gather(w_down, "fsdp", axis=2, tiled=True),
    )
    query_w, key_w, value_w, out_w, gain_one, gain_two = attn_full
    router_w, gate_w, up_w, down_w = moe_full
    rows_here = tokens.shape[0]
    model_width = tokens.shape[1]
    ctx_place = lax.axis_index("ctx")
    q_width = query_w.shape[1]
    kv_width = key_w.shape[1]
    heads_here = q_width // HD
    kv_heads = kv_width // HD
    group_share = heads_here // kv_heads
    score_scale = HD ** (-0.5)
    expert_count = router_w.shape[1]
    top_count = expert_ids.shape[1]
    ff_here = gate_w.shape[2]
    capacity = CAP
    inputs = tokens.astype(jnp.float32)
    grad_top = out_grad.astype(jnp.float32)
    rms_one = lax.rsqrt(jnp.mean(inputs * inputs, axis=1, keepdims=True) + epsilon)
    normed_f = inputs * rms_one
    gain_first = gain_one.astype(jnp.float32)
    normed = (normed_f * gain_first).astype(jnp.bfloat16)
    row_start = ctx_place * rows_here
    positions = row_start + jnp.arange(rows_here, dtype=jnp.int32)
    cosine, sine_table = rope_angles(positions, HD)
    queries = rotate(
        jnp.dot(normed, query_w, preferred_element_type=jnp.float32), cosine, sine_table, HD
    ).astype(jnp.bfloat16)
    keys_own = rotate(
        jnp.dot(normed, key_w, preferred_element_type=jnp.float32), cosine, sine_table, HD
    ).astype(jnp.bfloat16)
    values_own = jnp.dot(normed, value_w, preferred_element_type=jnp.float32).astype(jnp.bfloat16)
    keys_all, values_all = (
        lax.all_gather(keys_own, "ctx", axis=0, tiled=True),
        lax.all_gather(values_own, "ctx", axis=0, tiled=True),
    )
    query_doc = lax.dynamic_slice_in_dim(doc_ids, row_start, rows_here)
    query_block = lax.dynamic_slice_in_dim(block_ids, row_start, rows_here)
    allowed = (query_doc[:, None] == doc_ids[None, :]) & (
        block_ids[None, :] <= query_block[:, None]
    )
    head_outputs = []
    log_totals = []
    for which_head in range(heads_here):
        group_slot = which_head // group_share
        query_part = queries[:, which_head * HD : (which_head + 1) * HD]
        key_part = keys_all[:, group_slot * HD : (group_slot + 1) * HD]
        value_part = values_all[:, group_slot * HD : (group_slot + 1) * HD]
        scores = jnp.where(allowed, outer_cols(query_part, key_part) * score_scale, masked_score)
        top_score = jnp.max(scores, axis=1, keepdims=True)
        exp_scores = jnp.exp(scores - top_score)
        row_total = jnp.sum(exp_scores, axis=1, keepdims=True)
        weights_bf = (exp_scores / row_total).astype(jnp.bfloat16)
        head_outputs.append(
            jnp.dot(weights_bf, value_part, preferred_element_type=jnp.float32).astype(jnp.bfloat16)
        )
        log_totals.append(top_score + jnp.log(row_total))
    attn_mix = jnp.concatenate(head_outputs, axis=1)
    branch = lax.psum(jnp.dot(attn_mix, out_w, preferred_element_type=jnp.float32), "tp")
    hidden = inputs + branch
    rms_two = lax.rsqrt(jnp.mean(hidden * hidden, axis=1, keepdims=True) + epsilon)
    hidden_hat = hidden * rms_two
    gain_second = gain_two.astype(jnp.float32)
    normed_two = (hidden_hat * gain_second).astype(jnp.bfloat16)
    logits = jnp.dot(normed_two, router_w, preferred_element_type=jnp.float32)
    expert_hot = (
        expert_ids[:, :, None] == jnp.arange(expert_count, dtype=jnp.int32)[None, None, :]
    ).astype(jnp.float32)
    chosen = jnp.sum(expert_hot * logits[:, None, :], axis=2)
    gate_probs = jax.nn.softmax(chosen, axis=1)
    flat_ids = expert_ids.reshape(-1)
    flat_hot = (flat_ids[:, None] == jnp.arange(expert_count, dtype=jnp.int32)[None, :]).astype(
        jnp.int32
    )
    running = jnp.cumsum(flat_hot, axis=0)
    flat_slot = flat_ids * capacity + jnp.sum(running * flat_hot, axis=1) - 1
    slot_total = expert_count * capacity
    pair_rows = jnp.arange(rows_here * top_count, dtype=jnp.int32) // top_count
    source_row = jnp.zeros((slot_total,), jnp.int32).at[flat_slot].set(pair_rows)
    slot_gate = jnp.zeros((slot_total,), jnp.float32).at[flat_slot].set(gate_probs.reshape(-1))
    group_size = 4
    group_count = expert_count // group_size
    group_rows = source_row.reshape(group_count, group_size * capacity)
    group_gates = slot_gate.reshape(group_count, group_size * capacity)

    def expert_front(rows_idx, gate_part, up_part):
        taken_rows = normed_two[rows_idx].reshape(group_size, capacity, model_width)
        gate_val = jnp.einsum(
            "gcd,gdf->gcf", taken_rows, gate_part, preferred_element_type=jnp.float32
        )
        up_val = jnp.einsum("gcd,gdf->gcf", taken_rows, up_part, preferred_element_type=jnp.float32)
        return (taken_rows, gate_val, up_val)

    def forward_step(combined, pieces):
        rows_idx, gate_vals, gate_part, up_part, down_part = pieces
        taken_rows, gate_val, up_val = expert_front(rows_idx, gate_part, up_part)
        inner_act = (gate_val * jax.nn.sigmoid(gate_val) * up_val).astype(jnp.bfloat16)
        result = jnp.einsum(
            "gcf,gfd->gcd", inner_act, down_part, preferred_element_type=jnp.float32
        ).reshape(group_size * capacity, model_width)
        combined = combined.at[rows_idx].add(result * gate_vals[:, None])
        slot_dots = jnp.sum(result * grad_top[rows_idx], axis=1)
        return (combined, slot_dots)

    forward_pieces = (
        group_rows,
        group_gates,
        gate_w.reshape(group_count, group_size, model_width, ff_here),
        up_w.reshape(group_count, group_size, model_width, ff_here),
        down_w.reshape(group_count, group_size, ff_here, model_width),
    )
    combined, slot_dots = lax.scan(
        forward_step, jnp.zeros((rows_here, model_width), jnp.float32), forward_pieces
    )
    mixed = lax.psum(combined.astype(jnp.bfloat16), "tp").astype(jnp.float32)
    block_out = (hidden + mixed).astype(jnp.bfloat16)
    attn_back = (
        lax.all_gather(w_query, "fsdp", axis=0, tiled=True),
        lax.all_gather(w_key, "fsdp", axis=0, tiled=True),
        lax.all_gather(w_value, "fsdp", axis=0, tiled=True),
        lax.all_gather(w_out, "fsdp", axis=1, tiled=True),
        lax.all_gather(norm1_gain, "fsdp", axis=0, tiled=True),
        lax.all_gather(norm2_gain, "fsdp", axis=0, tiled=True),
    )
    moe_back = (
        lax.all_gather(w_router, "fsdp", axis=0, tiled=True),
        lax.all_gather(w_gate, "fsdp", axis=1, tiled=True),
        lax.all_gather(w_up, "fsdp", axis=1, tiled=True),
        lax.all_gather(w_down, "fsdp", axis=2, tiled=True),
    )
    query_b, key_b, value_b, out_b, gain_one_b, gain_two_b = attn_back
    router_b, gate_b, up_b, down_b = moe_back
    gate_dots_part = slot_dots.reshape(-1)[flat_slot].reshape(rows_here, top_count)

    def backward_step(grad_acc, pieces):
        rows_idx, gate_vals, gate_part, up_part, down_part = pieces
        taken_rows, gate_val, up_val = expert_front(rows_idx, gate_part, up_part)
        sigmoid_gate = jax.nn.sigmoid(gate_val)
        silu_gate = gate_val * sigmoid_gate
        inner_act = (silu_gate * up_val).astype(jnp.bfloat16)
        result_grad = (
            (grad_top[rows_idx] * gate_vals[:, None])
            .astype(jnp.bfloat16)
            .reshape(group_size, capacity, model_width)
        )
        inner_grad = jnp.einsum(
            "gcd,gfd->gcf", result_grad, down_part, preferred_element_type=jnp.float32
        )
        gate_grad = (
            inner_grad * up_val * sigmoid_gate * (1.0 + gate_val * (1.0 - sigmoid_gate))
        ).astype(jnp.bfloat16)
        up_grad = (inner_grad * silu_gate).astype(jnp.bfloat16)
        down_w_grad = jnp.einsum(
            "gcf,gcd->gfd", inner_act, result_grad, preferred_element_type=jnp.float32
        )
        gate_w_grad = jnp.einsum(
            "gcd,gcf->gdf", taken_rows, gate_grad, preferred_element_type=jnp.float32
        )
        up_w_grad = jnp.einsum(
            "gcd,gcf->gdf", taken_rows, up_grad, preferred_element_type=jnp.float32
        )
        taken_grad = jnp.einsum(
            "gcf,gdf->gcd", gate_grad, gate_part, preferred_element_type=jnp.float32
        ) + jnp.einsum("gcf,gdf->gcd", up_grad, up_part, preferred_element_type=jnp.float32)
        grad_acc = grad_acc.at[rows_idx].add(taken_grad.reshape(group_size * capacity, model_width))
        return (grad_acc, (gate_w_grad, up_w_grad, down_w_grad))

    backward_pieces = (
        group_rows,
        group_gates,
        gate_b.reshape(group_count, group_size, model_width, ff_here),
        up_b.reshape(group_count, group_size, model_width, ff_here),
        down_b.reshape(group_count, group_size, ff_here, model_width),
    )
    two_grad_part, expert_grads = lax.scan(
        backward_step, jnp.zeros((rows_here, model_width), jnp.float32), backward_pieces
    )
    gate_grads = expert_grads[0].reshape(expert_count, model_width, ff_here)
    up_grads = expert_grads[1].reshape(expert_count, model_width, ff_here)
    down_grads = expert_grads[2].reshape(expert_count, ff_here, model_width)
    gate_dots, two_grad = lax.psum((gate_dots_part, two_grad_part), "tp")
    mean_dot = jnp.sum(gate_probs * gate_dots, axis=1, keepdims=True)
    chosen_grad = gate_probs * (gate_dots - mean_dot)
    logit_grad = jnp.sum(expert_hot * chosen_grad[:, :, None], axis=1).astype(jnp.bfloat16)
    router_grad = inner_rows(normed_two, logit_grad)
    two_grad = two_grad + outer_cols(logit_grad, router_b)
    gain_two_grad = jnp.sum(two_grad * hidden_hat, axis=0)
    scaled_two = two_grad * gain_two_b.astype(jnp.float32)
    hidden_grad = grad_top + rms_two * (
        scaled_two - hidden_hat * jnp.mean(scaled_two * hidden_hat, axis=1, keepdims=True)
    )
    branch_grad = hidden_grad.astype(jnp.bfloat16)
    out_w_grad = inner_rows(attn_mix, branch_grad)
    mix_grad = outer_cols(branch_grad, out_b).astype(jnp.bfloat16)
    seq_rows = keys_all.shape[0]
    key_parts = [jnp.zeros((seq_rows, HD), jnp.float32) for which_group in range(kv_heads)]
    value_parts = [jnp.zeros((seq_rows, HD), jnp.float32) for which_group in range(kv_heads)]
    query_grads = []
    for which_head in range(heads_here):
        group_slot = which_head // group_share
        query_part = queries[:, which_head * HD : (which_head + 1) * HD]
        key_part = keys_all[:, group_slot * HD : (group_slot + 1) * HD]
        value_part = values_all[:, group_slot * HD : (group_slot + 1) * HD]
        scores = jnp.where(allowed, outer_cols(query_part, key_part) * score_scale, masked_score)
        probs_f = jnp.exp(scores - log_totals[which_head])
        weights_bf = probs_f.astype(jnp.bfloat16)
        head_grad = mix_grad[:, which_head * HD : (which_head + 1) * HD]
        prob_grad = outer_cols(head_grad, value_part)
        row_delta = jnp.sum(prob_grad * probs_f, axis=1, keepdims=True)
        score_grad = (probs_f * (prob_grad - row_delta)).astype(jnp.bfloat16)
        query_grads.append(
            jnp.dot(score_grad, key_part, preferred_element_type=jnp.float32) * score_scale
        )
        key_parts[group_slot] = (
            key_parts[group_slot] + inner_rows(score_grad, query_part) * score_scale
        )
        value_parts[group_slot] = value_parts[group_slot] + inner_rows(weights_bf, head_grad)
    key_grad_own, value_grad_own = (
        lax.psum_scatter(
            jnp.concatenate(key_parts, axis=1), "ctx", scatter_dimension=0, tiled=True
        ),
        lax.psum_scatter(
            jnp.concatenate(value_parts, axis=1), "ctx", scatter_dimension=0, tiled=True
        ),
    )
    query_lin_grad = rotate(jnp.concatenate(query_grads, axis=1), cosine, -sine_table, HD).astype(
        jnp.bfloat16
    )
    key_lin_grad = rotate(key_grad_own, cosine, -sine_table, HD).astype(jnp.bfloat16)
    value_lin_grad = value_grad_own.astype(jnp.bfloat16)
    one_grad_part = (
        outer_cols(query_lin_grad, query_b)
        + outer_cols(key_lin_grad, key_b)
        + outer_cols(value_lin_grad, value_b)
    )
    query_w_grad = inner_rows(normed, query_lin_grad)
    key_w_grad = inner_rows(normed, key_lin_grad)
    value_w_grad = inner_rows(normed, value_lin_grad)
    one_grad = lax.psum(one_grad_part, "tp")
    gain_one_grad = jnp.sum(one_grad * normed_f, axis=0)
    scaled_one = one_grad * gain_one_b.astype(jnp.float32)
    input_grad = hidden_grad + rms_one * (
        scaled_one - normed_f * jnp.mean(scaled_one * normed_f, axis=1, keepdims=True)
    )
    router_s, gate_s, up_s, down_s = (
        lax.psum_scatter(router_grad, "fsdp", scatter_dimension=0, tiled=True),
        lax.psum_scatter(gate_grads, "fsdp", scatter_dimension=1, tiled=True),
        lax.psum_scatter(up_grads, "fsdp", scatter_dimension=1, tiled=True),
        lax.psum_scatter(down_grads, "fsdp", scatter_dimension=2, tiled=True),
    )
    query_s, key_s, value_s, out_s, gain_one_s, gain_two_s = (
        lax.psum_scatter(query_w_grad, "fsdp", scatter_dimension=0, tiled=True),
        lax.psum_scatter(key_w_grad, "fsdp", scatter_dimension=0, tiled=True),
        lax.psum_scatter(value_w_grad, "fsdp", scatter_dimension=0, tiled=True),
        lax.psum_scatter(out_w_grad, "fsdp", scatter_dimension=1, tiled=True),
        lax.psum_scatter(gain_one_grad, "fsdp", scatter_dimension=0, tiled=True),
        lax.psum_scatter(gain_two_grad, "fsdp", scatter_dimension=0, tiled=True),
    )
    summed = lax.psum(
        (gain_one_s, query_s, key_s, value_s, out_s, gain_two_s, router_s, gate_s, up_s, down_s),
        "ctx",
    )
    return (
        block_out,
        input_grad.astype(jnp.bfloat16),
        summed[0],
        summed[1],
        summed[2],
        summed[3],
        summed[4],
        summed[5],
        summed[6],
        summed[7],
        summed[8],
        summed[9],
    )


def solution(mesh):
    return jax.shard_map(
        per_device,
        mesh=mesh,
        in_specs=(
            P(("fsdp", "ctx"), None),
            P(("fsdp", "ctx"), None),
            P("fsdp"),
            P("fsdp"),
            P(("fsdp", "ctx"), None),
            P("fsdp"),
            P("fsdp", "tp"),
            P("fsdp", "tp"),
            P("fsdp", "tp"),
            P("tp", "fsdp"),
            P("fsdp"),
            P("fsdp", None),
            P(None, "fsdp", "tp"),
            P(None, "fsdp", "tp"),
            P(None, "tp", "fsdp"),
        ),
        out_specs=(
            P(("fsdp", "ctx"), None),
            P(("fsdp", "ctx"), None),
            P("fsdp"),
            P("fsdp", "tp"),
            P("fsdp", "tp"),
            P("fsdp", "tp"),
            P("tp", "fsdp"),
            P("fsdp"),
            P("fsdp", None),
            P(None, "fsdp", "tp"),
            P(None, "fsdp", "tp"),
            P(None, "tp", "fsdp"),
        ),
        check_vma=False,
    )
```

profile of v0, /device:TPU:0, one launch (start us, length us, event | category | flops | bytes accessed | tf_op | source)
XLA Modules:
  0.0 3824.0 jit_solution(6046683299682049553)
XLA Ops:
  8.7 12.6 all-gather
  24.0 14.1 all_gather.48
  52.2 14.9 all_gather.47
  108.9 16.2 all_gather.52
  125.0 13.8 all_gather.50
  249.7 45.4 %scatter_custom_fusion.2 = s32[18432]{0:T(1024)S(1)} fusion(s32[12288]{0:T(1024)S(1)} %bitcast.224, s32[12288]{0:T(1024)S(1)} %add_select_fusion, s32[]{:T(128)} %constant.102.clone.1), kind=kCustom, calls=%fused_computation.246 | custom fusion | bytes 73732 | tf_op jit(solution)/shard_map/scatter | solution.py:160
  300.5 31.7 all_gather.57
  352.1 45.4 %scatter_custom_fusion.3 = f32[18432]{0:T(1024)S(1)} fusion(s32[12288]{0:T(1024)S(1)} %bitcast.226, f32[12288]{0:T(1024)S(1)} %reshape.458, f32[]{:T(128)} %constant.104.clone.1), kind=kCustom, calls=%fused_computation.244 | custom fusion | bytes 73732 | tf_op jit(solution)/shard_map/scatter | solution.py:161
  397.6 126.6 %all-gather.8.cloned.1.call-done = bf16[32,1024,128]{2,1,0:T(8,128)(2,1)} async-done(((bf16[32,256,128]{2,1,0:T(8,128)(2,1)}), bf16[32,1024,128]{2,1,0:T(8,128)(2,1)}) %all-gather.8.cloned.1.call-update) | async-done | bytes 8388624 | tf_op jit(solution)/shard_map/all_gather | solution.py:80
  524.2 149.1 %all-gather.6.cloned.1.call-done = bf16[32,1024,128]{2,1,0:T(8,128)(2,1)} async-done(((bf16[32,256,128]{2,1,0:T(8,128)(2,1)}), bf16[32,1024,128]{2,1,0:T(8,128)(2,1)}) %all-gather.6.cloned.1.call-update) | async-done | bytes 8388624 | tf_op jit(solution)/shard_map/all_gather | solution.py:79
  676.9 746.1 %while.29 = (s32[]{:T(128)}, f32[1536,1024]{1,0:T(8,128)}, f32[8,4,1024,128]{3,2,1,0:T(8,128)}, f32[8,4,1024,128]{3,2,1,0:T(8,128)}, f32[8,4,128,1024]{3,2,1,0:T...) while((s32[]{:T(128)}, f32[1536,1024]{1,0:T(8,128)}, ...), condition=%wide.region_26.27_spmd, body=%wide.region_24.26_spmd.sunk | while | flops 4851607552 | bytes 175628656 | solution.py:256
  694.2 13.8 gather_fusion.3
  723.9 28.8 scatter_fusion.1
  787.4 13.8 gather_fusion.3
  817.1 28.8 scatter_fusion.1
  880.5 13.8 gather_fusion.3
  910.2 28.8 scatter_fusion.1
  973.7 13.8 gather_fusion.3
  1003.4 28.8 scatter_fusion.1
  1067.0 13.8 gather_fusion.3
  1096.7 28.8 scatter_fusion.1
  1160.3 13.8 gather_fusion.3
  1190.0 28.8 scatter_fusion.1
  1253.5 13.8 gather_fusion.3
  1283.2 28.8 scatter_fusion.1
  1346.6 13.8 gather_fusion.3
  1376.3 28.8 scatter_fusion.1
  1426.5 611.3 %while.28 = (s32[]{:T(128)}, f32[1536,1024]{1,0:T(8,128)}, f32[8,2304]{1,0:T(8,128)S(1)}, s32[8,2304]{1,0:T(8,128)S(1)}, bf16[1536,1024]{1,0:T(8,128)(2,1)S(1)},...) while((s32[]{:T(128)}, f32[1536,1024]{1,0:T(8,128)}, ...), condition=%wide.region_22.23_spmd, body=%wide.region_19.22_spmd.sunk | while | flops 1823153664 | bytes 109456520 | solution.py:193
  1426.5 14.4 gather_fusion
  1454.0 12.4 multiply_reduce_fusion.10
  1474.6 28.8 scatter_fusion
  1503.8 13.9 gather_fusion
  1551.1 28.7 scatter_fusion
  1580.2 13.8 gather_fusion
  1607.0 12.3 multiply_reduce_fusion.10
  1627.4 28.7 scatter_fusion
  1656.4 13.8 gather_fusion
  1683.3 12.3 multiply_reduce_fusion.10
  1703.7 28.7 scatter_fusion
  1732.7 13.8 gather_fusion
  1759.6 12.3 multiply_reduce_fusion.10
  1780.0 28.7 scatter_fusion
  1809.0 13.8 gather_fusion
  1856.2 28.7 scatter_fusion
  1885.3 13.8 gather_fusion
  1932.5 28.7 scatter_fusion
  1961.6 13.8 gather_fusion
  2008.8 28.7 scatter_fusion
  2037.8 68.0 %gather_fusion.4 = f32[12288]{0:T(1024)S(1)} fusion(f32[18432]{0:T(1024)S(1)} %reshape.383, s32[12288]{0:T(1024)S(1)} %copy-done.58), kind=kCustom, calls=%fused_computation.4 | custom fusion | bytes 147456 | tf_op jit(solution)/shard_map/gather | solution.py:214
  2134.8 56.8 %all-reduce.13.cloned.1.call-done = bf16[1536,1024]{1,0:T(8,128)(2,1)} async-done(((bf16[1536,1024]{1,0:T(8,128)(2,1)}), bf16[1536,1024]{1,0:T(8,128)(2,1)}) %all-reduce.13.cloned.1.call-update) | async-done | bytes 3145744 | tf_op jit(solution)/shard_map/psum | solution.py:196
  2203.8 12.8 multiply_reduce_fusion.1
  2224.7 12.8 multiply_reduce_fusion.2
  2237.5 12.9 multiply_reduce_fusion.3
  2250.4 12.5 multiply_reduce_fusion.4
  2262.9 15.3 multiply_convert_fusion.10
  2296.9 19.3 multiply_convert_fusion.9
  2426.1 28.1 reduce-scatter.21.cloned.1.call-done
  2454.2 23.2 reduce-scatter.17.cloned.1.call-done
  2477.5 23.0 reduce-scatter.19.cloned.1.call-done
  2500.5 280.9 %reduce-scatter.25.cloned.1.call-done = f32[32,256,128]{2,1,0:T(8,128)} async-done(((f32[32,1024,128]{2,1,0:T(8,128)}), f32[32,256,128]{2,1,0:T(8,128)}) %reduce-scatter.25.cloned.1.call-update) | async-done | bytes 4194320 | tf_op jit(solution)/shard_map/reduce_scatter | solution.py:328
  2781.4 283.5 %reduce-scatter.27.cloned.1.call-done = f32[32,256,128]{2,1,0:T(8,128)} async-done(((f32[32,1024,128]{2,1,0:T(8,128)}), f32[32,256,128]{2,1,0:T(8,128)}) %reduce-scatter.27.cloned.1.call-update) | async-done | bytes 4194320 | tf_op jit(solution)/shard_map/reduce_scatter | solution.py:329
  3064.9 283.3 %reduce-scatter.29.cloned.1.call-done = f32[32,128,256]{2,1,0:T(8,128)} async-done(((f32[32,128,1024]{2,1,0:T(8,128)}), f32[32,128,256]{2,1,0:T(8,128)}) %reduce-scatter.29.cloned.1.call-update) | async-done | bytes 4194320 | tf_op jit(solution)/shard_map/reduce_scatter | solution.py:330
  3350.1 120.7 %all-reduce.17.cloned.1.call-done = f32[1536,1024]{1,0:T(8,128)} async-done(((f32[1536,1024]{1,0:T(8,128)}), f32[1536,1024]{1,0:T(8,128)}) %all-reduce.17.cloned.1.call-update) | async-done | bytes 6291472 | tf_op jit(solution)/shard_map/psum | solution.py:320
  3509.7 289.7 %all-reduce.19.cloned.1.call-done = (f32[256,256]{1,0:T(8,128)}, f32[256,128]{1,0:T(8,128)}, f32[256,128]{1,0:T(8,128)}, f32[256,256]{1,0:T(8,128)}, f32[32,256,...) async-done(((f32[256,256]{1,0:T(8,128)}, f32[256,128]{1,0:T(8,128)}, f32[256,128]{1,0:T(8,128)}, f32[256,256]{1,0:T(8,128)}, ...) | async-done | bytes 13369360 | tf_op jit(solution)/shard_map/psum | solution.py:340
  (656 shorter events, 1061.6 us)
Async XLA Ops:
  8.0 334.7 %all-reduce.11.cloned.1.call-start = ((), (), s32[]{:S(2)}) async-start(), calls=%async_computation.10 | async-start | bytes 12582912 | tf_op jit(solution)/shard_map/psum | solution.py:140
  21.4 20.7 copy-start.71
  24.0 19.7 copy-start.65
  38.1 14.2 copy-start.61
  40.9 97.9 %copy-start.10 = (bf16[1536,1024]{1,0:T(8,128)(2,1)}, bf16[1536,1024]{1,0:T(8,128)(2,1)S(1)}, u32[]{:S(2)}) copy-start(bf16[1536,1024]{1,0:T(8,128)(2,1)S(1)} %fusion.74) | copy-start | bytes 9437188
  43.5 25.5 copy-start.25
  71.9 27.9 copy-start.21
  99.9 25.2 copy-start.70
  148.2 62.6 %copy-start.16 = (bf16[3072,128]{1,0:T(8,128)(2,1)}, bf16[3072,128]{1,0:T(8,128)(2,1)S(1)}, u32[]{:S(2)}) copy-start(bf16[3072,128]{1,0:T(8,128)(2,1)S(1)} %all_gather.51) | copy-start | bytes 2359300
  166.5 52.9 %copy-start.46 = (bf16[1536,64]{0,1:T(8,128)(2,1)}, bf16[1536,64]{0,1:T(8,128)(2,1)S(1)}, u32[]{:S(2)}) copy-start(bf16[1536,64]{0,1:T(8,128)(2,1)S(1)} %fusion.90) | copy-start | bytes 589828
  184.1 35.3 copy-start.47
  201.8 17.6 copy-start.48
  223.9 173.7 %all-gather.10.cloned.1.call-start = ((), (), s32[]{:S(2)}) async-start(), calls=%async_computation.13 | async-start | bytes 10485760 | tf_op jit(solution)/shard_map/all_gather | solution.py:81
  224.5 299.7 %all-gather.8.cloned.1.call-start = ((), (), s32[]{:S(2)}) async-start(), calls=%async_computation.12 | async-start | bytes 10485760 | tf_op jit(solution)/shard_map/all_gather | solution.py:80
  225.1 448.3 %all-gather.6.cloned.1.call-start = ((), (), s32[]{:S(2)}) async-start(), calls=%async_computation.11 | async-start | bytes 10485760 | tf_op jit(solution)/shard_map/all_gather | solution.py:79
  225.6 1900.4 %all-reduce.15.cloned.1.call-start = ((), (), s32[]{:S(2)}) async-start(), calls=%async_computation.15 | async-start | bytes 12582912 | tf_op jit(solution)/shard_map/psum | solution.py:262
  235.7 110.7 %copy-start.68 = (f32[4,1,256]{2,1,0:T(1,128)}, f32[4,1,256]{2,1,0:T(1,128)S(1)}, u32[]{:S(2)}) copy-start(f32[4,1,256]{2,1,0:T(1,128)S(1)} %convert_element_type.178) | copy-start | bytes 12292
  248.4 94.4 %copy-start.8 = (bf16[1536,1024]{1,0:T(8,128)(2,1)S(1)}, bf16[1536,1024]{1,0:T(8,128)(2,1)}, u32[]{:S(2)}) copy-start(bf16[1536,1024]{1,0:T(8,128)(2,1)} %param.19) | copy-start | bytes 9437188
  332.2 14.9 copy-start.50
  349.4 327.5 %copy-start.37 = (f32[1536,8]{0,1:T(8,128)}, f32[1536,8]{0,1:T(8,128)S(1)}, u32[]{:S(2)}) copy-start(f32[1536,8]{0,1:T(8,128)S(1)} %select_reduce_fusion.1) | copy-start | bytes 147460
  1423.0 768.7 %all-reduce.13.cloned.1.call-start = ((), (), s32[]{:S(2)}) async-start(), calls=%async_computation.14 | async-start | bytes 6291456 | tf_op jit(solution)/shard_map/psum | solution.py:196
  1426.4 611.4 %copy-start.58 = (s32[12288]{0:T(1024)S(1)}, s32[12288]{0:T(1024)}, u32[]{:S(2)}) copy-start(s32[12288]{0:T(1024)} %broadcast_clamp_fusion) | copy-start | bytes 147460
  2037.8 68.1 %copy-start = (bf16[1536,1024]{1,0:T(8,128)(2,1)}, bf16[1536,1024]{1,0:T(8,128)(2,1)S(1)}, u32[]{:S(2)}) copy-start(bf16[1536,1024]{1,0:T(8,128)(2,1)S(1)} %get-tuple-element.494) | copy-start | bytes 9437188
  2108.6 17.1 copy-start.38
  2108.6 17.1 copy-start.57
  2108.6 17.1 copy-start.64
  2108.6 17.2 copy-start.45
  2108.6 17.4 copy-start.51
  2108.6 17.4 copy-start.60
  2108.6 17.4 copy-start.69
  2125.6 270.6 %reduce-scatter.11.cloned.1.call-start = ((), (), s32[]{:S(2)}) async-start(), calls=%async_computation.16 | async-start | bytes 2359296 | tf_op jit(solution)/shard_map/reduce_scatter | solution.py:300
  2126.0 65.7 %copy-start.18 = (bf16[1536,1024]{1,0:T(8,128)(2,1)S(1)}, bf16[1536,1024]{1,0:T(8,128)(2,1)}, u32[]{:S(2)}) copy-start(bf16[1536,1024]{1,0:T(8,128)(2,1)} %param.20) | copy-start | bytes 9437188
  2224.7 12.8 copy-start.54
  2237.5 12.9 copy-start.53
  2262.9 15.4 copy-start.22
  2262.9 19.8 slice-start.2
  2262.9 19.8 slice-start.3
  2262.9 19.8 slice-start.4
  2262.9 19.8 slice-start.5
  2296.9 19.3 slice-start.12
  2296.9 19.3 slice-start.13
  2296.9 19.3 slice-start.14
  2296.9 20.1 slice-start.15
  2296.9 20.7 slice-start.16
  2339.9 59.5 %reduce-scatter.13.cloned.1.call-start = ((), (), s32[]{:S(2)}) async-start(), calls=%async_computation.17 | async-start | bytes 2359296 | tf_op jit(solution)/shard_map/reduce_scatter | solution.py:303
  2339.9 17.8 slice-start.7
  2339.9 17.8 slice-start.8
  2339.9 17.8 slice-start.9
  2369.7 56.5 %reduce-scatter.15.cloned.1.call-start = ((), (), s32[]{:S(2)}) async-start(), calls=%async_computation.19 | async-start | bytes 1310720 | tf_op jit(solution)/shard_map/reduce_scatter | solution.py:333
  2370.0 13.6 slice-start.17
  2370.0 13.6 slice-start.18
  2390.8 63.4 %reduce-scatter.21.cloned.1.call-start = ((), (), s32[]{:S(2)}) async-start(), calls=%async_computation.22 | async-start | bytes 1310720 | tf_op jit(solution)/shard_map/reduce_scatter | solution.py:336
  2396.1 81.3 %reduce-scatter.17.cloned.1.call-start = ((), (), s32[]{:S(2)}) async-start(), calls=%async_computation.20 | async-start | bytes 655360 | tf_op jit(solution)/shard_map/reduce_scatter | solution.py:334
  2399.3 101.2 %reduce-scatter.19.cloned.1.call-start = ((), (), s32[]{:S(2)}) async-start(), calls=%async_computation.21 | async-start | bytes 655360 | tf_op jit(solution)/shard_map/reduce_scatter | solution.py:335
  2402.3 379.1 %reduce-scatter.25.cloned.1.call-start = ((), (), s32[]{:S(2)}) async-start(), calls=%async_computation.24 | async-start | bytes 20971520 | tf_op jit(solution)/shard_map/reduce_scatter | solution.py:328
  2402.9 662.0 %reduce-scatter.27.cloned.1.call-start = ((), (), s32[]{:S(2)}) async-start(), calls=%async_computation.25 | async-start | bytes 20971520 | tf_op jit(solution)/shard_map/reduce_scatter | solution.py:329
  2403.7 944.5 %reduce-scatter.29.cloned.1.call-start = ((), (), s32[]{:S(2)}) async-start(), calls=%async_computation.26 | async-start | bytes 20971520 | tf_op jit(solution)/shard_map/reduce_scatter | solution.py:330
  2404.3 1066.5 %all-reduce.17.cloned.1.call-start = ((), (), s32[]{:S(2)}) async-start(), calls=%async_computation.18 | async-start | bytes 12582912 | tf_op jit(solution)/shard_map/psum | solution.py:320
  2411.0 1082.1 %reduce-scatter.23.cloned.1.call-start = ((), (), s32[]{:S(2)}) async-start(), calls=%async_computation.23 | async-start | bytes 163840 | tf_op jit(solution)/shard_map/reduce_scatter | solution.py:327
  2414.3 1385.2 %all-reduce.19.cloned.1.call-start = ((), (), s32[]{:S(2)}) async-start(), calls=%async_computation.27 | async-start | bytes 26738688 | tf_op jit(solution)/shard_map/psum | solution.py:340
  3348.2 122.6 %copy-start.9 = (bf16[1536,1024]{1,0:T(8,128)(2,1)S(1)}, bf16[1536,1024]{1,0:T(8,128)(2,1)}, u32[]{:S(2)}) copy-start(bf16[1536,1024]{1,0:T(8,128)(2,1)} %param.19) | copy-start | bytes 9437188
  3348.2 122.6 %copy-start.66 = (f32[1536]{0:T(1024)S(1)}, f32[1536]{0:T(1024)}, u32[]{:S(2)}) copy-start(f32[1536]{0:T(1024)} %copy-done.65) | copy-start | bytes 18436
  3348.2 122.6 %copy-start.72 = (f32[4,1,256]{2,1,0:T(1,128)S(1)}, f32[4,1,256]{2,1,0:T(1,128)}, u32[]{:S(2)}) copy-start(f32[4,1,256]{2,1,0:T(1,128)} %copy-done.71) | copy-start | bytes 12292
  3348.2 126.6 %copy-start.76 = (f32[1024]{0:T(1024)S(1)}, f32[1024]{0:T(1024)}, u32[]{:S(2)}) copy-start(f32[1024]{0:T(1024)} %get-tuple-element.136) | copy-start | bytes 12292
  (104 other events, 575.6 us)
Sparse Core Ops, SparseCore 0:
  224.0 118.6 all-reduce.10
  1423.1 117.7 all-reduce.14
  2125.8 65.8 all-reduce.12
  2340.0 26.2 reduce-scatter.10
  2369.8 26.2 reduce-scatter.12
  2398.8 27.2 reduce-scatter.14
  2428.4 25.7 reduce-scatter.20
  2457.1 20.3 reduce-scatter.16
  2480.3 20.1 reduce-scatter.18
  2502.7 278.6 reduce-scatter.24
  2783.8 281.0 reduce-scatter.26
  3067.1 281.0 reduce-scatter.28
  3350.6 120.1 all-reduce.16
  3473.5 19.6 reduce-scatter.22
  3496.0 303.3 all-reduce.18
Sparse Core Ops, SparseCore 1:
  225.9 149.0 all-gather.9
  376.5 147.7 all-gather.7
  525.6 147.6 all-gather.5
where the time goes:
time: 3830 us; the launch traced here: 3820 us
  waiting for transfers between devices  1690 us (44%)
  matrix products  703 us (18%)
  other arithmetic  681 us (18%)
  local copies, waits for them, and re-layouts  564 us (15%)
  blocking collectives  163 us (4%)
    psum x1, waiting for transfers between devices, per_device(): lax.psum((gain_one_s, query_s, key_s, value_s, out_s, gain_two_s, router_...  290 us
    reduce_scatter x1, waiting for transfers between devices, per_device(): lax.psum_scatter(up_grads, 'fsdp', scatter_dimension=1, tiled=True)  283 us
    reduce_scatter x1, waiting for transfers between devices, per_device(): lax.psum_scatter(down_grads, 'fsdp', scatter_dimension=2, tiled=True)  283 us
    reduce_scatter x1, waiting for transfers between devices, per_device(): lax.psum_scatter(gate_grads, 'fsdp', scatter_dimension=1, tiled=True)  281 us
    scatter-add x8, other arithmetic, backward_step(): grad_acc.at[rows_idx]  230 us
    scatter-add x8, other arithmetic, forward_step(): combined = combined.at[rows_idx].add(result * gate_vals[:, None])  230 us
    all_gather x1, waiting for transfers between devices, per_device(): lax.all_gather(w_gate, 'fsdp', axis=1, tiled=True)  149 us
    gather x16, local copies, waits for them, and re-layouts, expert_front(): taken_rows = normed_two[rows_idx].reshape(group_size, capacity, model_width)  129 us
  transfers between devices with their start and end apart: 18, of which 14 were waited for; matrix products, arithmetic and copies ran while one was open for 24% of the time, Pallas kernels for 0%

commit v1 on v0

v1 whole, which is shorter than its diff:
```python
import functools
import jax
import jax.numpy as jnp
from jax import lax
from jax.experimental import pallas as pl
from jax.experimental.pallas import tpu as pltpu

HD = 64
DOC = 1024
BLK = 256
QB = 256
BAND = DOC + 2 * BLK
masked_score = -1e30
epsilon = 1e-06
VL = 60 * 1024 * 1024

def nt(a, b):
    return lax.dot_general(a, b, (((1,), (1,)), ((), ())), preferred_element_type=jnp.float32)

def tn(a, b):
    return lax.dot_general(a, b, (((0,), (0,)), ((), ())), preferred_element_type=jnp.float32)

def nn(a, b):
    return jnp.dot(a, b, preferred_element_type=jnp.float32)

def band_start(row, length):
    return pl.multiple_of(jnp.clip(row - DOC, 0, length - BAND), QB)

def flash_fwd_body(base_ref, q_ref, k_ref, v_ref, docq_ref, blkq_ref, dock_ref, blkk_ref, o_ref, *, share, length):
    step = pl.program_id(0)
    start = band_start(base_ref[0] + step * QB, length)
    keys = pl.ds(start, BAND)
    dock = dock_ref[:, keys]
    blkk = blkk_ref[:, keys]
    ok = (docq_ref[...] == dock) & (blkk <= blkq_ref[...])
    bias = jnp.where(ok, 0.0, masked_score)
    for head in range(q_ref.shape[0]):
        s = nt(q_ref[head], k_ref[head // share, keys, :]) + bias
        top = jnp.max(s, axis=1, keepdims=True)
        e = jnp.exp(s - top)
        p = e * (1.0 / jnp.sum(e, axis=1, keepdims=True))
        o_ref[head] = nn(p.astype(jnp.bfloat16), v_ref[head // share, keys, :]).astype(jnp.bfloat16)

def flash_fwd(base, q, k, v, docq, blkq, dock, blkk):
    heads, rows, _ = q.shape
    kv, length, _ = k.shape
    full = lambda shape: pl.BlockSpec(shape, lambda i, b: (0,) * len(shape))
    return pl.pallas_call(
        functools.partial(flash_fwd_body, share=heads // kv, length=length),
        grid_spec=pltpu.PrefetchScalarGridSpec(
            num_scalar_prefetch=1, grid=(rows // QB,),
            in_specs=[
                pl.BlockSpec((heads, QB, HD), lambda i, b: (0, i, 0)),
                full(k.shape), full(v.shape),
                pl.BlockSpec((QB, 1), lambda i, b: (i, 0)),
                pl.BlockSpec((QB, 1), lambda i, b: (i, 0)),
                full((1, length)), full((1, length)),
            ],
            out_specs=pl.BlockSpec((heads, QB, HD), lambda i, b: (0, i, 0)),
        ),
        out_shape=jax.ShapeDtypeStruct(q.shape, jnp.bfloat16),
        compiler_params=pltpu.CompilerParams(vmem_limit_bytes=VL),
        name="flash_fwd",
    )(base, q, k, v, docq, blkq, dock, blkk)

def flash_bwd_body(base_ref, q_ref, g_ref, k_ref, v_ref, docq_ref, blkq_ref, dock_ref, blkk_ref, dq_ref, dk_ref, dv_ref, *, share, length):
    step = pl.program_id(0)
    start = band_start(base_ref[0] + step * QB, length)
    keys = pl.ds(start, BAND)

    @pl.when(step == 0)
    def _():
        dk_ref[...] = jnp.zeros_like(dk_ref)
        dv_ref[...] = jnp.zeros_like(dv_ref)

    ok = (docq_ref[...] == dock_ref[keys, :]) & (blkk_ref[keys, :] <= blkq_ref[...])
    bias = jnp.where(ok, 0.0, masked_score)
    for head in range(q_ref.shape[0]):
        kvh = head // share
        q = q_ref[head]
        g = g_ref[head]
        k = k_ref[kvh, keys, :]
        s = nt(k, q) + bias
        e = jnp.exp(s - jnp.max(s, axis=0, keepdims=True))
        p = e * (1.0 / jnp.sum(e, axis=0, keepdims=True))
        dp = nt(v_ref[kvh, keys, :], g)
        delta = jnp.sum(dp * p, axis=0, keepdims=True)
        ds = (p * (dp - delta)).astype(jnp.bfloat16)
        dq_ref[head] = tn(ds, k)
        dk_ref[kvh, keys, :] += nn(ds, q)
        dv_ref[kvh, keys, :] += nn(p.astype(jnp.bfloat16), g)

def flash_bwd(base, q, g, k, v, docq, blkq, dock, blkk):
    heads, rows, _ = q.shape
    kv, length, _ = k.shape
    full = lambda shape: pl.BlockSpec(shape, lambda i, b: (0,) * len(shape))
    return pl.pallas_call(
        functools.partial(flash_bwd_body, share=heads // kv, length=length),
        grid_spec=pltpu.PrefetchScalarGridSpec(
            num_scalar_prefetch=1, grid=(rows // QB,),
            in_specs=[
                pl.BlockSpec((heads, QB, HD), lambda i, b: (0, i, 0)),
                pl.BlockSpec((heads, QB, HD), lambda i, b: (0, i, 0)),
                full(k.shape), full(v.shape),
                pl.BlockSpec((1, QB), lambda i, b: (0, i)),
                pl.BlockSpec((1, QB), lambda i, b: (0, i)),
                full((length, 1)), full((length, 1)),
            ],
            out_specs=[
                pl.BlockSpec((heads, QB, HD), lambda i, b: (0, i, 0)),
                full(k.shape), full(v.shape),
            ],
        ),
        out_shape=[
            jax.ShapeDtypeStruct(q.shape, jnp.float32),
            jax.ShapeDtypeStruct(k.shape, jnp.float32),
            jax.ShapeDtypeStruct(v.shape, jnp.float32),
        ],
        compiler_params=pltpu.CompilerParams(vmem_limit_bytes=VL),
        name="flash_bwd",
    )(base, q, g, k, v, docq, blkq, dock, blkk)

PAIR = 2
TM = 512

def moe_body(x_ref, g_ref, xt_ref, gt_ref, gates_ref, w_ref, a_ref, gu_ref, grads_ref, dots_ref):
    rows, width = x_ref.shape
    shards, _, pair, part, ff = w_ref.shape
    step = pl.program_id(0)

    def weights(which):
        return jnp.concatenate(
            [jnp.concatenate([w_ref[z, which, e] for z in range(shards)], axis=0) for e in range(pair)], axis=1
        )

    gate_w = weights(0)
    up_w = weights(1)
    down_w = weights(2)
    experts = gates_ref.shape[1]

    def tile(i, carry):
        here = pl.ds(pl.multiple_of(i * TM, TM), TM)
        x = x_ref[here, :]
        gate_val = nn(x, gate_w)
        up_val = nn(x, up_w)
        back = nn(g_ref[here, :], down_w)
        lanes = lax.broadcasted_iota(jnp.int32, (TM, experts), 1)
        gates = gates_ref[here, :]
        gate = jnp.concatenate(
            [
                jnp.broadcast_to(
                    jnp.sum(jnp.where(lanes == step * pair + e, gates, 0.0), axis=1, keepdims=True), (TM, ff)
                )
                for e in range(pair)
            ],
            axis=1,
        )
        sig = 1.0 / (1.0 + jnp.exp(-gate_val))
        silu = gate_val * sig
        inner = silu * up_val
        a_ref[here, :] = (inner * gate).astype(jnp.bfloat16)
        prod = inner * back
        for e in range(pair):
            dots_ref[0, here, e : e + 1] = jnp.sum(prod[:, e * ff : (e + 1) * ff], axis=1, keepdims=True)
        back = back * gate
        gu_ref[here, : pair * ff] = (back * up_val * sig * (1.0 + gate_val * (1.0 - sig))).astype(jnp.bfloat16)
        gu_ref[here, pair * ff :] = (back * silu).astype(jnp.bfloat16)
        return carry

    lax.fori_loop(0, rows // TM, tile, 0)
    for z in range(shards):
        part_rows = pl.ds(z * part, part)
        both = nn(xt_ref[part_rows, :], gu_ref[...])
        down = nn(gt_ref[part_rows, :], a_ref[...])
        for e in range(pair):
            grads_ref[z, 0, e] = both[:, e * ff : (e + 1) * ff].astype(jnp.bfloat16)
            grads_ref[z, 1, e] = both[:, (pair + e) * ff : (pair + e + 1) * ff].astype(jnp.bfloat16)
            grads_ref[z, 2, e] = down[:, e * ff : (e + 1) * ff].astype(jnp.bfloat16)

def moe_main(x, g, xt, gt, gates, w):
    rows, width = x.shape
    shards, three, count, part, ff = w.shape
    one = lambda shape: pl.BlockSpec(shape, lambda i: (0,) * len(shape), pipeline_mode=pl.Buffered(1))
    return pl.pallas_call(
        moe_body,
        grid=(count // PAIR,),
        in_specs=[
            one(x.shape), one(g.shape), one(xt.shape), one(gt.shape), one(gates.shape),
            pl.BlockSpec((shards, 3, PAIR, part, ff), lambda i: (0, 0, i, 0, 0)),
        ],
        out_specs=[
            pl.BlockSpec((rows, PAIR * ff), lambda i: (0, i)),
            pl.BlockSpec((rows, 2 * PAIR * ff), lambda i: (0, i)),
            pl.BlockSpec((shards, 3, PAIR, part, ff), lambda i: (0, 0, i, 0, 0)),
            pl.BlockSpec((1, rows, PAIR), lambda i: (i, 0, 0)),
        ],
        out_shape=[
            jax.ShapeDtypeStruct((rows, count * ff), jnp.bfloat16),
            jax.ShapeDtypeStruct((rows, 2 * count * ff), jnp.bfloat16),
            jax.ShapeDtypeStruct(w.shape, jnp.bfloat16),
            jax.ShapeDtypeStruct((count // PAIR, rows, PAIR), jnp.float32),
        ],
        compiler_params=pltpu.CompilerParams(vmem_limit_bytes=VL),
        cost_estimate=pl.CostEstimate(flops=2 * rows * width * count * ff * 6, bytes_accessed=8 * rows * width + 12 * count * ff * width, transcendentals=0),
        name="moe_main",
    )(x, g, xt, gt, gates, w)

def back_body(*refs, count, first, kinds):
    gu_refs, w_refs, o_ref = refs[:count], refs[count : 2 * count], refs[2 * count]
    shards, _, experts, part, ff = w_refs[0].shape
    for z in range(shards):
        total = None
        for gu_ref, w_ref in zip(gu_refs, w_refs):
            w = jnp.concatenate(
                [
                    w_ref[z, kind, p * PAIR + e]
                    for p in range(experts // PAIR)
                    for kind in range(kinds)
                    for e in range(PAIR)
                ],
                axis=1,
            )
            piece = nt(gu_ref[...], w)
            total = piece if total is None else total + piece
        o_ref[:, z * part : (z + 1) * part] = total.astype(o_ref.dtype)


def moe_back(gus, ws, first, kinds):
    shards, three, experts, part, ff = ws[0].shape
    rows = gus[0].shape[0]
    width = shards * part
    count = len(gus)
    return pl.pallas_call(
        functools.partial(back_body, count=count, first=first, kinds=kinds),
        grid=(rows // TM,),
        in_specs=[pl.BlockSpec((TM, kinds * experts * ff), lambda i: (i, 0)) for _ in gus]
        + [
            pl.BlockSpec(
                (shards, kinds, experts, part, ff),
                lambda i: (0, first // kinds, 0, 0, 0),
                pipeline_mode=pl.Buffered(1),
            )
            for _ in ws
        ],
        out_specs=pl.BlockSpec((TM, width), lambda i: (i, 0)),
        out_shape=jax.ShapeDtypeStruct((rows, width), jnp.bfloat16),
        compiler_params=pltpu.CompilerParams(vmem_limit_bytes=VL),
        cost_estimate=pl.CostEstimate(
            flops=2 * rows * width * count * experts * ff * kinds,
            bytes_accessed=2 * rows * kinds * count * experts * ff,
            transcendentals=0,
        ),
        name="moe_back" if kinds == 2 else "moe_out",
    )(*gus, *ws)


MESH = pl.DeviceIdType.MESH


class Place:
    def __init__(self):
        self.ctx = lax.axis_index("ctx")
        self.tp = lax.axis_index("tp")
        self.core = lax.rem(self.tp, 2)
        self.high = self.tp // 2
        self.pair_tp = self.high * 2 + 1 - self.core
        self.far_tp = (1 - self.high) * 2 + self.core
        self.cross_tp = (1 - self.high) * 2 + 1 - self.core
        self.pair = {"tp": self.pair_tp}
        self.far = {"tp": self.far_tp}
        self.side = {"ctx": 1 - self.ctx}

    def meet(self, who):
        barrier = pltpu.get_barrier_semaphore()
        for device in who:
            pl.semaphore_signal(barrier, inc=1, device_id=device, device_id_type=MESH)
        pl.semaphore_wait(barrier, len(who))


def push(src, dst, sems, slot, device):
    return pltpu.make_async_remote_copy(
        src_ref=src, dst_ref=dst, send_sem=sems.at[0, slot], recv_sem=sems.at[1, slot],
        device_id=device, device_id_type=MESH,
    )


def gather_four(place, all_ref, sems, at):
    here, far = all_ref.at[place.tp], all_ref.at[place.far_tp]
    to_far = push(here, here, sems, at, place.far)
    to_pair = push(here, here, sems, at + 1, place.pair)
    to_far.start()
    to_pair.start()
    to_far.wait_recv()
    on = push(far, far, sems, at + 2, place.pair)
    on.start()
    to_pair.wait_recv()
    on.wait_recv()
    to_far.wait_send()
    to_pair.wait_send()
    on.wait_send()


def gather_eight(place, all_ref, sems, at):
    rows = all_ref.shape[1]
    top, low = pl.ds(0, rows // 2), pl.ds(rows // 2, rows // 2)
    part = lambda ctx, tp: all_ref.at[ctx * 4 + tp]
    other = 1 - place.ctx
    here = part(place.ctx, place.tp)
    side = part(other, place.tp)
    far = part(place.ctx, place.far_tp)
    cross = part(other, place.far_tp)
    side_top, far_low = side.at[top], far.at[low]
    cross_top, cross_low = cross.at[top], cross.at[low]
    to_side = push(here, here, sems, at, place.side)
    to_far = push(here, here, sems, at + 1, place.far)
    to_pair = push(here, here, sems, at + 2, place.pair)
    for copy in (to_side, to_far, to_pair):
        copy.start()
    to_side.wait_recv()
    turn_far = push(side_top, side_top, sems, at + 3, place.far)
    pair_side = push(side, side, sems, at + 5, place.pair)
    turn_far.start()
    pair_side.start()
    to_far.wait_recv()
    turn_side = push(far_low, far_low, sems, at + 4, place.side)
    pair_far = push(far, far, sems, at + 6, place.pair)
    turn_side.start()
    pair_far.start()
    turn_far.wait_recv()
    pair_top = push(cross_top, cross_top, sems, at + 7, place.pair)
    pair_top.start()
    turn_side.wait_recv()
    pair_low = push(cross_low, cross_low, sems, at + 8, place.pair)
    pair_low.start()
    for copy in (to_pair, pair_side, pair_far, pair_top, pair_low):
        copy.wait_recv()
    for copy in (to_side, to_far, to_pair, turn_far, turn_side, pair_side, pair_far, pair_top, pair_low):
        copy.wait_send()


def reduce_four(place, produce, send_ref, pair_in, far_in, own_ref, sems, at):
    def fold(j):
        slot = j // 2

        @pl.when(lax.rem(j, 2) == place.core)
        def _():
            push(send_ref.at[j], pair_in.at[slot], sems, at + slot, place.pair).wait_recv()
            total = send_ref[j].astype(jnp.float32) + pair_in[slot].astype(jnp.float32)

            @pl.when(slot == place.high)
            def _():
                own_ref[...] = total

            @pl.when(slot != place.high)
            def _():
                send_ref[j] = total.astype(jnp.bfloat16)
                push(send_ref.at[j], far_in, sems, at + 2, place.far).start()

    def step(j, carry):
        produce(j)

        @pl.when(lax.rem(j, 2) != place.core)
        def _():
            slot = j // 2
            push(send_ref.at[j], pair_in.at[slot], sems, at + slot, place.pair).start()

        @pl.when(j > 0)
        def _():
            fold(j - 1)

        return carry

    lax.fori_loop(0, 4, step, 0)
    fold(3)
    last = push(send_ref.at[place.far_tp], far_in, sems, at + 2, place.far)
    last.wait_recv()
    own_ref[...] += far_in[...].astype(jnp.float32)
    last.wait_send()
    for slot in range(2):
        push(send_ref.at[place.pair_tp], pair_in.at[slot], sems, at + slot, place.pair).wait_send()


SMEMS = pl.BlockSpec(memory_space=pltpu.SMEM)
WHOLE = pl.BlockSpec(memory_space=pltpu.VMEM)


def normalize(x):
    r = lax.rsqrt(jnp.mean(x * x, axis=1, keepdims=True) + epsilon)
    return r, x * r


def mid_body(tok_ref, q_ref, k_ref, v_ref, docq_ref, blkq_ref, dock_ref, blkk_ref, w_ref, gain_ref,
             mix_ref, hid_ref, all_ref, send, pair_in, far_in, own, sems, *, share, length):
    place = Place()
    place.meet((place.pair, place.far, place.side))
    heads, rows, _ = q_ref.shape
    block = rows // 4
    band = min(DOC + block + BLK, length)

    def produce(j):
        at = pl.multiple_of(j * block, block)
        here = pl.ds(at, block)
        start = pl.multiple_of(jnp.clip(place.ctx * rows + at - DOC, 0, length - band), 128)
        keys = pl.ds(start, band)
        ok = (docq_ref[here, :] == dock_ref[:, keys]) & (blkk_ref[:, keys] <= blkq_ref[here, :])
        bias = jnp.where(ok, 0.0, masked_score)
        outs = []
        for head in range(heads):
            s = nt(q_ref[head, here, :], k_ref[head // share, keys, :]) + bias
            e = jnp.exp(s - jnp.max(s, axis=1, keepdims=True))
            p = e * (1.0 / jnp.sum(e, axis=1, keepdims=True))
            outs.append(nn(p.astype(jnp.bfloat16), v_ref[head // share, keys, :]).astype(jnp.bfloat16))
        mix = jnp.concatenate(outs, axis=1)
        mix_ref[here, :] = mix
        send[j] = nt(mix, w_ref[...]).astype(jnp.bfloat16)

    reduce_four(place, produce, send, pair_in, far_in, own, sems, 0)
    hidden = tok_ref[...].astype(jnp.float32) + own[...]
    hid_ref[...] = hidden
    all_ref[place.ctx * 4 + place.tp] = (normalize(hidden)[1] * gain_ref[...]).astype(jnp.bfloat16)
    gather_eight(place, all_ref, sems, 3)


def mid(tok, q, k, v, docq, blkq, dock, blkk, out_w, gain):
    heads, rows, _ = q.shape
    kv, length, _ = k.shape
    own, width = tok.shape
    return pl.pallas_call(
        functools.partial(mid_body, share=heads // kv, length=length),
        in_specs=[WHOLE] * 10,
        out_specs=[WHOLE] * 3,
        out_shape=[
            jax.ShapeDtypeStruct((rows, heads * HD), jnp.bfloat16),
            jax.ShapeDtypeStruct((own, width), jnp.float32),
            jax.ShapeDtypeStruct((8, own, width), jnp.bfloat16),
        ],
        scratch_shapes=[
            pltpu.VMEM((4, own, width), jnp.bfloat16),
            pltpu.VMEM((2, own, width), jnp.bfloat16),
            pltpu.VMEM((own, width), jnp.bfloat16),
            pltpu.VMEM((own, width), jnp.float32),
            pltpu.SemaphoreType.DMA((2, 12)),
        ],
        compiler_params=pltpu.CompilerParams(vmem_limit_bytes=VL, collective_id=0, has_side_effects=True),
        name="mid",
    )(tok, q, k, v, docq, blkq, dock, blkk, out_w, gain)


def tail_body(tok_ref, hg_ref, lin_ref, w_ref, gain_ref, all_ref, gg_ref, send, pair_in, far_in, own, sems):
    place = Place()
    place.meet((place.pair, place.far))
    block = lin_ref.shape[0] // 4

    def produce(j):
        here = pl.ds(pl.multiple_of(j * block, block), block)
        send[j] = nt(lin_ref[here, :], w_ref[...]).astype(jnp.bfloat16)

    reduce_four(place, produce, send, pair_in, far_in, own, sems, 0)
    one_grad = own[...]
    r, xhat = normalize(tok_ref[...].astype(jnp.float32))
    gg_ref[...] = jnp.sum(one_grad * xhat, axis=0, keepdims=True)
    n = one_grad * gain_ref[...]
    grad = hg_ref[...] + r * (n - xhat * jnp.mean(n * xhat, axis=1, keepdims=True))
    all_ref[place.tp] = grad.astype(jnp.bfloat16)
    gather_four(place, all_ref, sems, 3)


def tail(tok, hidden_grad, lin_grad, qkv_w, gain):
    own, width = tok.shape
    return pl.pallas_call(
        tail_body,
        in_specs=[WHOLE] * 5,
        out_specs=[WHOLE] * 2,
        out_shape=[
            jax.ShapeDtypeStruct((4, own, width), jnp.bfloat16),
            jax.ShapeDtypeStruct((1, width), jnp.float32),
        ],
        scratch_shapes=[
            pltpu.VMEM((4, own, width), jnp.bfloat16),
            pltpu.VMEM((2, own, width), jnp.bfloat16),
            pltpu.VMEM((own, width), jnp.bfloat16),
            pltpu.VMEM((own, width), jnp.float32),
            pltpu.SemaphoreType.DMA((2, 6)),
        ],
        compiler_params=pltpu.CompilerParams(vmem_limit_bytes=VL, collective_id=1, has_side_effects=True),
        name="tail",
    )(tok, hidden_grad, lin_grad, qkv_w, gain)


def turn_body(*refs, count, kinds, first, finish):
    gu_refs, w_refs = refs[:count], refs[count : 2 * count]
    lg_ref, router_ref, hid_ref, extra_ref, gain_ref = refs[2 * count : 2 * count + 5]
    outs = refs[2 * count + 5 : 2 * count + 8]
    gu_buf, gu_sem, give, keep, pair_in, cut, own, sems = refs[2 * count + 8 :]
    all_ref = outs[0]
    place = Place()
    place.meet((place.pair, place.far, place.side))
    block = hid_ref.shape[0]
    shards, _, experts, part, ff = w_refs[0].shape
    half = block // 2
    top, low = pl.ds(0, half), pl.ds(half, half)
    bf = jnp.bfloat16
    f = jnp.float32
    order = [(1, 1), (1, 0), (0, 1), (0, 0)]

    def tile_of(step):
        dx, dy = order[step // 2]
        ctx = place.ctx + dx * (1 - 2 * place.ctx)
        high = place.high + dy * (1 - 2 * place.high)
        core = 1 - place.core if step % 2 == 0 else place.core
        return ctx * 4 + high * 2 + core

    def fetch(step):
        at = pl.ds(pl.multiple_of(tile_of(step) * block, block), block)
        return [
            pltpu.make_async_copy(gu.at[at, :], gu_buf.at[step % 2, n], gu_sem.at[step % 2, n])
            for n, gu in enumerate(gu_refs)
        ]

    for copy in fetch(0):
        copy.start()

    def compute(step, dst):
        for copy in fetch(step):
            copy.wait()
        if step + 1 < 8:
            for copy in fetch(step + 1):
                copy.start()
        at = pl.ds(pl.multiple_of(tile_of(step) * block, block), block)
        for z in range(shards):
            cols = slice(z * part, (z + 1) * part)
            total = None
            if lg_ref is not None:
                total = nt(lg_ref[at, :], router_ref[cols, :])
            for n, w_ref in enumerate(w_refs):
                w = jnp.concatenate(
                    [
                        w_ref[z, kind, p * PAIR + e]
                        for p in range(experts // PAIR)
                        for kind in range(kinds)
                        for e in range(PAIR)
                    ],
                    axis=1,
                )
                piece = nt(gu_buf[step % 2, n], w)
                total = piece if total is None else total + piece
            dst[:, cols] = total.astype(bf)

    copies = []

    def send(src, dst, slot, device):
        copy = push(src, dst, sems, slot, device)
        copy.start()
        copies.append(copy)
        return copy

    for k in range(4):
        compute(2 * k, give.at[k])
        got = send(give.at[k], pair_in.at[k], k, place.pair)
        compute(2 * k + 1, keep.at[k])
        got.wait_recv()
        total = keep[k].astype(f) + pair_in[k].astype(f)
        if k == 0:
            keep[k] = total.astype(bf)
            a_cross = send(keep.at[k, top], cut.at[0], 4, place.side)
            b_cross = send(keep.at[k, low], cut.at[1], 5, place.far)
        elif k == 1:
            b_cross.wait_recv()
            keep[k, top] = total[:half].astype(bf)
            keep[k, low] = (total[half:] + cut[1].astype(f)).astype(bf)
            a_first = send(keep.at[k, top], cut.at[2], 6, place.side)
            b_last = send(keep.at[k, low], cut.at[5], 9, place.side)
        elif k == 2:
            a_cross.wait_recv()
            keep[k, low] = total[half:].astype(bf)
            keep[k, top] = (total[:half] + cut[0].astype(f)).astype(bf)
            b_first = send(keep.at[k, low], cut.at[4], 8, place.far)
            a_last = send(keep.at[k, top], cut.at[3], 7, place.far)
        else:
            for copy in (a_first, a_last, b_first, b_last):
                copy.wait_recv()
            own[top, :] = total[:half] + cut[2].astype(f) + cut[3].astype(f)
            own[low, :] = total[half:] + cut[4].astype(f) + cut[5].astype(f)
    finish(place, own, hid_ref, extra_ref, gain_ref, outs)
    gather_four(place, all_ref, sems, 10)
    for copy in copies:
        copy.wait_send()


def turn_back(place, own, hid_ref, grad_ref, gain_ref, outs):
    all_ref, hg_ref, gg_ref = outs
    two_grad = own[...]
    r, hhat = normalize(hid_ref[...])
    gg_ref[...] = jnp.sum(two_grad * hhat, axis=0, keepdims=True)
    m = two_grad * gain_ref[...]
    grad = grad_ref[...].astype(jnp.float32) + r * (m - hhat * jnp.mean(m * hhat, axis=1, keepdims=True))
    hg_ref[...] = grad
    all_ref[place.tp] = grad.astype(jnp.bfloat16)


def turn(gus, ws, logit_grad, router_w, hidden, grad_own, gain):
    shards, _, experts, part, ff = ws[0].shape
    own, width = hidden.shape
    count = len(gus)
    kinds = 2
    cols = gus[0].shape[1]
    anys = pl.BlockSpec(memory_space=pl.ANY)
    return pl.pallas_call(
        functools.partial(turn_body, count=count, kinds=kinds, first=0, finish=turn_back),
        grid=(1,),
        in_specs=[anys] * count
        + [
            pl.BlockSpec((shards, kinds, experts, part, ff), lambda i: (0, 0, 0, 0, 0), pipeline_mode=pl.Buffered(1))
            for _ in ws
        ]
        + [WHOLE] * 5,
        out_specs=[WHOLE] * 3,
        out_shape=[
            jax.ShapeDtypeStruct((4, own, width), jnp.bfloat16),
            jax.ShapeDtypeStruct((own, width), jnp.float32),
            jax.ShapeDtypeStruct((1, width), jnp.float32),
        ],
        scratch_shapes=[
            pltpu.VMEM((2, count, own, cols), jnp.bfloat16),
            pltpu.SemaphoreType.DMA((2, count)),
            pltpu.VMEM((4, own, width), jnp.bfloat16),
            pltpu.VMEM((4, own, width), jnp.bfloat16),
            pltpu.VMEM((4, own, width), jnp.bfloat16),
            pltpu.VMEM((6, own // 2, width), jnp.bfloat16),
            pltpu.VMEM((own, width), jnp.float32),
            pltpu.SemaphoreType.DMA((2, 13)),
        ],
        compiler_params=pltpu.CompilerParams(vmem_limit_bytes=VL, collective_id=2, has_side_effects=True),
        name="turn",
    )(*gus, *ws, logit_grad, router_w, hidden, grad_own, gain)


from jax.sharding import PartitionSpec as P

rope_base = 10000.0
CHUNKS = 4
bf16 = jnp.bfloat16
f32 = jnp.float32


def rope_tables(positions):
    half = HD // 2
    frequency = rope_base ** (-2.0 * jnp.arange(half, dtype=f32) / HD)
    angles = positions.astype(f32)[:, None] * frequency[None, :]
    return jnp.cos(angles)[:, None, :], jnp.sin(angles)[:, None, :]


def rotate(values, cosine, sine):
    shaped = values.reshape(values.shape[0], -1, HD)
    a, b = shaped[:, :, : HD // 2], shaped[:, :, HD // 2 :]
    return jnp.concatenate([a * cosine - b * sine, b * cosine + a * sine], axis=2)


def per_device(
    tokens, out_grad, doc_ids, block_ids, expert_ids, norm1_gain, w_query, w_key, w_value, w_out,
    norm2_gain, w_router, w_gate, w_up, w_down,
):
    shards = lax.axis_size("fsdp")
    ctx_size = lax.axis_size("ctx")
    tp_size = lax.axis_size("tp")
    ctx = lax.axis_index("ctx")
    tp = lax.axis_index("tp")
    rows, width = tokens.shape
    part = width // shards
    own = rows // tp_size
    length = doc_ids.shape[0]
    q_width, kv_width = w_query.shape[1], w_key.shape[1]
    heads, kv_heads = q_width // HD, kv_width // HD
    experts = w_gate.shape[0]
    mine = experts // ctx_size
    each = mine // CHUNKS
    ff = w_gate.shape[2]

    small = jnp.concatenate([w_router, norm1_gain[:, None], norm2_gain[:, None]], axis=1)
    spare = -small.shape[1] % 128
    packed = jnp.concatenate(
        [w_query, w_key, w_value, w_out.T, small, jnp.zeros((part, spare), bf16)], axis=1
    )
    packed = lax.all_gather(packed, "fsdp", axis=0, tiled=True)
    qkv_w = packed[:, : q_width + 2 * kv_width]
    at = q_width + 2 * kv_width
    out_w = packed[:, at : at + q_width]
    at += q_width
    router_w = packed[:, at : at + experts]
    gain_one = packed[:, at + experts].astype(f32)
    gain_two = packed[:, at + experts + 1].astype(f32)

    stacked = []
    for chunk in range(CHUNKS):
        first = ctx * mine + chunk * each
        pick = lambda w: lax.dynamic_slice_in_dim(w, first, each, 0)
        shard = jnp.stack([pick(w_gate), pick(w_up), pick(w_down).transpose(0, 2, 1)])
        stacked.append(lax.all_gather(shard, "fsdp", axis=0))
    grad_all = lax.all_gather(out_grad, "ctx", axis=0, tiled=True)
    ids_all = lax.all_gather(expert_ids, "ctx", axis=0, tiled=True)

    inputs = tokens.astype(f32)
    rms_one = lax.rsqrt(jnp.mean(inputs * inputs, axis=1, keepdims=True) + epsilon)
    normed = (inputs * rms_one * gain_one).astype(bf16)
    start = ctx * rows
    cosine, sine = rope_tables(start + jnp.arange(rows, dtype=jnp.int32))
    lin = jnp.dot(normed, qkv_w, preferred_element_type=f32)
    turned = rotate(lin[:, : q_width + kv_width], cosine, sine).astype(bf16)
    queries = turned[:, :heads].transpose(1, 0, 2) * bf16(HD**-0.5)
    keys_values = jnp.concatenate(
        [turned[:, heads:], lin[:, q_width + kv_width :].astype(bf16).reshape(rows, kv_heads, HD)], axis=1
    ).reshape(rows, 2 * kv_width)
    keys_values = lax.all_gather(keys_values, "ctx", axis=0, tiled=True)
    keys_values = keys_values.reshape(length, 2 * kv_heads, HD).transpose(1, 0, 2)
    keys, values = keys_values[:kv_heads], keys_values[kv_heads:]
    query_doc = lax.dynamic_slice_in_dim(doc_ids, start, rows)
    query_block = lax.dynamic_slice_in_dim(block_ids, start, rows)
    base = start.astype(jnp.int32).reshape(1)
    tokens_own = lax.dynamic_slice_in_dim(tokens, tp * own, own)
    grad_own = lax.dynamic_slice_in_dim(out_grad, tp * own, own)
    attn_mix, hidden, normed_two = mid(
        tokens_own, queries, keys, values, query_doc[:, None], query_block[:, None], doc_ids[None],
        block_ids[None], out_w, gain_two[None],
    )
    normed_two = normed_two.reshape(ctx_size * rows, width)

    logits = jnp.dot(normed_two, router_w, preferred_element_type=f32)
    chosen = jnp.any(ids_all[:, :, None] == jnp.arange(experts, dtype=jnp.int32)[None, None, :], axis=1)
    masked = jnp.where(chosen, logits, masked_score)
    powers = jnp.exp(masked - jnp.max(masked, axis=1, keepdims=True))
    gates = powers / jnp.sum(powers, axis=1, keepdims=True)
    gates_mine = lax.dynamic_slice_in_dim(gates, ctx * mine, mine, 1)

    normed_t, grad_t = normed_two.T, grad_all.T
    inner_all, outer_all, dots_all, shard_grads = [], [], [], []
    for chunk in range(CHUNKS):
        inner, outer, grads, dots = moe_main(
            normed_two, grad_all, normed_t, grad_t,
            gates_mine[:, chunk * each : (chunk + 1) * each], stacked[chunk],
        )
        inner_all.append(inner)
        outer_all.append(outer)
        dots_all.append(dots)
        scattered = lax.psum_scatter(grads, "fsdp", scatter_dimension=0, tiled=False)
        shard_grads.append(lax.all_gather(scattered, "ctx", axis=0))
    combined = moe_back(inner_all, stacked, 2, 1)

    dots = jnp.concatenate(dots_all, axis=0).transpose(1, 0, 2).reshape(ctx_size * rows, mine)
    weighted = gates_mine * dots
    dots_sum = jnp.sum(weighted, axis=1, keepdims=True)
    spread = lax.dynamic_update_slice_in_dim(jnp.zeros_like(gates), weighted, ctx * mine, 1)
    logit_grad = (spread - gates * dots_sum).astype(bf16)
    router_grad = lax.dot_general(
        normed_two, logit_grad, (((0,), (0,)), ((), ())), preferred_element_type=f32
    )
    branch_grad, hidden_grad, gain_two_grad = turn(
        outer_all, stacked, logit_grad, router_w, hidden, grad_own, gain_two[None]
    )
    branch_grad = branch_grad.reshape(rows, width)
    mixed = lax.psum_scatter(combined, ("ctx", "tp"), scatter_dimension=0, tiled=True)
    block_out = lax.all_gather((hidden + mixed.astype(f32)).astype(bf16), "tp", axis=0, tiled=True)

    out_w_grad = lax.dot_general(
        branch_grad, attn_mix, (((0,), (0,)), ((), ())), preferred_element_type=f32
    )
    mix_grad = jnp.dot(branch_grad, out_w, preferred_element_type=f32).astype(bf16)
    query_grad, key_grad, value_grad = flash_bwd(
        base, queries, mix_grad.reshape(rows, heads, HD).transpose(1, 0, 2), keys, values,
        query_doc[None], query_block[None], doc_ids[:, None], block_ids[:, None],
    )
    kv_grad = jnp.concatenate([key_grad, value_grad], axis=0).transpose(1, 0, 2).reshape(length, 2 * kv_width)
    kv_grad = lax.psum_scatter(kv_grad.astype(bf16), "ctx", scatter_dimension=0, tiled=True).astype(f32)
    query_grad = (query_grad * HD**-0.5).transpose(1, 0, 2).reshape(rows, q_width)
    turned_grad = rotate(
        jnp.concatenate([query_grad, kv_grad[:, :kv_width]], axis=1), cosine, -sine
    ).reshape(rows, q_width + kv_width)
    lin_grad = jnp.concatenate([turned_grad, kv_grad[:, kv_width:]], axis=1).astype(bf16)
    qkv_grad = lax.dot_general(normed, lin_grad, (((0,), (0,)), ((), ())), preferred_element_type=f32)

    input_grad, gain_one_grad = tail(tokens_own, hidden_grad, lin_grad, qkv_w, gain_one[None])
    input_grad = input_grad.reshape(rows, width)

    big = jnp.concatenate([qkv_grad, out_w_grad], axis=1).astype(bf16)
    big = lax.psum_scatter(big, "fsdp", scatter_dimension=0, tiled=True)
    big = lax.psum(big, "ctx").astype(f32)
    tiny = jnp.concatenate(
        [router_grad, gain_one_grad[0][:, None], gain_two_grad[0][:, None]], axis=1
    )
    tiny = lax.psum(lax.psum_scatter(tiny, "fsdp", scatter_dimension=0, tiled=True), ("ctx", "tp"))

    sums = jnp.stack(shard_grads, axis=1).astype(f32)
    gate_s, up_s, down_s = [sums[:, :, kind].reshape(experts, part, ff) for kind in range(3)]
    at = q_width + 2 * kv_width
    return (
        block_out,
        input_grad,
        tiny[:, experts],
        big[:, :q_width],
        big[:, q_width : q_width + kv_width],
        big[:, q_width + kv_width : at],
        big[:, at : at + q_width].T,
        tiny[:, experts + 1],
        tiny[:, :experts],
        gate_s,
        up_s,
        down_s.transpose(0, 2, 1),
    )


def solution(mesh):
    rows = P(("fsdp", "ctx"), None)
    return jax.shard_map(
        per_device,
        mesh=mesh,
        in_specs=(
            rows, rows, P("fsdp"), P("fsdp"), rows, P("fsdp"), P("fsdp", "tp"), P("fsdp", "tp"),
            P("fsdp", "tp"), P("tp", "fsdp"), P("fsdp"), P("fsdp", None), P(None, "fsdp", "tp"),
            P(None, "fsdp", "tp"), P(None, "tp", "fsdp"),
        ),
        out_specs=(
            rows, rows, P("fsdp"), P("fsdp", "tp"), P("fsdp", "tp"), P("fsdp", "tp"), P("tp", "fsdp"),
            P("fsdp"), P("fsdp", None), P(None, "fsdp", "tp"), P(None, "fsdp", "tp"), P(None, "tp", "fsdp"),
        ),
        check_vma=False,
    )
```

time: 3830 us -> 1280 us (0.33)
  waiting for transfers between devices: 1690 us -> 557 us
  matrix products: 703 us -> 24 us
  other arithmetic: 681 us -> 55 us
  Pallas kernels: 0 us -> 445 us
  local copies, waits for them, and re-layouts: 564 us -> 143 us
  blocking collectives: 163 us -> 29.3 us
    dot_general x119 -> x6, matrix products: 703 us -> 24 us  [the longest x1 4.71 us: per_device(): logits = jnp.dot(normed_two, router_w, preferred_element_type=f32)]
    reduce_scatter x10 -> x8, waiting for transfers between devices: 940 us -> 306 us  [the longest x4 205 us: per_device(): lax.psum_scatter(grads, 'fsdp', scatter_dimension=0, tiled=False)]
    psum x5 -> x1, waiting for transfers between devices: 473 us -> 1.65 us  [per_device(): big = lax.psum(big, 'ctx').astype(f32)]
    scatter-add x16 -> x0, other arithmetic: 460 us -> none  [the longest x8 230 us: backward_step(): grad_acc.at[rows_idx]]
    pallas_call x0 -> x9, Pallas kernels: none -> 445 us  [the longest x4 145 us: moe_main(): pl.pallas_call(moe_body, grid=(count // PAIR,), in_specs=[one(x.shape), o...]
    gather x33 -> x0, local copies, waits for them, and re-layouts: 418 us -> none  [the longest x16 129 us: expert_front(): taken_rows = normed_two[rows_idx].reshape(group_size, capacity, model_width)]
    all_gather x9 -> x1, blocking collectives: 129 us -> 5.68 us  [per_device(): ids_all = lax.all_gather(expert_ids, 'ctx', axis=0, tiled=True)]
    scatter x2 -> x0, local copies, waits for them, and re-layouts: 90.8 us -> none  [the longest x1 45.4 us: per_device(): jnp.zeros((slot_total,), jnp.int32).at[flat_slot].set(pair_rows)]
  transfers between devices with their start and end apart: 18 -> 21, of which waited for: 14 -> 18; matrix products, arithmetic and copies ran while one was open for 24% -> 10% of each run, Pallas kernels for 0% -> 22%
where the time goes in v1:
time: 1280 us; the launch traced here: 1270 us
  waiting for transfers between devices  557 us (44%)
  Pallas kernels  445 us (35%)
  local copies, waits for them, and re-layouts  143 us (11%)
  other arithmetic  55 us (4%)
  blocking collectives  29.3 us (2%)
  matrix products  24 us (2%)
  between operations  15.4 us (1%)
    reduce_scatter x4, waiting for transfers between devices, per_device(): lax.psum_scatter(grads, 'fsdp', scatter_dimension=0, tiled=False)  205 us
    pallas_call x4, Pallas kernels, moe_main(): pl.pallas_call(moe_body, grid=(count // PAIR,), in_specs=[one(x.shape), o...  145 us
    all_gather x4, waiting for transfers between devices, per_device(): shard_grads.append(lax.all_gather(scattered, 'ctx', axis=0))  104 us
    pallas_call x1, Pallas kernels, mid(): pl.pallas_call(functools.partial(mid_body, share=heads // kv, length=leng...  101 us
    all_gather x4, waiting for transfers between devices, per_device(): stacked.append(lax.all_gather(shard, 'fsdp', axis=0))  97.3 us
    pallas_call x1, Pallas kernels, turn(): pl.pallas_call(functools.partial(turn_body, count=count, kinds=kinds, fir...  74.9 us
    reduce_scatter x1, waiting for transfers between devices, per_device(): lax.psum_scatter(combined, ('ctx', 'tp'), scatter_dimension=0, tiled=True)  64.9 us
    pallas_call x1, Pallas kernels, flash_bwd(): pl.pallas_call(functools.partial(flash_bwd_body, share=heads // kv, lengt...  55.8 us
  transfers between devices with their start and end apart: 21, of which 18 were waited for; matrix products, arithmetic and copies ran while one was open for 10% of the time, Pallas kernels for 22%

profile of v1, /device:TPU:0, one launch (start us, length us, event | category | flops | bytes accessed | tf_op | source)
XLA Modules:
  0.0 1269.1 jit_solution(15131002607445652289)
XLA Ops:
  12.5 2.6 fusion
  15.1 4.3 fusion.13
  19.4 37.2 %all-gather.17.cloned.1.call-done = bf16[1024,896]{1,0:T(8,128)(2,1)} async-done(((bf16[256,896]{1,0:T(8,128)(2,1)}), bf16[1024,896]{1,0:T(8,128)(2,1)}) %all-gather.17.cloned.1.call-update) | async-done | bytes 1835024 | tf_op jit(solution)/shard_map/all_gather | solution.py:684
  58.7 4.1 fusion.11
  63.3 3.0 copy.220
  66.2 3.0 copy.221
  69.6 5.0 add_convert_fusion.1
  74.7 3.4 fusion.7
  79.5 4.6 copy.178
  100.7 5.7 all_gather.54
  114.3 3.2 copy.174
  119.4 101.2 %mid.1 = (bf16[1536,256]{1,0:T(8,128)(2,1)}, f32[384,1024]{1,0:T(8,128)}, bf16[8,384,1024]{2,1,0:T(8,128)(2,1)}) custom-call(bf16[384,1024]{1,0:T(8,128)(2,1)} %constant_dynamic-slice_fusion.9.tok_ref, bf16[4,1536,64]{2,1,0:T(8,128)(2,1)} %get-tuple-element.126.q_ref, bf16[2,3072,64]{2,1,0:T(8,128)(2,1)} %get-tuple-element.128.k_ref, ...), custom_call_target="tpu_custom_call" | custom-call | tf_op jit(solution)/shard_map/mid/pallas_call | solution.py:428
  220.6 8.7 copy.219
  229.3 4.7 fusion.24
  236.7 4.4 constant_dynamic-slice_fusion
  241.1 8.7 copy.183.g_ref
  249.7 21.9 %all-gather.39.cloned.1.call-done = bf16[12,4,256,128]{3,2,1,0:T(8,128)(2,1)} async-done(((bf16[3,4,256,128]{3,2,1,0:T(8,128)(2,1)}), bf16[12,4,256,128]{3,2,1,0:T(8,128)(2,1)}) %all-gather.39.cloned.1.call-update) | async-done | bytes 3145744 | tf_op jit(solution)/shard_map/all_gather | solution.py:698
  271.7 36.2 %moe_main.7 = (bf16[3072,512]{1,0:T(8,128)(2,1)}, bf16[3072,1024]{1,0:T(8,128)(2,1)}, bf16[4,3,4,256,128]{4,3,2,1,0:T(8,128)(2,1)}, f32[2,3072,2]{2,1,0:T(8,128)}) custom-call(bf16[3072,1024]{1,0:T(8,128)(2,1)} %bitcast.97, bf16[3072,1024]{1,0:T(8,128)(2,1)} %copy.183.g_ref, bf16[1024,3072]{1,0:T(8,128)(2,1)} %bitcast.110, bf16[1024,3072]{1,0:T(8,128)(2,1)} %bitcast.106, ...), custom_call_target="tpu_custom_call" | custom-call | flops 19327352832 | bytes 31457280 | tf_op jit(solution)/shard_map/moe_main/pallas_call | solution.py:184
  307.8 2.4 copy.196
  310.2 25.0 %all-gather.37.cloned.1.call-done = bf16[12,4,256,128]{3,2,1,0:T(8,128)(2,1)} async-done(((bf16[3,4,256,128]{3,2,1,0:T(8,128)(2,1)}), bf16[12,4,256,128]{3,2,1,0:T(8,128)(2,1)}) %all-gather.37.cloned.1.call-update) | async-done | bytes 3145744 | tf_op jit(solution)/shard_map/all_gather | solution.py:698
  335.2 36.5 %moe_main.6 = (bf16[3072,512]{1,0:T(8,128)(2,1)}, bf16[3072,1024]{1,0:T(8,128)(2,1)}, bf16[4,3,4,256,128]{4,3,2,1,0:T(8,128)(2,1)}, f32[2,3072,2]{2,1,0:T(8,128)}) custom-call(bf16[3072,1024]{1,0:T(8,128)(2,1)} %bitcast.98, bf16[3072,1024]{1,0:T(8,128)(2,1)} %copy.183.g_ref, bf16[1024,3072]{1,0:T(8,128)(2,1)} %bitcast.111, bf16[1024,3072]{1,0:T(8,128)(2,1)} %bitcast.107, ...), custom_call_target="tpu_custom_call" | custom-call | flops 19327352832 | bytes 31457280 | tf_op jit(solution)/shard_map/moe_main/pallas_call | solution.py:184
  371.7 2.4 copy.195
  374.1 25.2 %all-gather.35.cloned.1.call-done = bf16[12,4,256,128]{3,2,1,0:T(8,128)(2,1)} async-done(((bf16[3,4,256,128]{3,2,1,0:T(8,128)(2,1)}), bf16[12,4,256,128]{3,2,1,0:T(8,128)(2,1)}) %all-gather.35.cloned.1.call-update) | async-done | bytes 3145744 | tf_op jit(solution)/shard_map/all_gather | solution.py:698
  399.3 36.1 %moe_main.5 = (bf16[3072,512]{1,0:T(8,128)(2,1)}, bf16[3072,1024]{1,0:T(8,128)(2,1)}, bf16[4,3,4,256,128]{4,3,2,1,0:T(8,128)(2,1)}, f32[2,3072,2]{2,1,0:T(8,128)}) custom-call(bf16[3072,1024]{1,0:T(8,128)(2,1)} %bitcast.99, bf16[3072,1024]{1,0:T(8,128)(2,1)} %copy.183.g_ref, bf16[1024,3072]{1,0:T(8,128)(2,1)} %bitcast.112, bf16[1024,3072]{1,0:T(8,128)(2,1)} %bitcast.108, ...), custom_call_target="tpu_custom_call" | custom-call | flops 19327352832 | bytes 31457280 | tf_op jit(solution)/shard_map/moe_main/pallas_call | solution.py:184
  435.4 2.4 copy.194
  437.8 25.2 %all-gather.33.cloned.1.call-done = bf16[12,4,256,128]{3,2,1,0:T(8,128)(2,1)} async-done(((bf16[3,4,256,128]{3,2,1,0:T(8,128)(2,1)}), bf16[12,4,256,128]{3,2,1,0:T(8,128)(2,1)}) %all-gather.33.cloned.1.call-update) | async-done | bytes 3145744 | tf_op jit(solution)/shard_map/all_gather | solution.py:698
  463.0 35.7 %moe_main.4 = (bf16[3072,512]{1,0:T(8,128)(2,1)}, bf16[3072,1024]{1,0:T(8,128)(2,1)}, bf16[4,3,4,256,128]{4,3,2,1,0:T(8,128)(2,1)}, f32[2,3072,2]{2,1,0:T(8,128)}) custom-call(bf16[3072,1024]{1,0:T(8,128)(2,1)} %bitcast.100, bf16[3072,1024]{1,0:T(8,128)(2,1)} %copy.183.g_ref, bf16[1024,3072]{1,0:T(8,128)(2,1)} %bitcast.113, bf16[1024,3072]{1,0:T(8,128)(2,1)} %bitcast.109, ...), custom_call_target="tpu_custom_call" | custom-call | flops 19327352832 | bytes 31457280 | tf_op jit(solution)/shard_map/moe_main/pallas_call | solution.py:184
  498.7 2.4 copy.193
  503.1 3.0 fusion.17
  506.2 11.5 dynamic_update_slice.3
  517.8 2.6 subtract_convert_fusion.2.refs_8_
  520.3 74.9 %turn.1 = (bf16[4,384,1024]{2,1,0:T(8,128)(2,1)}, f32[384,1024]{1,0:T(8,128)}, f32[1,1024]{1,0:T(1,128)}) custom-call(bf16[3072,1024]{1,0:T(8,128)(2,1)} %get-tuple-element.45.refs_0_, bf16[3072,1024]{1,0:T(8,128)(2,1)} %get-tuple-element.46.refs_1_, bf16[3072,1024]{1,0:T(8,128)(2,1)} %get-tuple-element.47.refs_2_, ...), custom_call_target="tpu_custom_call" | custom-call | tf_op jit(solution)/shard_map/turn/pallas_call | solution.py:608
  595.2 3.0 convolution_convert_fusion
  599.7 55.8 %flash_bwd.1 = (f32[4,1536,64]{2,1,0:T(8,128)}, f32[2,3072,64]{2,1,0:T(8,128)}, f32[2,3072,64]{2,1,0:T(8,128)}) custom-call(s32[1]{0:T(128)} %bitcast.33.base_ref, bf16[4,1536,64]{2,1,0:T(8,128)(2,1)} %get-tuple-element.126.q_ref, bf16[4,1536,64]{2,1,0:T(8,128)(2,1)} %bitcast.116, bf16[2,3072,64]{2,1,0:T(8,128)(2,1)} %get-tuple-element.128.k_ref, ...), custom_call_target="tpu_custom_call" | custom-call | tf_op jit(solution)/shard_map/flash_bwd/pallas_call | solution.py:97
  659.2 2.5 copy.203
  661.7 2.6 copy.204
  668.6 4.2 convolution_convert_fusion.2
  672.8 16.4 %reduce-scatter.11.cloned.1.call-done = bf16[1536,256]{1,0:T(8,128)(2,1)} async-done(((bf16[3072,256]{1,0:T(8,128)(2,1)}), bf16[1536,256]{1,0:T(8,128)(2,1)}) %reduce-scatter.11.cloned.1.call-update) | async-done | bytes 786448 | tf_op jit(solution)/shard_map/reduce_scatter | solution.py:772
  691.8 2.9 copy.226
  694.7 3.0 copy.227
  697.6 5.0 subtract_convert_fusion
  706.0 3.9 convolution_convert_fusion.1
  714.0 18.3 %moe_out.1 = bf16[3072,1024]{1,0:T(8,128)(2,1)} custom-call(bf16[3072,512]{1,0:T(8,128)(2,1)} %get-tuple-element.41.refs_0_, bf16[3072,512]{1,0:T(8,128)(2,1)} %get-tuple-element.42.refs_1_, bf16[3072,512]{1,0:T(8,128)(2,1)} %get-tuple-element.43.refs_2_, bf16[3072,512]{1,0:T(8,128)(2,1)} %get-tuple-element.44.refs_3_, ...), custom_call_target="tpu_custom_call" | custom-call | flops 12884901888 | bytes 12582912 | tf_op jit(solution)/shard_map/moe_out/pallas_call | solution.py:233
  732.4 2.3 slice.131.w_ref
  734.7 4.0 fusion.25
  740.0 49.8 %tail.1 = (bf16[4,384,1024]{2,1,0:T(8,128)(2,1)}, f32[1,1024]{1,0:T(1,128)}) custom-call(bf16[384,1024]{1,0:T(8,128)(2,1)} %constant_dynamic-slice_fusion.9.tok_ref, f32[384,1024]{1,0:T(8,128)} %get-tuple-element.53.hg_ref, bf16[1536,512]{1,0:T(8,128)(2,1)} %pad_maximum_fusion.3.lin_ref, bf16[1024,512]{1,0:T(8,128)(2,1)} %slice.131.w_ref, f32[1,1024]{1,0:T(1,128)} %bitcast.152), custom_call_target="tpu_custom_call" | custom-call | tf_op jit(solution)/shard_map/tail/pallas_call | solution.py:470
  791.9 16.3 %reduce-scatter.23.cloned.1.call-done = bf16[1,3,4,256,128]{4,3,2,1,0:T(8,128)(2,1)} async-done(((bf16[4,3,4,256,128]{4,3,2,1,0:T(8,128)(2,1)}), bf16[1,3,4,256,128]{4,3,2,1,0:T(8,128)(2,1)}) %reduce-scatter.23.cloned.1.call-update) | async-done | bytes 786448 | tf_op jit(solution)/shard_map/reduce_scatter | solution.py:744
  808.3 62.6 %reduce-scatter.21.cloned.1.call-done = bf16[1,3,4,256,128]{4,3,2,1,0:T(8,128)(2,1)} async-done(((bf16[4,3,4,256,128]{4,3,2,1,0:T(8,128)(2,1)}), bf16[1,3,4,256,128]{4,3,2,1,0:T(8,128)(2,1)}) %reduce-scatter.21.cloned.1.call-update) | async-done | bytes 786448 | tf_op jit(solution)/shard_map/reduce_scatter | solution.py:744
  871.0 63.0 %reduce-scatter.19.cloned.1.call-done = bf16[1,3,4,256,128]{4,3,2,1,0:T(8,128)(2,1)} async-done(((bf16[4,3,4,256,128]{4,3,2,1,0:T(8,128)(2,1)}), bf16[1,3,4,256,128]{4,3,2,1,0:T(8,128)(2,1)}) %reduce-scatter.19.cloned.1.call-update) | async-done | bytes 786448 | tf_op jit(solution)/shard_map/reduce_scatter | solution.py:744
  934.1 63.2 %reduce-scatter.17.cloned.1.call-done = bf16[1,3,4,256,128]{4,3,2,1,0:T(8,128)(2,1)} async-done(((bf16[4,3,4,256,128]{4,3,2,1,0:T(8,128)(2,1)}), bf16[1,3,4,256,128]{4,3,2,1,0:T(8,128)(2,1)}) %reduce-scatter.17.cloned.1.call-update) | async-done | bytes 786448 | tf_op jit(solution)/shard_map/reduce_scatter | solution.py:744
  997.3 64.9 %reduce-scatter.9.cloned.1.call-done = bf16[384,1024]{1,0:T(8,128)(2,1)} async-done(((bf16[3072,1024]{1,0:T(8,128)(2,1)}), bf16[384,1024]{1,0:T(8,128)(2,1)}) %reduce-scatter.9.cloned.1.call-update) | async-done | bytes 786448 | tf_op jit(solution)/shard_map/reduce_scatter | solution.py:760
  1062.2 2.3 add_convert_fusion.2
  1064.5 19.9 %reduce-scatter.13.cloned.1.call-done = f32[256,34]{0,1:T(8,128)} async-done(((f32[1024,34]{0,1:T(8,128)}), f32[256,34]{0,1:T(8,128)}) %reduce-scatter.13.cloned.1.call-update) | async-done | bytes 34832 | tf_op jit(solution)/shard_map/reduce_scatter | solution.py:789
  1084.4 23.6 %psum.14 = f32[256,34]{0,1:T(8,128)S(1)} all-reduce(f32[256,34]{0,1:T(8,128)} %reduce-scatter.13.cloned.1.call-done), channel_id=1, replica_groups=mesh['fsdp'=4,'ctx'=2,'tp'=4] {'ctx','tp'}, use_global_device_ids=true, to_apply=%region_8.9 | all-reduce | flops 8704 | bytes 69632 | tf_op jit(solution)/shard_map/psum | solution.py:789
  1115.9 23.5 %all-gather.31.cloned.1.call-done = bf16[2,3,4,256,128]{4,3,2,1,0:T(8,128)(2,1)} async-done(((bf16[1,3,4,256,128]{4,3,2,1,0:T(8,128)(2,1)}), bf16[2,3,4,256,128]{4,3,2,1,0:T(8,128)(2,1)}) %all-gather.31.cloned.1.call-update) | async-done | bytes 1572880 | tf_op jit(solution)/shard_map/all_gather | solution.py:745
  1140.9 27.1 %all-gather.29.cloned.1.call-done = bf16[2,3,4,256,128]{4,3,2,1,0:T(8,128)(2,1)} async-done(((bf16[1,3,4,256,128]{4,3,2,1,0:T(8,128)(2,1)}), bf16[2,3,4,256,128]{4,3,2,1,0:T(8,128)(2,1)}) %all-gather.29.cloned.1.call-update) | async-done | bytes 1572880 | tf_op jit(solution)/shard_map/all_gather | solution.py:745
  1169.5 27.2 %all-gather.27.cloned.1.call-done = bf16[2,3,4,256,128]{4,3,2,1,0:T(8,128)(2,1)} async-done(((bf16[1,3,4,256,128]{4,3,2,1,0:T(8,128)(2,1)}), bf16[2,3,4,256,128]{4,3,2,1,0:T(8,128)(2,1)}) %all-gather.27.cloned.1.call-update) | async-done | bytes 1572880 | tf_op jit(solution)/shard_map/all_gather | solution.py:745
  1196.8 2.7 copy.234
  1199.5 25.9 %all-gather.25.cloned.1.call-done = bf16[2,3,4,256,128]{4,3,2,1,0:T(8,128)(2,1)} async-done(((bf16[1,3,4,256,128]{4,3,2,1,0:T(8,128)(2,1)}), bf16[2,3,4,256,128]{4,3,2,1,0:T(8,128)(2,1)}) %all-gather.25.cloned.1.call-update) | async-done | bytes 1572880 | tf_op jit(solution)/shard_map/all_gather | solution.py:745
  1227.3 4.9 maximum_convert_fusion
  1232.2 10.8 fusion.18
  1243.0 5.6 copy.217
  1248.6 7.5 all-gather.23.cloned.1.call-done
  1256.1 4.0 copy.241
  (170 shorter events, 77.9 us)
Async XLA Ops:
  7.2 49.5 %all-gather.17.cloned.1.call-start = ((), (), s32[]{:S(2)}) async-start(), calls=%async_computation.8 | async-start | bytes 2293760 | tf_op jit(solution)/shard_map/all_gather | solution.py:684
  12.4 101.9 %all-gather.19.cloned.1.call-start = ((), (), s32[]{:S(2)}) async-start(), calls=%async_computation.9 | async-start | bytes 2359296 | tf_op jit(solution)/shard_map/all_gather | solution.py:713
  15.1 47.8 %copy-start.21 = (f32[1536]{0:T(1024)}, f32[1536]{0:T(1024)S(1)}, u32[]{:S(2)}) copy-start(f32[1536]{0:T(1024)S(1)} %add_rsqrt_fusion) | copy-start | bytes 18436
  19.4 50.2 %copy-start.1 = (f32[1536,32]{1,0:T(8,128)}, f32[1536,32]{1,0:T(8,128)S(1)}, u32[]{:S(2)}) copy-start(f32[1536,32]{1,0:T(8,128)S(1)} %get-tuple-element.157) | copy-start | bytes 589828
  58.7 4.2 copy-start.19
  66.2 3.3 copy-start.9
  79.4 161.6 %all-gather.21.cloned.1.call-start = ((), (), s32[]{:S(2)}) async-start(), calls=%async_computation.10 | async-start | bytes 9437184 | tf_op jit(solution)/shard_map/all_gather | solution.py:699
  84.1 1.8 copy-start.12
  84.1 187.5 %all-gather.39.cloned.1.call-start = ((), (), s32[]{:S(2)}) async-start(), calls=%async_computation.28 | async-start | bytes 3932160 | tf_op jit(solution)/shard_map/all_gather | solution.py:698
  89.0 246.2 %all-gather.37.cloned.1.call-start = ((), (), s32[]{:S(2)}) async-start(), calls=%async_computation.27 | async-start | bytes 3932160 | tf_op jit(solution)/shard_map/all_gather | solution.py:698
  90.3 309.1 %all-gather.35.cloned.1.call-start = ((), (), s32[]{:S(2)}) async-start(), calls=%async_computation.26 | async-start | bytes 3932160 | tf_op jit(solution)/shard_map/all_gather | solution.py:698
  91.5 371.5 %all-gather.33.cloned.1.call-start = ((), (), s32[]{:S(2)}) async-start(), calls=%async_computation.25 | async-start | bytes 3932160 | tf_op jit(solution)/shard_map/all_gather | solution.py:698
  92.7 4.4 copy-start.16
  92.7 6.2 copy-start.17
  92.7 596.5 %reduce-scatter.11.cloned.1.call-start = ((), (), s32[]{:S(2)}) async-start(), calls=%async_computation.13 | async-start | bytes 2359296 | tf_op jit(solution)/shard_map/reduce_scatter | solution.py:772
  92.8 7.9 copy-start.18
  235.0 6.1 copy-start.14
  506.1 11.6 copy-start.15
  655.5 2.8 copy-start.7
  664.3 127.1 %reduce-scatter.15.cloned.1.call-start = ((), (), s32[]{:S(2)}) async-start(), calls=%async_computation.15 | async-start | bytes 1966080 | tf_op jit(solution)/shard_map/reduce_scatter | solution.py:784
  672.8 18.6 %copy-start.4 = (f32[1536,4,64]{0,2,1:T(8,128)S(1)}, f32[1536,4,64]{0,2,1:T(8,128)}, u32[]{:S(2)}) copy-start(f32[1536,4,64]{0,2,1:T(8,128)} %copy.202) | copy-start | bytes 4718596
  694.7 3.0 copy-start.2
  694.7 3.0 copy-start.8
  704.0 1.8 copy-start.20
  704.0 1.8 copy-start.22
  705.0 1.0 copy-start.11
  706.0 3.9 copy-start.13
  711.3 97.0 %reduce-scatter.23.cloned.1.call-start = ((), (), s32[]{:S(2)}) async-start(), calls=%async_computation.23 | async-start | bytes 3932160 | tf_op jit(solution)/shard_map/reduce_scatter | solution.py:744
  711.8 159.1 %reduce-scatter.21.cloned.1.call-start = ((), (), s32[]{:S(2)}) async-start(), calls=%async_computation.21 | async-start | bytes 3932160 | tf_op jit(solution)/shard_map/reduce_scatter | solution.py:744
  712.6 221.4 %reduce-scatter.19.cloned.1.call-start = ((), (), s32[]{:S(2)}) async-start(), calls=%async_computation.19 | async-start | bytes 3932160 | tf_op jit(solution)/shard_map/reduce_scatter | solution.py:744
  713.2 284.1 %reduce-scatter.17.cloned.1.call-start = ((), (), s32[]{:S(2)}) async-start(), calls=%async_computation.17 | async-start | bytes 3932160 | tf_op jit(solution)/shard_map/reduce_scatter | solution.py:744
  713.9 348.3 %reduce-scatter.9.cloned.1.call-start = ((), (), s32[]{:S(2)}) async-start(), calls=%async_computation.11 | async-start | bytes 7077888 | tf_op jit(solution)/shard_map/reduce_scatter | solution.py:760
  732.3 2.4 copy-start
  732.3 352.1 %reduce-scatter.13.cloned.1.call-start = ((), (), s32[]{:S(2)}) async-start(), calls=%async_computation.14 | async-start | bytes 204800 | tf_op jit(solution)/shard_map/reduce_scatter | solution.py:789
  740.0 49.8 %copy-start.23 = (f32[1,1024]{1,0:T(1,128)S(1)}, f32[1,1024]{1,0:T(1,128)}, u32[]{:S(2)}) copy-start(f32[1,1024]{1,0:T(1,128)} %get-tuple-element.60) | copy-start | bytes 12292
  789.8 272.4 %copy-start.5 = (f32[384,1024]{1,0:T(8,128)S(1)}, f32[384,1024]{1,0:T(8,128)}, u32[]{:S(2)}) copy-start(f32[384,1024]{1,0:T(8,128)} %get-tuple-element.39.refs_10_) | copy-start | bytes 4718596
  791.3 319.5 %all-reduce.2.cloned.1.call-start = ((), (), s32[]{:S(2)}) async-start(), calls=%async_computation.16 | async-start | bytes 786432 | tf_op jit(solution)/shard_map/psum | solution.py:785
  791.9 347.5 %all-gather.31.cloned.1.call-start = ((), (), s32[]{:S(2)}) async-start(), calls=%async_computation.24 | async-start | bytes 2359296 | tf_op jit(solution)/shard_map/all_gather | solution.py:745
  808.3 359.7 %all-gather.29.cloned.1.call-start = ((), (), s32[]{:S(2)}) async-start(), calls=%async_computation.22 | async-start | bytes 2359296 | tf_op jit(solution)/shard_map/all_gather | solution.py:745
  871.0 325.8 %all-gather.27.cloned.1.call-start = ((), (), s32[]{:S(2)}) async-start(), calls=%async_computation.20 | async-start | bytes 2359296 | tf_op jit(solution)/shard_map/all_gather | solution.py:745
  934.0 291.4 %all-gather.25.cloned.1.call-start = ((), (), s32[]{:S(2)}) async-start(), calls=%async_computation.18 | async-start | bytes 2359296 | tf_op jit(solution)/shard_map/all_gather | solution.py:745
  997.3 258.8 %all-gather.23.cloned.1.call-start = ((), (), s32[]{:S(2)}) async-start(), calls=%async_computation.12 | async-start | bytes 3932160 | tf_op jit(solution)/shard_map/all_gather | solution.py:761
  1110.8 4.2 copy-start.10
  1225.4 1.9 copy-start.3
  1256.1 4.0 copy-start.6
Sparse Core Ops, SparseCore 0:
  12.5 44.0 all-gather.16
  79.6 27.0 all-gather.18
  108.8 97.2 all-gather.20
  207.4 64.1 all-gather.38
  273.1 62.0 all-gather.36
  337.2 62.0 all-gather.34
  400.9 62.0 all-gather.32
  664.4 24.7 reduce-scatter.10
  711.4 35.4 reduce-scatter.14
  749.0 59.2 reduce-scatter.22
  810.6 60.3 reduce-scatter.20
  873.7 60.3 reduce-scatter.18
  936.9 60.3 reduce-scatter.16
  1000.5 61.6 reduce-scatter.8
  1064.8 19.5 reduce-scatter.12
  1086.6 24.2 all-reduce.1
  1112.2 27.1 all-gather.30
  1140.8 27.1 all-gather.28
  1169.6 27.1 all-gather.26
  1198.2 27.1 all-gather.24
  1227.5 28.5 all-gather.22

commit v2 on v1

--- a/solution.py
+++ b/solution.py
@@ -117,6 +117,7 @@
             jax.ShapeDtypeStruct(v.shape, jnp.float32),
         ],
         compiler_params=pltpu.CompilerParams(vmem_limit_bytes=VL),
+        cost_estimate=busy(55),
         name="flash_bwd",
     )(base, q, g, k, v, docq, blkq, dock, blkk)
 
@@ -442,6 +443,7 @@
             pltpu.SemaphoreType.DMA((2, 12)),
         ],
         compiler_params=pltpu.CompilerParams(vmem_limit_bytes=VL, collective_id=0, has_side_effects=True),
+        cost_estimate=busy(100),
         name="mid",
     )(tok, q, k, v, docq, blkq, dock, blkk, out_w, gain)
 
@@ -483,6 +485,7 @@
             pltpu.SemaphoreType.DMA((2, 6)),
         ],
         compiler_params=pltpu.CompilerParams(vmem_limit_bytes=VL, collective_id=1, has_side_effects=True),
+        cost_estimate=busy(50),
         name="tail",
     )(tok, hidden_grad, lin_grad, qkv_w, gain)
 
@@ -631,6 +634,7 @@
             pltpu.SemaphoreType.DMA((2, 13)),
         ],
         compiler_params=pltpu.CompilerParams(vmem_limit_bytes=VL, collective_id=2, has_side_effects=True),
+        cost_estimate=busy(75),
         name="turn",
     )(*gus, *ws, logit_grad, router_w, hidden, grad_own, gain)
 
@@ -648,6 +652,18 @@
     frequency = rope_base ** (-2.0 * jnp.arange(half, dtype=f32) / HD)
     angles = positions.astype(f32)[:, None] * frequency[None, :]
     return jnp.cos(angles)[:, None, :], jnp.sin(angles)[:, None, :]
+
+
+def busy(us):
+    return pl.CostEstimate(flops=int(us * 1e9), bytes_accessed=1 << 20, transcendentals=0)
+
+
+def swap(x):
+    return lax.ppermute(x, "ctx", [(0, 1), (1, 0)])
+
+
+def after(x, *done):
+    return lax.optimization_barrier((x, *done))
 
 
 def rotate(values, cosine, sine):
@@ -677,11 +693,20 @@
     ff = w_gate.shape[2]
 
     small = jnp.concatenate([w_router, norm1_gain[:, None], norm2_gain[:, None]], axis=1)
+    ordered = lambda here, there, axis=0: jnp.concatenate(
+        [jnp.where(ctx == 0, here, there), jnp.where(ctx == 0, there, here)], axis=axis
+    )
     spare = -small.shape[1] % 128
     packed = jnp.concatenate(
         [w_query, w_key, w_value, w_out.T, small, jnp.zeros((part, spare), bf16)], axis=1
     )
     packed = lax.all_gather(packed, "fsdp", axis=0, tiled=True)
+    shard_list = []
+    for chunk in range(CHUNKS):
+        first = ctx * mine + chunk * each
+        pick = lambda w: lax.dynamic_slice_in_dim(w, first, each, 0)
+        shard_list.append(jnp.stack([pick(w_gate), pick(w_up), pick(w_down).transpose(0, 2, 1)]))
+    packed, *shard_list = after(packed, *shard_list)
     qkv_w = packed[:, : q_width + 2 * kv_width]
     at = q_width + 2 * kv_width
     out_w = packed[:, at : at + q_width]
@@ -690,14 +715,8 @@
     gain_one = packed[:, at + experts].astype(f32)
     gain_two = packed[:, at + experts + 1].astype(f32)
 
-    stacked = []
-    for chunk in range(CHUNKS):
-        first = ctx * mine + chunk * each
-        pick = lambda w: lax.dynamic_slice_in_dim(w, first, each, 0)
-        shard = jnp.stack([pick(w_gate), pick(w_up), pick(w_down).transpose(0, 2, 1)])
-        stacked.append(lax.all_gather(shard, "fsdp", axis=0))
-    grad_all = lax.all_gather(out_grad, "ctx", axis=0, tiled=True)
-    ids_all = lax.all_gather(expert_ids, "ctx", axis=0, tiled=True)
+    stacked = [lax.all_gather(shard, "fsdp", axis=0) for shard in shard_list]
+    ids_all = ordered(expert_ids, swap(expert_ids))
 
     inputs = tokens.astype(f32)
     rms_one = lax.rsqrt(jnp.mean(inputs * inputs, axis=1, keepdims=True) + epsilon)
@@ -710,7 +729,9 @@
     keys_values = jnp.concatenate(
         [turned[:, heads:], lin[:, q_width + kv_width :].astype(bf16).reshape(rows, kv_heads, HD)], axis=1
     ).reshape(rows, 2 * kv_width)
-    keys_values = lax.all_gather(keys_values, "ctx", axis=0, tiled=True)
+    keys_values = ordered(keys_values, swap(keys_values))
+    grad_here, keys_values = after(out_grad, keys_values)
+    grad_all = ordered(grad_here, swap(grad_here))
     keys_values = keys_values.reshape(length, 2 * kv_heads, HD).transpose(1, 0, 2)
     keys, values = keys_values[:kv_heads], keys_values[kv_heads:]
     query_doc = lax.dynamic_slice_in_dim(doc_ids, start, rows)
@@ -741,8 +762,7 @@
         inner_all.append(inner)
         outer_all.append(outer)
         dots_all.append(dots)
-        scattered = lax.psum_scatter(grads, "fsdp", scatter_dimension=0, tiled=False)
-        shard_grads.append(lax.all_gather(scattered, "ctx", axis=0))
+        shard_grads.append(lax.psum_scatter(grads, "fsdp", scatter_dimension=0, tiled=False))
     combined = moe_back(inner_all, stacked, 2, 1)
 
     dots = jnp.concatenate(dots_all, axis=0).transpose(1, 0, 2).reshape(ctx_size * rows, mine)
@@ -753,12 +773,13 @@
     router_grad = lax.dot_general(
         normed_two, logit_grad, (((0,), (0,)), ((), ())), preferred_element_type=f32
     )
+    grad_own, shard_grads[0] = after(grad_own, shard_grads[0])
     branch_grad, hidden_grad, gain_two_grad = turn(
         outer_all, stacked, logit_grad, router_w, hidden, grad_own, gain_two[None]
     )
+    branch_grad, *first = after(branch_grad, *shard_grads[:3])
+    there = [swap(piece) for piece in first]
     branch_grad = branch_grad.reshape(rows, width)
-    mixed = lax.psum_scatter(combined, ("ctx", "tp"), scatter_dimension=0, tiled=True)
-    block_out = lax.all_gather((hidden + mixed.astype(f32)).astype(bf16), "tp", axis=0, tiled=True)
 
     out_w_grad = lax.dot_general(
         branch_grad, attn_mix, (((0,), (0,)), ((), ())), preferred_element_type=f32
@@ -768,8 +789,14 @@
         base, queries, mix_grad.reshape(rows, heads, HD).transpose(1, 0, 2), keys, values,
         query_doc[None], query_block[None], doc_ids[:, None], block_ids[:, None],
     )
+    query_grad, key_grad, value_grad, *there = after(query_grad, key_grad, value_grad, *there)
     kv_grad = jnp.concatenate([key_grad, value_grad], axis=0).transpose(1, 0, 2).reshape(length, 2 * kv_width)
-    kv_grad = lax.psum_scatter(kv_grad.astype(bf16), "ctx", scatter_dimension=0, tiled=True).astype(f32)
+    kv_grad = kv_grad.astype(bf16)
+    kept = lax.dynamic_slice_in_dim(kv_grad, start, rows)
+    given = lax.dynamic_slice_in_dim(kv_grad, rows - start, rows)
+    kv_grad = kept.astype(f32) + swap(given).astype(f32)
+    kv_grad, last = after(kv_grad, shard_grads[3])
+    there.append(swap(last))
     query_grad = (query_grad * HD**-0.5).transpose(1, 0, 2).reshape(rows, q_width)
     turned_grad = rotate(
         jnp.concatenate([query_grad, kv_grad[:, :kv_width]], axis=1), cosine, -sine
@@ -779,28 +806,36 @@
 
     input_grad, gain_one_grad = tail(tokens_own, hidden_grad, lin_grad, qkv_w, gain_one[None])
     input_grad = input_grad.reshape(rows, width)
+    hidden, gain_one_grad = after(hidden, gain_one_grad)
+    mixed = lax.psum_scatter(combined, ("ctx", "tp"), scatter_dimension=0, tiled=True)
+    block_out = lax.all_gather((hidden + mixed.astype(f32)).astype(bf16), "tp", axis=0, tiled=True)
 
     big = jnp.concatenate([qkv_grad, out_w_grad], axis=1).astype(bf16)
     big = lax.psum_scatter(big, "fsdp", scatter_dimension=0, tiled=True)
-    big = lax.psum(big, "ctx").astype(f32)
-    tiny = jnp.concatenate(
-        [router_grad, gain_one_grad[0][:, None], gain_two_grad[0][:, None]], axis=1
-    )
-    tiny = lax.psum(lax.psum_scatter(tiny, "fsdp", scatter_dimension=0, tiled=True), ("ctx", "tp"))
-
-    sums = jnp.stack(shard_grads, axis=1).astype(f32)
-    gate_s, up_s, down_s = [sums[:, :, kind].reshape(experts, part, ff) for kind in range(3)]
+    big = big.astype(f32) + swap(big).astype(f32)
+    everywhere = ("fsdp", "ctx", "tp")
+    tiny = lax.psum(jnp.concatenate([router_grad.T, gain_two_grad], axis=0), everywhere)
+    gain_one_grad = lax.psum(gain_one_grad, everywhere)[0]
+    mine_of = lambda x: lax.dynamic_slice_in_dim(x, lax.axis_index("fsdp") * part, part, x.ndim - 1)
+
+    gate_s, up_s, down_s = [
+        ordered(
+            jnp.concatenate([piece[kind] for piece in shard_grads]),
+            jnp.concatenate([piece[kind] for piece in there]),
+        ).astype(f32)
+        for kind in range(3)
+    ]
     at = q_width + 2 * kv_width
     return (
         block_out,
         input_grad,
-        tiny[:, experts],
+        mine_of(gain_one_grad),
         big[:, :q_width],
         big[:, q_width : q_width + kv_width],
         big[:, q_width + kv_width : at],
         big[:, at : at + q_width].T,
-        tiny[:, experts + 1],
-        tiny[:, :experts],
+        mine_of(tiny[experts]),
+        mine_of(tiny[:experts]).T,
         gate_s,
         up_s,
         down_s.transpose(0, 2, 1),

time: 1280 us -> 877 us (0.69)
  waiting for transfers between devices: 557 us -> 119 us
  blocking collectives: 29.3 us -> 46.4 us
  other arithmetic: 55 us -> 68.2 us
    reduce_scatter x4, waiting for transfers between devices: 205 us -> 0.08 us  [per_device(): lax.psum_scatter(grads, 'fsdp', scatter_dimension=0, tiled=False)]
    all_gather x10 -> x4, waiting for transfers between devices: 201 us -> 0.06 us  [per_device(): stacked = [lax.all_gather(shard, 'fsdp', axis=0) for shard in shard_list]]
    reduce_scatter x1, waiting for transfers between devices: 64.9 us -> 0.02 us  [per_device(): lax.psum_scatter(combined, ('ctx', 'tp'), scatter_dimension=0, tiled=True)]
    psum x1, waiting for transfers between devices: 1.65 us -> 47.4 us  [per_device(): lax.psum(jnp.concatenate([router_grad.T, gain_two_grad], axis=0), everywh...]
    ppermute x0 -> x9, waiting for transfers between devices: none -> 36.4 us  [swap(): return lax.ppermute(x, 'ctx', [(0, 1), (1, 0)])]
    reduce_scatter x2 -> x0, waiting for transfers between devices: 36.3 us -> none  [the longest x1 19.9 us: per_device(): lax.psum_scatter(tiny, 'fsdp', scatter_dimension=0, tiled=True)]
    psum x1, blocking collectives: 23.6 us -> 46.4 us  [per_device(): gain_one_grad = lax.psum(gain_one_grad, everywhere)[0]]
    all_gather x5 -> x0, local copies, waits for them, and re-layouts: 16 us -> none  [the longest x1 8.66 us: per_device(): grad_all = lax.all_gather(out_grad, 'ctx', axis=0, tiled=True)]
  transfers between devices with their start and end apart: 21 -> 22, of which waited for: 18 -> 6; matrix products, arithmetic and copies ran while one was open for 10% -> 25% of each run, Pallas kernels for 22% -> 51%
where the time goes in v2:
time: 877 us; the launch traced here: 867 us
  Pallas kernels  443 us (51%)
  local copies, waits for them, and re-layouts  141 us (16%)
  waiting for transfers between devices  119 us (14%)
  other arithmetic  68.2 us (8%)
  blocking collectives  46.4 us (5%)
  matrix products  22.5 us (3%)
  between operations  14.9 us (2%)
  starting transfers between devices  11.5 us (1%)
    pallas_call x4, Pallas kernels, moe_main(): pl.pallas_call(moe_body, grid=(count // PAIR,), in_specs=[one(x.shape), o...  143 us
    pallas_call x1, Pallas kernels, mid(): pl.pallas_call(functools.partial(mid_body, share=heads // kv, length=leng...  99 us
    pallas_call x1, Pallas kernels, turn(): pl.pallas_call(functools.partial(turn_body, count=count, kinds=kinds, fir...  76.4 us
    pallas_call x1, Pallas kernels, flash_bwd(): pl.pallas_call(functools.partial(flash_bwd_body, share=heads // kv, lengt...  55.7 us
    pallas_call x1, Pallas kernels, tail(): pl.pallas_call(tail_body, in_specs=[WHOLE] * 5, out_specs=[WHOLE] * 2, ou...  49.5 us
    psum x1, waiting for transfers between devices, per_device(): lax.psum(jnp.concatenate([router_grad.T, gain_two_grad], axis=0), everywh...  47.4 us
    psum x1, blocking collectives, per_device(): gain_one_grad = lax.psum(gain_one_grad, everywhere)[0]  46.4 us
    ppermute x9, waiting for transfers between devices, swap(): return lax.ppermute(x, 'ctx', [(0, 1), (1, 0)])  36.4 us
  transfers between devices with their start and end apart: 22, of which 6 were waited for; matrix products, arithmetic and copies ran while one was open for 25% of the time, Pallas kernels for 51%

profile of v2, /device:TPU:0, one launch (start us, length us, event | category | flops | bytes accessed | tf_op | source)
XLA Modules:
  0.0 866.6 jit_solution(13327607074299809216)
XLA Ops:
  14.5 2.5 dynamic-slice_bitcast_fusion
  19.9 2.2 pad_maximum_fusion.13
  22.0 34.6 %all-gather.11.cloned.1.call-done = bf16[1024,896]{1,0:T(8,128)(2,1)} async-done(((bf16[256,896]{1,0:T(8,128)(2,1)}), bf16[1024,896]{1,0:T(8,128)(2,1)}) %all-gather.11.cloned.1.call-update) | async-done | bytes 1835024 | tf_op jit(solution)/shard_map/all_gather | solution.py:703
  64.4 4.3 fusion.13
  69.6 2.0 fusion.11
  72.0 2.9 copy.225
  74.9 3.0 copy.226
  78.3 5.1 add_convert_fusion.1
  83.5 3.4 fusion.7
  92.2 14.1 %collective-permute-done = bf16[1536,256]{0,1:T(8,128)(2,1)S(1)} collective-permute-done((bf16[1536,256]{0,1:T(8,128)(2,1)S(1)}, bf16[1536,256]{0,1:T(8,128)(2,1)S(1)}, u32[]{:S(2)}, u32[]{:S(2)}) %collective-permute-start) | collective-permute-done | bytes 786464 | tf_op jit(solution)/shard_map/ppermute | solution.py:662
  107.8 3.1 copy.180
  112.7 4.6 copy.185
  118.0 99.0 %mid.1 = (bf16[1536,256]{1,0:T(8,128)(2,1)}, f32[384,1024]{1,0:T(8,128)}, bf16[8,384,1024]{2,1,0:T(8,128)(2,1)}) custom-call(bf16[384,1024]{1,0:T(8,128)(2,1)} %constant_dynamic-slice_fusion.13.tok_ref, bf16[4,1536,64]{2,1,0:T(8,128)(2,1)} %get-tuple-element.173.q_ref, bf16[2,3072,64]{2,1,0:T(8,128)(2,1)} %get-tuple-element.175.k_ref, ...), custom_call_target="tpu_custom_call" | custom-call | flops 99999997952 | bytes 1048576 | tf_op jit(solution)/shard_map/mid/pallas_call | solution.py:429
  217.0 8.7 %copy.220 = bf16[3072,1024]{0,1:T(8,128)(2,1)} copy(bf16[3072,1024]{1,0:T(8,128)(2,1)} %bitcast.135) | data formatting | bytes 12582912 | tf_op jit(solution)/shard_map/reshape | solution.py:746
  225.7 4.7 fusion.23
  233.0 4.4 constant_dynamic-slice_fusion.3
  237.4 3.3 broadcast_select_fusion.1
  240.6 5.2 fusion.17
  245.8 8.7 %copy.190.g_ref = bf16[3072,1024]{1,0:T(8,128)(2,1)} copy(bf16[3072,1024]{0,1:T(8,128)(2,1)} %get-tuple-element.169) | data formatting | bytes 12582912 | tf_op jit(solution)/shard_map/concatenate | solution.py:696
  254.5 36.1 %moe_main.4 = (bf16[3072,512]{1,0:T(8,128)(2,1)}, bf16[3072,1024]{1,0:T(8,128)(2,1)}, bf16[4,3,4,256,128]{4,3,2,1,0:T(8,128)(2,1)}, f32[2,3072,2]{2,1,0:T(8,128)}) custom-call(bf16[3072,1024]{1,0:T(8,128)(2,1)} %bitcast.137, bf16[3072,1024]{1,0:T(8,128)(2,1)} %copy.190.g_ref, bf16[1024,3072]{1,0:T(8,128)(2,1)} %bitcast.145, ...), custom_call_target="tpu_custom_call" | custom-call | flops 19327352832 | bytes 31457280 | tf_op jit(solution)/shard_map/moe_main/pallas_call | solution.py:185
  290.9 35.7 %moe_main.6 = (bf16[3072,512]{1,0:T(8,128)(2,1)}, bf16[3072,1024]{1,0:T(8,128)(2,1)}, bf16[4,3,4,256,128]{4,3,2,1,0:T(8,128)(2,1)}, f32[2,3072,2]{2,1,0:T(8,128)}) custom-call(bf16[3072,1024]{1,0:T(8,128)(2,1)} %bitcast.138, bf16[3072,1024]{1,0:T(8,128)(2,1)} %copy.190.g_ref, bf16[1024,3072]{1,0:T(8,128)(2,1)} %bitcast.146, ...), custom_call_target="tpu_custom_call" | custom-call | flops 19327352832 | bytes 31457280 | tf_op jit(solution)/shard_map/moe_main/pallas_call | solution.py:185
  326.7 35.8 %moe_main.5 = (bf16[3072,512]{1,0:T(8,128)(2,1)}, bf16[3072,1024]{1,0:T(8,128)(2,1)}, bf16[4,3,4,256,128]{4,3,2,1,0:T(8,128)(2,1)}, f32[2,3072,2]{2,1,0:T(8,128)}) custom-call(bf16[3072,1024]{1,0:T(8,128)(2,1)} %bitcast.139, bf16[3072,1024]{1,0:T(8,128)(2,1)} %copy.190.g_ref, bf16[1024,3072]{1,0:T(8,128)(2,1)} %bitcast.147, ...), custom_call_target="tpu_custom_call" | custom-call | flops 19327352832 | bytes 31457280 | tf_op jit(solution)/shard_map/moe_main/pallas_call | solution.py:185
  362.8 35.7 %moe_main.7 = (bf16[3072,512]{1,0:T(8,128)(2,1)}, bf16[3072,1024]{1,0:T(8,128)(2,1)}, bf16[4,3,4,256,128]{4,3,2,1,0:T(8,128)(2,1)}, f32[2,3072,2]{2,1,0:T(8,128)}) custom-call(bf16[3072,1024]{1,0:T(8,128)(2,1)} %bitcast.140, bf16[3072,1024]{1,0:T(8,128)(2,1)} %copy.190.g_ref, bf16[1024,3072]{1,0:T(8,128)(2,1)} %bitcast.148, ...), custom_call_target="tpu_custom_call" | custom-call | flops 19327352832 | bytes 31457280 | tf_op jit(solution)/shard_map/moe_main/pallas_call | solution.py:185
  403.7 2.1 constant_dynamic-slice_fusion.8.refs_11_
  407.5 2.3 slice.165.w_ref
  409.8 2.4 copy.200
  412.2 2.4 copy.199
  414.5 2.4 copy.198
  416.9 2.4 copy.197
  421.3 3.0 fusion.18
  424.5 11.5 %dynamic_update_slice.3 = f32[3072,32]{1,0:T(8,128)S(1)} dynamic-update-slice(f32[3072,32]{1,0:T(8,128)S(1)} %broadcast_in_dim.62, f32[3072,16]{1,0:T(8,128)} %get-tuple-element.163, s32[]{:T(128)} %constant.16.clone.1, s32[]{:T(128)S(6)} %select_n.108) | dynamic-update-slice | bytes 393220 | tf_op jit(solution)/shard_map/dynamic_update_slice | solution.py:771
  436.0 2.1 subtract_convert_fusion.2.refs_8_
  438.1 5.0 fusion.24
  443.1 18.9 %moe_out.1 = bf16[3072,1024]{1,0:T(8,128)(2,1)} custom-call(bf16[3072,512]{1,0:T(8,128)(2,1)} %get-tuple-element.100.refs_0_, bf16[3072,512]{1,0:T(8,128)(2,1)} %get-tuple-element.101.refs_1_, bf16[3072,512]{1,0:T(8,128)(2,1)} %get-tuple-element.102.refs_2_, bf16[3072,512]{1,0:T(8,128)(2,1)} %get-tuple-element.103.refs_3_, ...), custom_call_target="tpu_custom_call" | custom-call | flops 12884901888 | bytes 12582912 | tf_op jit(solution)/shard_map/moe_out/pallas_call | solution.py:234
  462.5 76.4 %turn.1 = (bf16[4,384,1024]{2,1,0:T(8,128)(2,1)}, f32[384,1024]{1,0:T(8,128)}, f32[1,1024]{1,0:T(1,128)}) custom-call(bf16[3072,1024]{1,0:T(8,128)(2,1)} %get-tuple-element.68.refs_0_, bf16[3072,1024]{1,0:T(8,128)(2,1)} %get-tuple-element.70.refs_1_, bf16[3072,1024]{1,0:T(8,128)(2,1)} %get-tuple-element.72.refs_2_, ...), custom_call_target="tpu_custom_call" | custom-call | flops 74999996416 | bytes 1048576 | tf_op jit(solution)/shard_map/turn/pallas_call | solution.py:611
  539.0 3.2 convolution_convert_fusion
  546.4 55.7 %flash_bwd.1 = (f32[4,1536,64]{2,1,0:T(8,128)}, f32[2,3072,64]{2,1,0:T(8,128)}, f32[2,3072,64]{2,1,0:T(8,128)}) custom-call(s32[1]{0:T(128)} %bitcast.34.base_ref, bf16[4,1536,64]{2,1,0:T(8,128)(2,1)} %get-tuple-element.173.q_ref, bf16[4,1536,64]{2,1,0:T(8,128)(2,1)} %bitcast.155, bf16[2,3072,64]{2,1,0:T(8,128)(2,1)} %get-tuple-element.175.k_ref, ...), custom_call_target="tpu_custom_call" | custom-call | flops 54999998464 | bytes 1048576 | tf_op jit(solution)/shard_map/flash_bwd/pallas_call | solution.py:97
  602.1 2.5 collective-permute-done.5
  604.6 2.4 convert.40
  607.9 2.4 copy.207
  613.6 3.7 convolution_convert_fusion.2
  619.6 2.6 multiply_bitcast_fusion
  622.2 2.0 copy.206
  624.2 15.4 %collective-permute-done.6 = bf16[1536,256]{1,0:T(8,128)(2,1)} collective-permute-done((bf16[1536,256]{1,0:T(8,128)(2,1)}, bf16[1536,256]{1,0:T(8,128)(2,1)}, u32[]{:S(2)}, u32[]{:S(2)}) %collective-permute-start.6) | collective-permute-done | bytes 786464 | tf_op jit(solution)/shard_map/ppermute | solution.py:662
  644.7 2.9 copy.229
  647.6 2.9 copy.230
  650.5 5.1 subtract_convert_fusion
  658.7 4.0 convolution_convert_fusion.1
  665.4 49.5 %tail.1 = (bf16[4,384,1024]{2,1,0:T(8,128)(2,1)}, f32[1,1024]{1,0:T(1,128)}) custom-call(bf16[384,1024]{1,0:T(8,128)(2,1)} %constant_dynamic-slice_fusion.13.tok_ref, f32[384,1024]{1,0:T(8,128)} %get-tuple-element.81.hg_ref, bf16[1536,512]{1,0:T(8,128)(2,1)} %pad_maximum_fusion.5.lin_ref, bf16[1024,512]{1,0:T(8,128)(2,1)} %slice.165.w_ref, f32[1,1024]{1,0:T(1,128)} %bitcast.171), custom_call_target="tpu_custom_call" | custom-call | flops 49999998976 | bytes 1048576 | tf_op jit(solution)/shard_map/tail/pallas_call | solution.py:472
  714.9 2.4 add_convert_fusion.2
  717.4 1.9 slice_bitcast_fusion.1
  722.0 47.4 %all-reduce.2.cloned.1.call-done = f32[33,1024]{1,0:T(8,128)} async-done(((f32[33,1024]{1,0:T(8,128)}), f32[33,1024]{1,0:T(8,128)}) %all-reduce.2.cloned.1.call-update) | async-done | bytes 135184 | tf_op jit(solution)/shard_map/psum | solution.py:817
  773.7 2.0 slice_bitcast_fusion.15
  775.7 1.9 slice_bitcast_fusion.14
  777.7 1.9 slice_bitcast_fusion.13
  779.6 46.4 %psum.14 = f32[1,1024]{1,0:T(1,128)S(1)} all-reduce(f32[1,1024]{1,0:T(1,128)S(1)} %copy-done.45), channel_id=1, replica_groups=mesh['fsdp'=4,'ctx'=2,'tp'=4] {'fsdp','ctx','tp'}, use_global_device_ids=true, to_apply=%region_10.11 | all-reduce | flops 1024 | bytes 8192 | tf_op jit(solution)/shard_map/psum | solution.py:818
  826.6 1.9 slice_bitcast_fusion
  828.8 2.3 convert_bitcast_fusion
  831.1 5.6 copy.218
  839.7 2.2 collective-permute-start.7
  842.0 2.3 maximum_convert_fusion.1
  844.3 2.3 maximum_convert_fusion
  846.6 4.4 collective-permute-done.7
  854.2 4.0 copy.236
  (229 shorter events, 78.7 us)
Async XLA Ops:
  7.2 49.5 %all-gather.11.cloned.1.call-start = ((), (), s32[]{:S(2)}) async-start(), calls=%async_computation.6 | async-start | bytes 2293760 | tf_op jit(solution)/shard_map/all_gather | solution.py:703
  12.4 242.1 %all-gather.15.cloned.1.call-start = ((), (), s32[]{:S(2)}) async-start(), calls=%async_computation.15 | async-start | bytes 3932160 | tf_op jit(solution)/shard_map/all_gather | solution.py:718
  17.9 41.1 %copy-start.36 = (s32[3072]{0:T(1024)S(1)}, s32[3072]{0:T(1024)}, u32[]{:S(2)}) copy-start(s32[3072]{0:T(1024)} %param.17) | copy-start | bytes 36868
  18.9 41.9 %copy-start.38 = (s32[3072]{0:T(1024)S(1)}, s32[3072]{0:T(1024)}, u32[]{:S(2)}) copy-start(s32[3072]{0:T(1024)} %param.18) | copy-start | bytes 36868
  19.9 42.9 %copy-start.3 = (bf16[1536,1024]{1,0:T(8,128)(2,1)S(1)}, bf16[1536,1024]{1,0:T(8,128)(2,1)}, u32[]{:S(2)}) copy-start(bf16[1536,1024]{1,0:T(8,128)(2,1)} %param.15) | copy-start | bytes 9437188
  56.7 234.2 %all-gather.19.cloned.1.call-start = ((), (), s32[]{:S(2)}) async-start(), calls=%async_computation.17 | async-start | bytes 3932160 | tf_op jit(solution)/shard_map/all_gather | solution.py:718
  57.4 269.3 %all-gather.17.cloned.1.call-start = ((), (), s32[]{:S(2)}) async-start(), calls=%async_computation.16 | async-start | bytes 3932160 | tf_op jit(solution)/shard_map/all_gather | solution.py:718
  57.4 30.7 %collective-permute-start.2 = (s32[1536,8]{0,1:T(8,128)}, s32[1536,8]{0,1:T(8,128)}, u32[]{:S(2)}, u32[]{:S(2)}) collective-permute-start(s32[1536,8]{0,1:T(8,128)} %param.19), channel_id=1, source_target_pairs={{0,4},{4,0},{1,5},{5,1},{2,6},{6,2},{3,7},{7,3},{8,12},{12,8},{9,1... | collective-permute-start | bytes 147464 | tf_op jit(solution)/shard_map/ppermute | solution.py:662
  62.7 300.1 %all-gather.21.cloned.1.call-start = ((), (), s32[]{:S(2)}) async-start(), calls=%async_computation.18 | async-start | bytes 3932160 | tf_op jit(solution)/shard_map/all_gather | solution.py:718
  63.7 5.0 copy-start.6
  63.7 5.9 copy-start.4
  64.4 7.2 copy-start.40
  68.7 9.6 %copy-start = (f32[1536,32]{1,0:T(8,128)}, f32[1536,32]{1,0:T(8,128)S(1)}, u32[]{:S(2)}) copy-start(f32[1536,32]{1,0:T(8,128)S(1)} %get-tuple-element.238) | copy-start | bytes 589828
  69.6 2.0 copy-start.42
  74.9 3.4 copy-start.11
  87.5 18.8 %collective-permute-start = (bf16[1536,256]{0,1:T(8,128)(2,1)S(1)}, bf16[1536,256]{0,1:T(8,128)(2,1)S(1)}, u32[]{:S(2)}, u32[]{:S(2)}) collective-permute-start(bf16[1536,256]{0,1:T(8,128)(2,1)S(1)} %bitcast.154), channel_id=1, source_target_pairs={{0,4},{4,0},{1,5},{5,1},{2,6},{6,2},{3,7},{7,3},{8,12},{12,8},{9,1... | collective-permute-start | bytes 2359304 | tf_op jit(solution)/shard_map/ppermute | solution.py:662
  91.9 370.6 %reduce-scatter.7.cloned.1.call-start = ((), (), s32[]{:S(2)}) async-start(), calls=%async_computation.7 | async-start | bytes 3932160 | tf_op jit(solution)/shard_map/reduce_scatter | solution.py:765
  117.4 120.0 %collective-permute-start.1 = (bf16[1536,1024]{0,1:T(8,128)(2,1)}, bf16[1536,1024]{0,1:T(8,128)(2,1)}, u32[]{:S(2)}, u32[]{:S(2)}) collective-permute-start(bf16[1536,1024]{0,1:T(8,128)(2,1)} %copy.185), channel_id=1, source_target_pairs={{0,4},{4,0},{1,5},{5,1},{2,6},{6,2},{3,7},{7,3},{8,12},{12,8},{9,1... | collective-permute-start | bytes 9437192 | tf_op jit(solution)/shard_map/ppermute | solution.py:662
  231.3 6.1 copy-start.30
  290.6 248.3 %reduce-scatter.11.cloned.1.call-start = ((), (), s32[]{:S(2)}) async-start(), calls=%async_computation.9 | async-start | bytes 3932160 | tf_op jit(solution)/shard_map/reduce_scatter | solution.py:765
  326.6 212.3 %reduce-scatter.9.cloned.1.call-start = ((), (), s32[]{:S(2)}) async-start(), calls=%async_computation.8 | async-start | bytes 3932160 | tf_op jit(solution)/shard_map/reduce_scatter | solution.py:765
  362.5 278.7 %reduce-scatter.13.cloned.1.call-start = ((), (), s32[]{:S(2)}) async-start(), calls=%async_computation.10 | async-start | bytes 3932160 | tf_op jit(solution)/shard_map/reduce_scatter | solution.py:765
  398.5 1.9 copy-start.37
  398.5 3.6 copy-start.39
  398.5 316.4 %reduce-scatter.15.cloned.1.call-start = ((), (), s32[]{:S(2)}) async-start(), calls=%async_computation.11 | async-start | bytes 7077888 | tf_op jit(solution)/shard_map/reduce_scatter | solution.py:810
  424.4 11.6 %copy-start.31 = (f32[3072]{0:T(1024)S(1)}, f32[3072]{0:T(1024)}, u32[]{:S(2)}) copy-start(f32[3072]{0:T(1024)} %copy-done.30) | copy-start | bytes 36868
  438.1 5.0 copy-start.9
  462.0 307.4 %all-reduce.2.cloned.1.call-start = ((), (), s32[]{:S(2)}) async-start(), calls=%async_computation.14 | async-start | bytes 327680 | tf_op jit(solution)/shard_map/psum | solution.py:817
  539.0 4.9 copy-start.21
  539.0 5.4 copy-start.24
  539.0 6.9 copy-start.23
  543.9 58.2 %collective-permute-start.3 = (bf16[3,4,256,128]{3,2,1,0:T(8,128)(2,1)S(1)}, bf16[3,4,256,128]{3,2,1,0:T(8,128)(2,1)}, u32[]{:S(2)}, u32[]{:S(2)}) collective-permute-start(bf16[3,4,256,128]{3,2,1,0:T(8,128)(2,1)S(1)} %bitcast.161), channel_id=1, source_target_pairs={{0,4},{4,0},{1,5},{5,1},{2,6},{6,2},{3,7},{7,3},{8,12},{12,8},{9,1... | collective-permute-start | bytes 2359304 | tf_op jit(solution)/shard_map/ppermute | solution.py:662
  544.3 57.7 %collective-permute-start.4 = (bf16[3,4,256,128]{3,2,1,0:T(8,128)(2,1)S(1)}, bf16[3,4,256,128]{3,2,1,0:T(8,128)(2,1)}, u32[]{:S(2)}, u32[]{:S(2)}) collective-permute-start(bf16[3,4,256,128]{3,2,1,0:T(8,128)(2,1)S(1)} %bitcast.164), channel_id=1, source_target_pairs={{0,4},{4,0},{1,5},{5,1},{2,6},{6,2},{3,7},{7,3},{8,12},{12,8},{9,1... | collective-permute-start | bytes 2359304 | tf_op jit(solution)/shard_map/ppermute | solution.py:662
  545.9 58.7 %collective-permute-start.5 = (bf16[3,4,256,128]{3,2,1,0:T(8,128)(2,1)S(1)}, bf16[3,4,256,128]{3,2,1,0:T(8,128)(2,1)S(1)}, u32[]{:S(2)}, u32[]{:S(2)}) collective-permute-start(bf16[3,4,256,128]{3,2,1,0:T(8,128)(2,1)S(1)} %bitcast.163), channel_id=1, source_target_pairs={{0,4},{4,0},{1,5},{5,1},{2,6},{6,2},{3,7},{7,3},{8,12},{12,8},{9,1... | collective-permute-start | bytes 2359304 | tf_op jit(solution)/shard_map/ppermute | solution.py:662
  602.1 5.0 copy-start.8
  604.6 2.4 copy-start.26
  610.3 3.3 copy-start.46
  613.0 4.3 copy-start.27
  613.0 4.3 copy-start.44
  613.0 26.7 %collective-permute-start.6 = (bf16[1536,256]{1,0:T(8,128)(2,1)}, bf16[1536,256]{1,0:T(8,128)(2,1)}, u32[]{:S(2)}, u32[]{:S(2)}) collective-permute-start(bf16[1536,256]{1,0:T(8,128)(2,1)} %copy.228), channel_id=1, source_target_pairs={{0,4},{4,0},{1,5},{5,1},{2,6},{6,2},{3,7},{7,3},{8,12},{12,8},{9,1... | collective-permute-start | bytes 2359304 | tf_op jit(solution)/shard_map/ppermute | solution.py:662
  618.0 221.8 %reduce-scatter.17.cloned.1.call-start = ((), (), s32[]{:S(2)}) async-start(), calls=%async_computation.13 | async-start | bytes 1966080 | tf_op jit(solution)/shard_map/reduce_scatter | solution.py:814
  624.2 20.1 %copy-start.2 = (f32[1536,4,64]{0,2,1:T(8,128)S(1)}, f32[1536,4,64]{0,2,1:T(8,128)}, u32[]{:S(2)}) copy-start(f32[1536,4,64]{0,2,1:T(8,128)} %copy.206) | copy-start | bytes 4718596
  647.6 2.9 copy-start.1
  647.6 2.9 copy-start.10
  656.9 1.8 copy-start.41
  656.9 1.8 copy-start.43
  658.7 4.0 copy-start.13
  665.3 188.8 %all-gather.13.cloned.1.call-start = ((), (), s32[]{:S(2)}) async-start(), calls=%async_computation.12 | async-start | bytes 3932160 | tf_op jit(solution)/shard_map/all_gather | solution.py:811
  665.4 49.5 %copy-start.12 = (f32[384,1024]{1,0:T(8,128)S(1)}, f32[384,1024]{1,0:T(8,128)}, u32[]{:S(2)}) copy-start(f32[384,1024]{1,0:T(8,128)} %get-tuple-element.99.refs_10_) | copy-start | bytes 4718596
  714.9 2.5 copy-start.22
  717.3 3.9 copy-start.25
  721.2 58.4 %copy-start.45 = (f32[1,1024]{1,0:T(1,128)S(1)}, f32[1,1024]{1,0:T(1,128)}, u32[]{:S(2)}) copy-start(f32[1,1024]{1,0:T(1,128)} %get-tuple-element.105) | copy-start | bytes 12292
  772.3 54.4 %collective-permute-start.8 = (bf16[3,4,256,128]{3,2,1,0:T(8,128)(2,1)}, bf16[3,4,256,128]{3,2,1,0:T(8,128)(2,1)}, u32[]{:S(2)}, u32[]{:S(2)}) collective-permute-start(bf16[3,4,256,128]{3,2,1,0:T(8,128)(2,1)} %bitcast.46), channel_id=1, source_target_pairs={{0,4},{4,0},{1,5},{5,1},{2,6},{6,2},{3,7},{7,3},{8,12},{12,8},{9,1... | collective-permute-start | bytes 2359304 | tf_op jit(solution)/shard_map/ppermute | solution.py:662
  836.7 1.7 copy-start.14
  836.7 1.7 copy-start.15
  836.7 1.7 copy-start.16
  836.7 1.7 copy-start.17
  836.7 1.7 copy-start.18
  836.7 1.7 copy-start.19
  836.8 1.7 copy-start.20
  839.7 11.2 %collective-permute-start.7 = (bf16[256,768]{0,1:T(8,128)(2,1)}, bf16[256,768]{0,1:T(8,128)(2,1)S(1)}, u32[]{:S(2)}, u32[]{:S(2)}) collective-permute-start(bf16[256,768]{0,1:T(8,128)(2,1)} %reduce-scatter.17.cloned.1.call-done), channel_id=1, source_target_pairs={{0,4},{4,0},{1,5},{5,1},{2,6},{6,2},{3,7},{7,3},{8,12},{12,8},{9,1... | collective-permute-start | bytes 1179656 | tf_op jit(solution)/shard_map/ppermute | solution.py:662
  842.0 2.3 copy-start.5
  844.3 6.7 copy-start.29
  854.2 4.0 copy-start.7
  (5 other events, 4.5 us)
Sparse Core Ops, SparseCore 0:
  12.5 44.0 all-gather.10
  58.2 62.2 all-gather.14
  122.1 62.0 all-gather.18
  185.6 62.0 all-gather.16
  249.1 62.0 all-gather.20
  314.0 59.0 reduce-scatter.6
  375.4 60.3 reduce-scatter.10
  438.6 60.3 reduce-scatter.8
  501.3 60.2 reduce-scatter.12
  564.9 74.8 reduce-scatter.14
  645.9 123.4 all-reduce.1
  772.1 37.9 reduce-scatter.16
  811.7 28.1 all-gather.12

commit v3 on v2

--- a/solution.py
+++ b/solution.py
@@ -161,8 +161,11 @@
         inner = silu * up_val
         a_ref[here, :] = (inner * gate).astype(jnp.bfloat16)
         prod = inner * back
+        dots = jnp.where(step == 0, 0.0, dots_ref[here, :])
         for e in range(pair):
-            dots_ref[0, here, e : e + 1] = jnp.sum(prod[:, e * ff : (e + 1) * ff], axis=1, keepdims=True)
+            total = jnp.sum(prod[:, e * ff : (e + 1) * ff], axis=1, keepdims=True)
+            dots = jnp.where(lanes == step * pair + e, total, dots)
+        dots_ref[here, :] = dots
         back = back * gate
         gu_ref[here, : pair * ff] = (back * up_val * sig * (1.0 + gate_val * (1.0 - sig))).astype(jnp.bfloat16)
         gu_ref[here, pair * ff :] = (back * silu).astype(jnp.bfloat16)
@@ -193,13 +196,13 @@
             pl.BlockSpec((rows, PAIR * ff), lambda i: (0, i)),
             pl.BlockSpec((rows, 2 * PAIR * ff), lambda i: (0, i)),
             pl.BlockSpec((shards, 3, PAIR, part, ff), lambda i: (0, 0, i, 0, 0)),
-            pl.BlockSpec((1, rows, PAIR), lambda i: (i, 0, 0)),
+            pl.BlockSpec((rows, count), lambda i: (0, 0)),
         ],
         out_shape=[
             jax.ShapeDtypeStruct((rows, count * ff), jnp.bfloat16),
             jax.ShapeDtypeStruct((rows, 2 * count * ff), jnp.bfloat16),
             jax.ShapeDtypeStruct(w.shape, jnp.bfloat16),
-            jax.ShapeDtypeStruct((count // PAIR, rows, PAIR), jnp.float32),
+            jax.ShapeDtypeStruct((rows, count), jnp.float32),
         ],
         compiler_params=pltpu.CompilerParams(vmem_limit_bytes=VL),
         cost_estimate=pl.CostEstimate(flops=2 * rows * width * count * ff * 6, bytes_accessed=8 * rows * width + 12 * count * ff * width, transcendentals=0),
@@ -448,10 +451,14 @@
     )(tok, q, k, v, docq, blkq, dock, blkk, out_w, gain)
 
 
-def tail_body(tok_ref, hg_ref, lin_ref, w_ref, gain_ref, all_ref, gg_ref, send, pair_in, far_in, own, sems):
+def tail_body(tok_ref, hg_ref, lin_ref, w_ref, gain_ref, small_ref, all_ref, sum_ref,
+              send, pair_in, far_in, own, mine, theirs, split, split_in, sems, small_sems, *, shards):
     place = Place()
-    place.meet((place.pair, place.far))
+    z = lax.axis_index("fsdp")
+    others = [{"fsdp": lax.rem(z + d, shards)} for d in range(1, shards)]
+    place.meet((place.pair, place.far, place.side, *others))
     block = lin_ref.shape[0] // 4
+    part = sum_ref.shape[1]
 
     def produce(j):
         here = pl.ds(pl.multiple_of(j * block, block), block)
@@ -460,34 +467,79 @@
     reduce_four(place, produce, send, pair_in, far_in, own, sems, 0)
     one_grad = own[...]
     r, xhat = normalize(tok_ref[...].astype(jnp.float32))
-    gg_ref[...] = jnp.sum(one_grad * xhat, axis=0, keepdims=True)
     n = one_grad * gain_ref[...]
     grad = hg_ref[...] + r * (n - xhat * jnp.mean(n * xhat, axis=1, keepdims=True))
     all_ref[place.tp] = grad.astype(jnp.bfloat16)
-    gather_four(place, all_ref, sems, 3)
-
-
-def tail(tok, hidden_grad, lin_grad, qkv_w, gain):
+    row = lax.broadcasted_iota(jnp.int32, small_ref.shape, 0)
+    mine[0] = jnp.where(
+        row == small_ref.shape[0] - 1, jnp.sum(one_grad * xhat, axis=0, keepdims=True), small_ref[...]
+    )
+    hops = [
+        push(mine.at[i], theirs.at[i], small_sems, i, device)
+        for i, device in enumerate((place.pair, place.side, place.far))
+    ]
+    hops[0].start()
+    here, far = all_ref.at[place.tp], all_ref.at[place.far_tp]
+    to_far = push(here, here, sems, 3, place.far)
+    to_pair = push(here, here, sems, 4, place.pair)
+    to_far.start()
+    to_pair.start()
+    for i in range(2):
+        hops[i].wait_recv()
+        mine[i + 1] = mine[i] + theirs[i]
+        hops[i + 1].start()
+    to_far.wait_recv()
+    on = push(far, far, sems, 5, place.pair)
+    on.start()
+    hops[2].wait_recv()
+    total = mine[2] + theirs[2]
+    for j in range(shards):
+        split[j] = total[:, j * part : (j + 1) * part]
+    spread = [
+        push(split.at[lax.rem(z + d, shards)], split_in.at[d - 1], small_sems, 2 + d, others[d - 1])
+        for d in range(1, shards)
+    ]
+    for copy in spread:
+        copy.start()
+    to_pair.wait_recv()
+    on.wait_recv()
+    result = split[z]
+    for d in range(1, shards):
+        spread[d - 1].wait_recv()
+        result = result + split_in[d - 1]
+    sum_ref[...] = result
+    for copy in (to_far, to_pair, on, *hops, *spread):
+        copy.wait_send()
+
+
+def tail(tok, hidden_grad, lin_grad, qkv_w, gain, small, shards):
     own, width = tok.shape
+    count = small.shape[0]
+    part = width // shards
     return pl.pallas_call(
-        tail_body,
-        in_specs=[WHOLE] * 5,
+        functools.partial(tail_body, shards=shards),
+        in_specs=[WHOLE] * 6,
         out_specs=[WHOLE] * 2,
         out_shape=[
             jax.ShapeDtypeStruct((4, own, width), jnp.bfloat16),
-            jax.ShapeDtypeStruct((1, width), jnp.float32),
+            jax.ShapeDtypeStruct((count, part), jnp.float32),
         ],
         scratch_shapes=[
             pltpu.VMEM((4, own, width), jnp.bfloat16),
             pltpu.VMEM((2, own, width), jnp.bfloat16),
             pltpu.VMEM((own, width), jnp.bfloat16),
             pltpu.VMEM((own, width), jnp.float32),
+            pltpu.VMEM((3, count, width), jnp.float32),
+            pltpu.VMEM((3, count, width), jnp.float32),
+            pltpu.VMEM((shards, count, part), jnp.float32),
+            pltpu.VMEM((shards - 1, count, part), jnp.float32),
             pltpu.SemaphoreType.DMA((2, 6)),
+            pltpu.SemaphoreType.DMA((2, 2 + shards)),
         ],
         compiler_params=pltpu.CompilerParams(vmem_limit_bytes=VL, collective_id=1, has_side_effects=True),
         cost_estimate=busy(50),
         name="tail",
-    )(tok, hidden_grad, lin_grad, qkv_w, gain)
+    )(tok, hidden_grad, lin_grad, qkv_w, gain, small)
 
 
 def turn_body(*refs, count, kinds, first, finish):
@@ -723,12 +775,12 @@
     normed = (inputs * rms_one * gain_one).astype(bf16)
     start = ctx * rows
     cosine, sine = rope_tables(start + jnp.arange(rows, dtype=jnp.int32))
-    lin = jnp.dot(normed, qkv_w, preferred_element_type=f32)
-    turned = rotate(lin[:, : q_width + kv_width], cosine, sine).astype(bf16)
-    queries = turned[:, :heads].transpose(1, 0, 2) * bf16(HD**-0.5)
+    kv_lin = jnp.dot(normed, qkv_w[:, q_width:], preferred_element_type=f32)
     keys_values = jnp.concatenate(
-        [turned[:, heads:], lin[:, q_width + kv_width :].astype(bf16).reshape(rows, kv_heads, HD)], axis=1
-    ).reshape(rows, 2 * kv_width)
+        [rotate(kv_lin[:, :kv_width], cosine, sine).reshape(rows, kv_width), kv_lin[:, kv_width:]], axis=1
+    ).astype(bf16)
+    queries = rotate(jnp.dot(normed, qkv_w[:, :q_width], preferred_element_type=f32), cosine, sine)
+    queries = queries.astype(bf16).transpose(1, 0, 2) * bf16(HD**-0.5)
     keys_values = ordered(keys_values, swap(keys_values))
     grad_here, keys_values = after(out_grad, keys_values)
     grad_all = ordered(grad_here, swap(grad_here))
@@ -750,7 +802,7 @@
     masked = jnp.where(chosen, logits, masked_score)
     powers = jnp.exp(masked - jnp.max(masked, axis=1, keepdims=True))
     gates = powers / jnp.sum(powers, axis=1, keepdims=True)
-    gates_mine = lax.dynamic_slice_in_dim(gates, ctx * mine, mine, 1)
+    gates_mine = jnp.where(ctx == 0, gates[:, :mine], gates[:, mine:])
 
     normed_t, grad_t = normed_two.T, grad_all.T
     inner_all, outer_all, dots_all, shard_grads = [], [], [], []
@@ -765,13 +817,12 @@
         shard_grads.append(lax.psum_scatter(grads, "fsdp", scatter_dimension=0, tiled=False))
     combined = moe_back(inner_all, stacked, 2, 1)
 
-    dots = jnp.concatenate(dots_all, axis=0).transpose(1, 0, 2).reshape(ctx_size * rows, mine)
-    weighted = gates_mine * dots
+    dots = jnp.concatenate(dots_all, axis=1)
+    weighted = gates * ordered(dots, jnp.zeros_like(dots), axis=1)
     dots_sum = jnp.sum(weighted, axis=1, keepdims=True)
-    spread = lax.dynamic_update_slice_in_dim(jnp.zeros_like(gates), weighted, ctx * mine, 1)
-    logit_grad = (spread - gates * dots_sum).astype(bf16)
+    logit_grad = (weighted - gates * dots_sum).astype(bf16)
     router_grad = lax.dot_general(
-        normed_two, logit_grad, (((0,), (0,)), ((), ())), preferred_element_type=f32
+        logit_grad, normed_two, (((0,), (0,)), ((), ())), preferred_element_type=f32
     )
     grad_own, shard_grads[0] = after(grad_own, shard_grads[0])
     branch_grad, hidden_grad, gain_two_grad = turn(
@@ -804,20 +855,20 @@
     lin_grad = jnp.concatenate([turned_grad, kv_grad[:, kv_width:]], axis=1).astype(bf16)
     qkv_grad = lax.dot_general(normed, lin_grad, (((0,), (0,)), ((), ())), preferred_element_type=f32)
 
-    input_grad, gain_one_grad = tail(tokens_own, hidden_grad, lin_grad, qkv_w, gain_one[None])
+    small_grads = jnp.concatenate(
+        [router_grad, gain_two_grad, jnp.zeros((8 - (experts + 1) % 8, width), f32)], axis=0
+    )
+    input_grad, small_grads = tail(
+        tokens_own, hidden_grad, lin_grad, qkv_w, gain_one[None], small_grads, shards
+    )
     input_grad = input_grad.reshape(rows, width)
-    hidden, gain_one_grad = after(hidden, gain_one_grad)
+    hidden, small_grads = after(hidden, small_grads)
     mixed = lax.psum_scatter(combined, ("ctx", "tp"), scatter_dimension=0, tiled=True)
     block_out = lax.all_gather((hidden + mixed.astype(f32)).astype(bf16), "tp", axis=0, tiled=True)
 
     big = jnp.concatenate([qkv_grad, out_w_grad], axis=1).astype(bf16)
     big = lax.psum_scatter(big, "fsdp", scatter_dimension=0, tiled=True)
     big = big.astype(f32) + swap(big).astype(f32)
-    everywhere = ("fsdp", "ctx", "tp")
-    tiny = lax.psum(jnp.concatenate([router_grad.T, gain_two_grad], axis=0), everywhere)
-    gain_one_grad = lax.psum(gain_one_grad, everywhere)[0]
-    mine_of = lambda x: lax.dynamic_slice_in_dim(x, lax.axis_index("fsdp") * part, part, x.ndim - 1)
-
     gate_s, up_s, down_s = [
         ordered(
             jnp.concatenate([piece[kind] for piece in shard_grads]),
@@ -829,13 +880,13 @@
     return (
         block_out,
         input_grad,
-        mine_of(gain_one_grad),
+        small_grads[-1],
         big[:, :q_width],
         big[:, q_width : q_width + kv_width],
         big[:, q_width + kv_width : at],
         big[:, at : at + q_width].T,
-        mine_of(tiny[experts]),
-        mine_of(tiny[:experts]).T,
+        small_grads[experts],
+        small_grads[:experts].T,
         gate_s,
         up_s,
         down_s.transpose(0, 2, 1),

time: 877 us -> 763 us (0.87)
  blocking collectives: 46.4 us -> 0 us
  waiting for transfers between devices: 119 us -> 86.5 us
  local copies, waits for them, and re-layouts: 141 us -> 115 us
  other arithmetic: 68.2 us -> 58.8 us
    psum x1 -> x0, waiting for transfers between devices: 47.4 us -> none  [per_device(): lax.psum(jnp.concatenate([router_grad.T, gain_two_grad], axis=0), everywh...]
    psum x1 -> x0, blocking collectives: 46.4 us -> none  [per_device(): gain_one_grad = lax.psum(gain_one_grad, everywhere)[0]]
    ppermute x9, waiting for transfers between devices: 36.4 us -> 49.8 us  [swap(): return lax.ppermute(x, 'ctx', [(0, 1), (1, 0)])]
    dynamic_update_slice x1 -> x0, local copies, waits for them, and re-layouts: 11.5 us -> none  [per_device(): lax.dynamic_update_slice_in_dim(jnp.zeros_like(gates), weighted, ctx * mi...]
    unnamed x112 -> x134, local copies, waits for them, and re-layouts: 32.2 us -> 29.1 us
  transfers between devices with their start and end apart: 22 -> 21, of which waited for: 6 -> 5; matrix products, arithmetic and copies ran while one was open for 25% -> 24% of each run, Pallas kernels for 51% -> 59%
where the time goes in v3:
time: 763 us; the launch traced here: 755 us
  Pallas kernels  445 us (58%)
  local copies, waits for them, and re-layouts  115 us (15%)
  waiting for transfers between devices  86.5 us (11%)
  other arithmetic  58.8 us (8%)
  matrix products  20.2 us (3%)
  between operations  15.6 us (2%)
  starting transfers between devices  13 us (2%)
    pallas_call x4, Pallas kernels, moe_main(): pl.pallas_call(moe_body, grid=(count // PAIR,), in_specs=[one(x.shape), o...  144 us
    pallas_call x1, Pallas kernels, mid(): pl.pallas_call(functools.partial(mid_body, share=heads // kv, length=leng...  98.3 us
    pallas_call x1, Pallas kernels, turn(): pl.pallas_call(functools.partial(turn_body, count=count, kinds=kinds, fir...  74.7 us
    pallas_call x1, Pallas kernels, flash_bwd(): pl.pallas_call(functools.partial(flash_bwd_body, share=heads // kv, lengt...  55.7 us
    pallas_call x1, Pallas kernels, tail(): pl.pallas_call(functools.partial(tail_body, shards=shards), in_specs=[WHO...  54.5 us
    ppermute x9, waiting for transfers between devices, swap(): return lax.ppermute(x, 'ctx', [(0, 1), (1, 0)])  49.8 us
    all_gather x1, waiting for transfers between devices, per_device(): packed = lax.all_gather(packed, 'fsdp', axis=0, tiled=True)  35.7 us
    unnamed x134, local copies, waits for them, and re-layouts  29.1 us
  transfers between devices with their start and end apart: 21, of which 5 were waited for; matrix products, arithmetic and copies ran while one was open for 24% of the time, Pallas kernels for 59%

profile of v3, /device:TPU:0, one launch (start us, length us, event | category | flops | bytes accessed | tf_op | source)
XLA Modules:
  0.0 754.8 jit_solution(827286373877691229)
XLA Ops:
  10.8 1.8 concatenate.79
  13.5 2.5 dynamic-slice_bitcast_fusion
  18.9 2.2 pad_maximum_fusion.12
  21.1 35.7 %all-gather.11.cloned.1.call-done = bf16[1024,896]{1,0:T(8,128)(2,1)} async-done(((bf16[256,896]{1,0:T(8,128)(2,1)}), bf16[1024,896]{1,0:T(8,128)(2,1)}) %all-gather.11.cloned.1.call-update) | async-done | bytes 1835024 | tf_op jit(solution)/shard_map/all_gather | solution.py:755
  79.1 2.0 copy.275
  81.1 3.1 copy.276
  84.5 3.1 subtract_convert_fusion
  87.7 2.1 fusion.4.q_ref
  89.8 5.3 collective-permute-done
  97.9 3.1 copy.232
  100.9 2.0 fusion.21
  102.9 3.2 copy.237
  106.9 98.3 %mid.1 = (bf16[1536,256]{1,0:T(8,128)(2,1)}, f32[384,1024]{1,0:T(8,128)}, bf16[8,384,1024]{2,1,0:T(8,128)(2,1)}) custom-call(bf16[384,1024]{1,0:T(8,128)(2,1)} %constant_dynamic-slice_fusion.7.tok_ref, bf16[4,1536,64]{2,1,0:T(8,128)(2,1)} %fusion.4.q_ref, bf16[2,3072,64]{2,1,0:T(8,128)(2,1)} %get-tuple-element.183.k_ref, ...), custom_call_target="tpu_custom_call" | custom-call | flops 99999997952 | bytes 1048576 | tf_op jit(solution)/shard_map/mid/pallas_call | solution.py:432
  205.2 8.7 %copy.270 = bf16[3072,1024]{0,1:T(8,128)(2,1)} copy(bf16[3072,1024]{1,0:T(8,128)(2,1)} %bitcast.129) | data formatting | bytes 12582912 | tf_op jit(solution)/shard_map/reshape | solution.py:798
  213.9 4.7 fusion.26
  219.6 1.7 fusion.5
  221.8 4.0 fusion.22
  225.8 2.3 broadcast_select_fusion.1
  228.1 5.1 fusion.19
  233.2 8.7 %copy.242.g_ref = bf16[3072,1024]{1,0:T(8,128)(2,1)} copy(bf16[3072,1024]{0,1:T(8,128)(2,1)} %get-tuple-element.179) | data formatting | bytes 12582912 | tf_op jit(solution)/shard_map/concatenate | solution.py:748
  241.8 35.7 %moe_main.4 = (bf16[3072,512]{1,0:T(8,128)(2,1)}, bf16[3072,1024]{1,0:T(8,128)(2,1)}, bf16[4,3,4,256,128]{4,3,2,1,0:T(8,128)(2,1)}, f32[3072,4]{1,0:T(8,128)}) custom-call(bf16[3072,1024]{1,0:T(8,128)(2,1)} %bitcast.131, bf16[3072,1024]{1,0:T(8,128)(2,1)} %copy.242.g_ref, bf16[1024,3072]{1,0:T(8,128)(2,1)} %bitcast.140, ...), custom_call_target="tpu_custom_call" | custom-call | flops 19327352832 | bytes 31457280 | tf_op jit(solution)/shard_map/moe_main/pallas_call | solution.py:188
  277.8 35.8 %moe_main.6 = (bf16[3072,512]{1,0:T(8,128)(2,1)}, bf16[3072,1024]{1,0:T(8,128)(2,1)}, bf16[4,3,4,256,128]{4,3,2,1,0:T(8,128)(2,1)}, f32[3072,4]{1,0:T(8,128)}) custom-call(bf16[3072,1024]{1,0:T(8,128)(2,1)} %bitcast.132, bf16[3072,1024]{1,0:T(8,128)(2,1)} %copy.242.g_ref, bf16[1024,3072]{1,0:T(8,128)(2,1)} %bitcast.141, ...), custom_call_target="tpu_custom_call" | custom-call | flops 19327352832 | bytes 31457280 | tf_op jit(solution)/shard_map/moe_main/pallas_call | solution.py:188
  313.7 36.3 %moe_main.5 = (bf16[3072,512]{1,0:T(8,128)(2,1)}, bf16[3072,1024]{1,0:T(8,128)(2,1)}, bf16[4,3,4,256,128]{4,3,2,1,0:T(8,128)(2,1)}, f32[3072,4]{1,0:T(8,128)}) custom-call(bf16[3072,1024]{1,0:T(8,128)(2,1)} %bitcast.133, bf16[3072,1024]{1,0:T(8,128)(2,1)} %copy.242.g_ref, bf16[1024,3072]{1,0:T(8,128)(2,1)} %bitcast.142, ...), custom_call_target="tpu_custom_call" | custom-call | flops 19327352832 | bytes 31457280 | tf_op jit(solution)/shard_map/moe_main/pallas_call | solution.py:188
  350.4 35.8 %moe_main.7 = (bf16[3072,512]{1,0:T(8,128)(2,1)}, bf16[3072,1024]{1,0:T(8,128)(2,1)}, bf16[4,3,4,256,128]{4,3,2,1,0:T(8,128)(2,1)}, f32[3072,4]{1,0:T(8,128)}) custom-call(bf16[3072,1024]{1,0:T(8,128)(2,1)} %bitcast.134, bf16[3072,1024]{1,0:T(8,128)(2,1)} %copy.242.g_ref, bf16[1024,3072]{1,0:T(8,128)(2,1)} %bitcast.143, ...), custom_call_target="tpu_custom_call" | custom-call | flops 19327352832 | bytes 31457280 | tf_op jit(solution)/shard_map/moe_main/pallas_call | solution.py:188
  388.1 1.7 copy.257.dock_ref
  389.8 1.7 copy.258.blkk_ref
  392.0 2.1 constant_dynamic-slice_fusion.2.refs_11_
  395.9 1.9 copy.252
  398.2 2.0 copy.250
  400.3 1.9 copy.249
  402.3 1.6 copy.255
  403.9 3.8 fusion.20
  407.8 3.1 subtract_convert_fusion.1.refs_8_
  410.9 1.9 fusion.27
  412.8 18.3 %moe_out.1 = bf16[3072,1024]{1,0:T(8,128)(2,1)} custom-call(bf16[3072,512]{1,0:T(8,128)(2,1)} %get-tuple-element.101.refs_0_, bf16[3072,512]{1,0:T(8,128)(2,1)} %get-tuple-element.102.refs_1_, bf16[3072,512]{1,0:T(8,128)(2,1)} %get-tuple-element.103.refs_2_, bf16[3072,512]{1,0:T(8,128)(2,1)} %get-tuple-element.104.refs_3_, ...), custom_call_target="tpu_custom_call" | custom-call | flops 12884901888 | bytes 12582912 | tf_op jit(solution)/shard_map/moe_out/pallas_call | solution.py:237
  431.6 74.7 %turn.1 = (bf16[4,384,1024]{2,1,0:T(8,128)(2,1)}, f32[384,1024]{1,0:T(8,128)}, f32[1,1024]{1,0:T(1,128)}) custom-call(bf16[3072,1024]{1,0:T(8,128)(2,1)} %get-tuple-element.68.refs_0_, bf16[3072,1024]{1,0:T(8,128)(2,1)} %get-tuple-element.70.refs_1_, bf16[3072,1024]{1,0:T(8,128)(2,1)} %get-tuple-element.72.refs_2_, ...), custom_call_target="tpu_custom_call" | custom-call | flops 74999996416 | bytes 1048576 | tf_op jit(solution)/shard_map/turn/pallas_call | solution.py:663
  506.3 3.6 convolution_convert_fusion
  510.0 1.7 copy.256
  514.7 55.7 %flash_bwd.1 = (f32[4,1536,64]{2,1,0:T(8,128)}, f32[2,3072,64]{2,1,0:T(8,128)}, f32[2,3072,64]{2,1,0:T(8,128)}) custom-call(s32[1]{0:T(128)} %bitcast.33.base_ref, bf16[4,1536,64]{2,1,0:T(8,128)(2,1)} %fusion.4.q_ref, bf16[4,1536,64]{2,1,0:T(8,128)(2,1)} %bitcast.152, bf16[2,3072,64]{2,1,0:T(8,128)(2,1)} %get-tuple-element.183.k_ref, ...), custom_call_target="tpu_custom_call" | custom-call | flops 54999998464 | bytes 1048576 | tf_op jit(solution)/shard_map/flash_bwd/pallas_call | solution.py:97
  570.4 4.2 convolution_convert_fusion.2
  575.5 1.7 copy-done.11
  578.1 2.6 copy.260
  586.6 2.1 multiply_bitcast_fusion
  588.7 2.0 copy.259
  590.7 25.3 %collective-permute-done.6 = bf16[1536,256]{1,0:T(8,128)(2,1)} collective-permute-done((bf16[1536,256]{1,0:T(8,128)(2,1)}, bf16[1536,256]{1,0:T(8,128)(2,1)}, u32[]{:S(2)}, u32[]{:S(2)}) %collective-permute-start.6) | collective-permute-done | bytes 786464 | tf_op jit(solution)/shard_map/ppermute | solution.py:714
  616.0 1.6 convert_add_fusion
  622.6 2.6 copy.264
  625.3 3.4 convolution_convert_fusion.1
  631.8 54.5 %tail.1 = (bf16[4,384,1024]{2,1,0:T(8,128)(2,1)}, f32[40,256]{1,0:T(8,128)}) custom-call(bf16[384,1024]{1,0:T(8,128)(2,1)} %constant_dynamic-slice_fusion.7.tok_ref, f32[384,1024]{1,0:T(8,128)} %get-tuple-element.81.hg_ref, bf16[1536,512]{1,0:T(8,128)(2,1)} %pad_maximum_fusion.3.lin_ref, bf16[1024,512]{1,0:T(8,128)(2,1)} %slice.205.w_ref, ...), custom_call_target="tpu_custom_call" | custom-call | flops 49999998976 | bytes 1048576 | tf_op jit(solution)/shard_map/tail/pallas_call | solution.py:519
  686.4 2.3 add_convert_fusion.1
  688.9 2.0 slice_bitcast_fusion.1
  692.4 2.0 slice_bitcast_fusion.15
  694.3 2.1 collective-permute-start.8
  696.5 2.0 slice_bitcast_fusion.14
  700.5 14.0 %collective-permute-done.8 = bf16[3,4,256,128]{3,2,1,0:T(8,128)(2,1)S(1)} collective-permute-done((bf16[3,4,256,128]{3,2,1,0:T(8,128)(2,1)S(1)}, bf16[3,4,256,128]{3,2,1,0:T(8,128)(2,1)S(1)}, u32[]{:S(2)}, u32[]{:S(2)}) %collective-permute-start.8) | collective-permute-done | bytes 786464 | tf_op jit(solution)/shard_map/ppermute | solution.py:714
  715.7 2.3 convert_bitcast_fusion
  718.0 5.6 copy.268
  723.6 1.6 broadcast_select_fusion.5
  726.6 2.3 collective-permute-start.7
  728.9 2.3 maximum_convert_fusion.1
  731.2 2.3 maximum_convert_fusion
  733.4 5.2 collective-permute-done.7
  741.8 4.0 copy.282
  745.8 1.7 copy.283
  (247 shorter events, 68.5 us)
Async XLA Ops:
  7.2 5.5 copy-start.40
  7.2 49.6 %all-gather.11.cloned.1.call-start = ((), (), s32[]{:S(2)}) async-start(), calls=%async_computation.6 | async-start | bytes 2293760 | tf_op jit(solution)/shard_map/all_gather | solution.py:755
  12.6 229.3 %all-gather.15.cloned.1.call-start = ((), (), s32[]{:S(2)}) async-start(), calls=%async_computation.14 | async-start | bytes 3932160 | tf_op jit(solution)/shard_map/all_gather | solution.py:770
  18.9 40.3 %copy-start.2 = (bf16[1536,1024]{1,0:T(8,128)(2,1)S(1)}, bf16[1536,1024]{1,0:T(8,128)(2,1)}, u32[]{:S(2)}) copy-start(bf16[1536,1024]{1,0:T(8,128)(2,1)} %param.15) | copy-start | bytes 9437188
  56.8 221.0 %all-gather.19.cloned.1.call-start = ((), (), s32[]{:S(2)}) async-start(), calls=%async_computation.16 | async-start | bytes 3932160 | tf_op jit(solution)/shard_map/all_gather | solution.py:770
  57.5 256.2 %all-gather.17.cloned.1.call-start = ((), (), s32[]{:S(2)}) async-start(), calls=%async_computation.15 | async-start | bytes 3932160 | tf_op jit(solution)/shard_map/all_gather | solution.py:770
  57.6 10.9 %collective-permute-start.2 = (s32[1536,8]{0,1:T(8,128)}, s32[1536,8]{0,1:T(8,128)}, u32[]{:S(2)}, u32[]{:S(2)}) collective-permute-start(s32[1536,8]{0,1:T(8,128)} %param.19), channel_id=1, source_target_pairs={{0,4},{4,0},{1,5},{5,1},{2,6},{6,2},{3,7},{7,3},{8,12},{12,8},{9,1... | collective-permute-start | bytes 147464 | tf_op jit(solution)/shard_map/ppermute | solution.py:714
  59.1 291.2 %all-gather.21.cloned.1.call-start = ((), (), s32[]{:S(2)}) async-start(), calls=%async_computation.17 | async-start | bytes 3932160 | tf_op jit(solution)/shard_map/all_gather | solution.py:770
  59.9 5.4 copy-start.47
  62.0 4.6 copy-start.14
  62.0 4.6 copy-start.17
  65.3 5.8 copy-start.6
  65.3 6.7 copy-start.51
  65.4 4.0 copy-start.43
  67.4 2.0 copy-start.45
  72.0 4.6 copy-start.53
  76.1 19.0 %collective-permute-start = (bf16[1536,256]{0,1:T(8,128)(2,1)}, bf16[1536,256]{0,1:T(8,128)(2,1)}, u32[]{:S(2)}, u32[]{:S(2)}) collective-permute-start(bf16[1536,256]{0,1:T(8,128)(2,1)} %pad_maximum_fusion.16), channel_id=1, source_target_pairs={{0,4},{4,0},{1,5},{5,1},{2,6},{6,2},{3,7},{7,3},{8,12},{12,8},{9,1... | collective-permute-start | bytes 2359304 | tf_op jit(solution)/shard_map/ppermute | solution.py:714
  84.3 347.3 %reduce-scatter.7.cloned.1.call-start = ((), (), s32[]{:S(2)}) async-start(), calls=%async_computation.7 | async-start | bytes 3932160 | tf_op jit(solution)/shard_map/reduce_scatter | solution.py:817
  87.7 7.4 copy-start.9
  106.1 119.6 %collective-permute-start.1 = (bf16[1536,1024]{0,1:T(8,128)(2,1)S(1)}, bf16[1536,1024]{0,1:T(8,128)(2,1)}, u32[]{:S(2)}, u32[]{:S(2)}) collective-permute-start(bf16[1536,1024]{0,1:T(8,128)(2,1)S(1)} %copy.237), channel_id=1, source_target_pairs={{0,4},{4,0},{1,5},{5,1},{2,6},{6,2},{3,7},{7,3},{8,12},{12,8},{9,1... | collective-permute-start | bytes 9437192 | tf_op jit(solution)/shard_map/ppermute | solution.py:714
  205.2 8.7 %copy-start.21 = (pred[3072,32]{1,0:T(32,128)(4,1)S(1)}, pred[3072,32]{1,0:T(32,128)(4,1)}, u32[]{:S(2)}) copy-start(pred[3072,32]{1,0:T(32,128)(4,1)} %copy.239) | copy-start | bytes 294916
  218.7 2.7 copy-start
  277.6 228.7 %reduce-scatter.11.cloned.1.call-start = ((), (), s32[]{:S(2)}) async-start(), calls=%async_computation.9 | async-start | bytes 3932160 | tf_op jit(solution)/shard_map/reduce_scatter | solution.py:817
  313.6 192.7 %reduce-scatter.9.cloned.1.call-start = ((), (), s32[]{:S(2)}) async-start(), calls=%async_computation.8 | async-start | bytes 3932160 | tf_op jit(solution)/shard_map/reduce_scatter | solution.py:817
  350.1 267.6 %reduce-scatter.13.cloned.1.call-start = ((), (), s32[]{:S(2)}) async-start(), calls=%async_computation.10 | async-start | bytes 3932160 | tf_op jit(solution)/shard_map/reduce_scatter | solution.py:817
  386.2 1.9 copy-start.48
  386.2 3.6 copy-start.49
  386.3 300.2 %reduce-scatter.15.cloned.1.call-start = ((), (), s32[]{:S(2)}) async-start(), calls=%async_computation.11 | async-start | bytes 7077888 | tf_op jit(solution)/shard_map/reduce_scatter | solution.py:866
  388.1 6.0 copy-start.7
  394.1 3.7 copy-start.20
  398.2 12.6 %slice-start = ((s8[6291456]{0:T(1024)(128)(4,1)}), s8[2097152]{0:T(1024)(128)(4,1)S(1)}, s32[]{:S(2)}) async-start(s8[6291456]{0:T(1024)(128)(4,1)} %bitcast.135), calls=%async_computation.18 | async-start | bytes 4194304
  403.9 7.0 slice-start.1
  410.9 1.9 copy-start.13
  431.1 295.5 %reduce-scatter.17.cloned.1.call-start = ((), (), s32[]{:S(2)}) async-start(), calls=%async_computation.13 | async-start | bytes 1966080 | tf_op jit(solution)/shard_map/reduce_scatter | solution.py:870
  509.9 2.7 copy-start.34
  510.0 3.8 copy-start.31
  511.7 62.9 %collective-permute-start.3 = (bf16[3,4,256,128]{3,2,1,0:T(8,128)(2,1)S(1)}, bf16[3,4,256,128]{3,2,1,0:T(8,128)(2,1)}, u32[]{:S(2)}, u32[]{:S(2)}) collective-permute-start(bf16[3,4,256,128]{3,2,1,0:T(8,128)(2,1)S(1)} %bitcast.158), channel_id=1, source_target_pairs={{0,4},{4,0},{1,5},{5,1},{2,6},{6,2},{3,7},{7,3},{8,12},{12,8},{9,1... | collective-permute-start | bytes 2359304 | tf_op jit(solution)/shard_map/ppermute | solution.py:714
  512.7 62.0 %collective-permute-start.4 = (bf16[3,4,256,128]{3,2,1,0:T(8,128)(2,1)S(1)}, bf16[3,4,256,128]{3,2,1,0:T(8,128)(2,1)}, u32[]{:S(2)}, u32[]{:S(2)}) collective-permute-start(bf16[3,4,256,128]{3,2,1,0:T(8,128)(2,1)S(1)} %bitcast.162), channel_id=1, source_target_pairs={{0,4},{4,0},{1,5},{5,1},{2,6},{6,2},{3,7},{7,3},{8,12},{12,8},{9,1... | collective-permute-start | bytes 2359304 | tf_op jit(solution)/shard_map/ppermute | solution.py:714
  513.7 60.9 %collective-permute-start.5 = (bf16[3,4,256,128]{3,2,1,0:T(8,128)(2,1)S(1)}, bf16[3,4,256,128]{3,2,1,0:T(8,128)(2,1)S(1)}, u32[]{:S(2)}, u32[]{:S(2)}) collective-permute-start(bf16[3,4,256,128]{3,2,1,0:T(8,128)(2,1)S(1)} %bitcast.160), channel_id=1, source_target_pairs={{0,4},{4,0},{1,5},{5,1},{2,6},{6,2},{3,7},{7,3},{8,12},{12,8},{9,1... | collective-permute-start | bytes 2359304 | tf_op jit(solution)/shard_map/ppermute | solution.py:714
  570.4 4.2 copy-start.12
  574.6 2.6 copy-start.11
  580.7 4.0 copy-start.39
  580.7 4.0 copy-start.55
  580.7 4.0 copy-start.56
  583.4 32.6 %collective-permute-start.6 = (bf16[1536,256]{1,0:T(8,128)(2,1)}, bf16[1536,256]{1,0:T(8,128)(2,1)}, u32[]{:S(2)}, u32[]{:S(2)}) collective-permute-start(bf16[1536,256]{1,0:T(8,128)(2,1)} %copy.278), channel_id=1, source_target_pairs={{0,4},{4,0},{1,5},{5,1},{2,6},{6,2},{3,7},{7,3},{8,12},{12,8},{9,1... | collective-permute-start | bytes 2359304 | tf_op jit(solution)/shard_map/ppermute | solution.py:714
  617.7 2.4 copy-start.1
  621.5 3.8 copy-start.3
  621.5 3.8 copy-start.52
  621.5 3.7 copy-start.54
  625.3 3.4 copy-start.41
  628.7 1.8 copy-start.4
  631.8 110.0 %all-gather.13.cloned.1.call-start = ((), (), s32[]{:S(2)}) async-start(), calls=%async_computation.12 | async-start | bytes 3932160 | tf_op jit(solution)/shard_map/all_gather | solution.py:867
  631.8 54.6 %copy-start.19 = (f32[384,1024]{1,0:T(8,128)S(1)}, f32[384,1024]{1,0:T(8,128)}, u32[]{:S(2)}) copy-start(f32[384,1024]{1,0:T(8,128)} %get-tuple-element.100.refs_10_) | copy-start | bytes 4718596
  686.4 2.4 copy-start.30
  688.8 2.1 copy-start.32
  688.8 2.8 copy-start.35
  690.9 3.5 copy-start.33
  691.6 6.9 copy-start.37
  692.4 7.0 copy-start.50
  694.3 20.2 %collective-permute-start.8 = (bf16[3,4,256,128]{3,2,1,0:T(8,128)(2,1)S(1)}, bf16[3,4,256,128]{3,2,1,0:T(8,128)(2,1)S(1)}, u32[]{:S(2)}, u32[]{:S(2)}) collective-permute-start(bf16[3,4,256,128]{3,2,1,0:T(8,128)(2,1)S(1)} %bitcast.161), channel_id=1, source_target_pairs={{0,4},{4,0},{1,5},{5,1},{2,6},{6,2},{3,7},{7,3},{8,12},{12,8},{9,1... | collective-permute-start | bytes 2359304 | tf_op jit(solution)/shard_map/ppermute | solution.py:714
  726.6 12.0 %collective-permute-start.7 = (bf16[256,768]{0,1:T(8,128)(2,1)}, bf16[256,768]{0,1:T(8,128)(2,1)S(1)}, u32[]{:S(2)}, u32[]{:S(2)}) collective-permute-start(bf16[256,768]{0,1:T(8,128)(2,1)} %reduce-scatter.17.cloned.1.call-done), channel_id=1, source_target_pairs={{0,4},{4,0},{1,5},{5,1},{2,6},{6,2},{3,7},{7,3},{8,12},{12,8},{9,1... | collective-permute-start | bytes 1179656 | tf_op jit(solution)/shard_map/ppermute | solution.py:714
  728.9 2.3 copy-start.5
  731.1 7.4 copy-start.42
  741.8 4.0 copy-start.10
  (16 other events, 21.0 us)
Sparse Core Ops, SparseCore 0:
  12.7 44.0 all-gather.10
  58.3 62.3 all-gather.14
  122.3 62.0 all-gather.18
  185.8 62.0 all-gather.16
  249.3 62.0 all-gather.20
  314.2 59.0 reduce-scatter.6
  375.6 60.3 reduce-scatter.10
  438.8 60.2 reduce-scatter.8
  501.5 60.3 reduce-scatter.12
  565.0 72.1 reduce-scatter.14
  640.1 35.4 reduce-scatter.16
  688.9 29.1 all-gather.12

commit v4 on v3

--- a/solution.py
+++ b/solution.py
@@ -124,7 +124,7 @@
 PAIR = 2
 TM = 512
 
-def moe_body(x_ref, g_ref, xt_ref, gt_ref, gates_ref, w_ref, a_ref, gu_ref, grads_ref, dots_ref):
+def moe_body(base_ref, x_ref, g_ref, xt_ref, gt_ref, gates_ref, prev_ref, w_ref, a_ref, gu_ref, grads_ref, dots_ref):
     rows, width = x_ref.shape
     shards, _, pair, part, ff = w_ref.shape
     step = pl.program_id(0)
@@ -138,6 +138,7 @@
     up_w = weights(1)
     down_w = weights(2)
     experts = gates_ref.shape[1]
+    lane = base_ref[0] + step * pair
 
     def tile(i, carry):
         here = pl.ds(pl.multiple_of(i * TM, TM), TM)
@@ -150,7 +151,7 @@
         gate = jnp.concatenate(
             [
                 jnp.broadcast_to(
-                    jnp.sum(jnp.where(lanes == step * pair + e, gates, 0.0), axis=1, keepdims=True), (TM, ff)
+                    jnp.sum(jnp.where(lanes == lane + e, gates, 0.0), axis=1, keepdims=True), (TM, ff)
                 )
                 for e in range(pair)
             ],
@@ -161,10 +162,10 @@
         inner = silu * up_val
         a_ref[here, :] = (inner * gate).astype(jnp.bfloat16)
         prod = inner * back
-        dots = jnp.where(step == 0, 0.0, dots_ref[here, :])
+        dots = jnp.where(step == 0, prev_ref[here, :], dots_ref[here, :])
         for e in range(pair):
             total = jnp.sum(prod[:, e * ff : (e + 1) * ff], axis=1, keepdims=True)
-            dots = jnp.where(lanes == step * pair + e, total, dots)
+            dots = jnp.where(lanes == lane + e, total, dots)
         dots_ref[here, :] = dots
         back = back * gate
         gu_ref[here, : pair * ff] = (back * up_val * sig * (1.0 + gate_val * (1.0 - sig))).astype(jnp.bfloat16)
@@ -181,7 +182,7 @@
             grads_ref[z, 1, e] = both[:, (pair + e) * ff : (pair + e + 1) * ff].astype(jnp.bfloat16)
             grads_ref[z, 2, e] = down[:, e * ff : (e + 1) * ff].astype(jnp.bfloat16)
 
-def moe_main(x, g, xt, gt, gates, w):
+def moe_main(base, x, g, xt, gt, gates, dots, w):
     rows, width = x.shape
     shards, three, count, part, ff = w.shape
     one = lambda shape: pl.BlockSpec(shape, lambda i: (0,) * len(shape), pipeline_mode=pl.Buffered(1))
@@ -189,25 +190,26 @@
         moe_body,
         grid=(count // PAIR,),
         in_specs=[
-            one(x.shape), one(g.shape), one(xt.shape), one(gt.shape), one(gates.shape),
+            SMEMS, one(x.shape), one(g.shape), one(xt.shape), one(gt.shape), one(gates.shape), one(dots.shape),
             pl.BlockSpec((shards, 3, PAIR, part, ff), lambda i: (0, 0, i, 0, 0)),
         ],
         out_specs=[
             pl.BlockSpec((rows, PAIR * ff), lambda i: (0, i)),
             pl.BlockSpec((rows, 2 * PAIR * ff), lambda i: (0, i)),
             pl.BlockSpec((shards, 3, PAIR, part, ff), lambda i: (0, 0, i, 0, 0)),
-            pl.BlockSpec((rows, count), lambda i: (0, 0)),
+            one(dots.shape),
         ],
         out_shape=[
             jax.ShapeDtypeStruct((rows, count * ff), jnp.bfloat16),
             jax.ShapeDtypeStruct((rows, 2 * count * ff), jnp.bfloat16),
             jax.ShapeDtypeStruct(w.shape, jnp.bfloat16),
-            jax.ShapeDtypeStruct((rows, count), jnp.float32),
+            jax.ShapeDtypeStruct(dots.shape, jnp.float32),
         ],
         compiler_params=pltpu.CompilerParams(vmem_limit_bytes=VL),
         cost_estimate=pl.CostEstimate(flops=2 * rows * width * count * ff * 6, bytes_accessed=8 * rows * width + 12 * count * ff * width, transcendentals=0),
         name="moe_main",
-    )(x, g, xt, gt, gates, w)
+        input_output_aliases={6: 3},
+    )(base, x, g, xt, gt, gates, dots, w)
 
 def back_body(*refs, count, first, kinds):
     gu_refs, w_refs, o_ref = refs[:count], refs[count : 2 * count], refs[2 * count]
@@ -744,28 +746,28 @@
     each = mine // CHUNKS
     ff = w_gate.shape[2]
 
-    small = jnp.concatenate([w_router, norm1_gain[:, None], norm2_gain[:, None]], axis=1)
+    front = jnp.concatenate(
+        [jnp.concatenate([w_query, w_key, w_value], axis=1),
+         jnp.pad(norm1_gain[None], ((0, 7), (0, q_width + 2 * kv_width - part)))], axis=0
+    )
+    front = lax.all_gather(front, "fsdp", axis=0)
+    packed = jnp.concatenate([w_out.T, w_router, norm2_gain[:, None]], axis=1)
+    packed = jnp.pad(packed, ((0, 8), (0, 2 * q_width - packed.shape[1])))
     ordered = lambda here, there, axis=0: jnp.concatenate(
         [jnp.where(ctx == 0, here, there), jnp.where(ctx == 0, there, here)], axis=axis
     )
-    spare = -small.shape[1] % 128
-    packed = jnp.concatenate(
-        [w_query, w_key, w_value, w_out.T, small, jnp.zeros((part, spare), bf16)], axis=1
-    )
-    packed = lax.all_gather(packed, "fsdp", axis=0, tiled=True)
     shard_list = []
     for chunk in range(CHUNKS):
         first = ctx * mine + chunk * each
         pick = lambda w: lax.dynamic_slice_in_dim(w, first, each, 0)
         shard_list.append(jnp.stack([pick(w_gate), pick(w_up), pick(w_down).transpose(0, 2, 1)]))
-    packed, *shard_list = after(packed, *shard_list)
-    qkv_w = packed[:, : q_width + 2 * kv_width]
-    at = q_width + 2 * kv_width
-    out_w = packed[:, at : at + q_width]
-    at += q_width
-    router_w = packed[:, at : at + experts]
-    gain_one = packed[:, at + experts].astype(f32)
-    gain_two = packed[:, at + experts + 1].astype(f32)
+    front, packed, *shard_list = after(front, packed, *shard_list)
+    packed = lax.all_gather(packed, "fsdp", axis=0)[:, :part].reshape(width, 2 * q_width)
+    qkv_w = front[:, :part].reshape(width, q_width + 2 * kv_width)
+    gain_one = front[:, part, :part].reshape(width).astype(f32)
+    out_w = packed[:, :q_width]
+    router_w = packed[:, q_width : q_width + experts]
+    gain_two = packed[:, q_width + experts].astype(f32)
 
     stacked = [lax.all_gather(shard, "fsdp", axis=0) for shard in shard_list]
     ids_all = ordered(expert_ids, swap(expert_ids))
@@ -781,7 +783,12 @@
     ).astype(bf16)
     queries = rotate(jnp.dot(normed, qkv_w[:, :q_width], preferred_element_type=f32), cosine, sine)
     queries = queries.astype(bf16).transpose(1, 0, 2) * bf16(HD**-0.5)
-    keys_values = ordered(keys_values, swap(keys_values))
+    near = min(DOC, rows)
+    apart = lambda x: jnp.where(
+        ctx == 0, jnp.pad(x, ((0, rows - near), (0, 0))), jnp.pad(x, ((rows - near, 0), (0, 0)))
+    )
+    window = lax.dynamic_slice_in_dim(keys_values, jnp.where(ctx == 0, rows - near, 0), near)
+    keys_values = ordered(keys_values, apart(swap(window)))
     grad_here, keys_values = after(out_grad, keys_values)
     grad_all = ordered(grad_here, swap(grad_here))
     keys_values = keys_values.reshape(length, 2 * kv_heads, HD).transpose(1, 0, 2)
@@ -802,23 +809,21 @@
     masked = jnp.where(chosen, logits, masked_score)
     powers = jnp.exp(masked - jnp.max(masked, axis=1, keepdims=True))
     gates = powers / jnp.sum(powers, axis=1, keepdims=True)
-    gates_mine = jnp.where(ctx == 0, gates[:, :mine], gates[:, mine:])
 
     normed_t, grad_t = normed_two.T, grad_all.T
-    inner_all, outer_all, dots_all, shard_grads = [], [], [], []
+    inner_all, outer_all, shard_grads = [], [], []
+    dots = jnp.zeros_like(gates)
     for chunk in range(CHUNKS):
         inner, outer, grads, dots = moe_main(
-            normed_two, grad_all, normed_t, grad_t,
-            gates_mine[:, chunk * each : (chunk + 1) * each], stacked[chunk],
+            (ctx * mine + chunk * each).astype(jnp.int32).reshape(1),
+            normed_two, grad_all, normed_t, grad_t, gates, dots, stacked[chunk],
         )
         inner_all.append(inner)
         outer_all.append(outer)
-        dots_all.append(dots)
         shard_grads.append(lax.psum_scatter(grads, "fsdp", scatter_dimension=0, tiled=False))
     combined = moe_back(inner_all, stacked, 2, 1)
 
-    dots = jnp.concatenate(dots_all, axis=1)
-    weighted = gates * ordered(dots, jnp.zeros_like(dots), axis=1)
+    weighted = gates * dots
     dots_sum = jnp.sum(weighted, axis=1, keepdims=True)
     logit_grad = (weighted - gates * dots_sum).astype(bf16)
     router_grad = lax.dot_general(
@@ -844,8 +849,12 @@
     kv_grad = jnp.concatenate([key_grad, value_grad], axis=0).transpose(1, 0, 2).reshape(length, 2 * kv_width)
     kv_grad = kv_grad.astype(bf16)
     kept = lax.dynamic_slice_in_dim(kv_grad, start, rows)
-    given = lax.dynamic_slice_in_dim(kv_grad, rows - start, rows)
-    kv_grad = kept.astype(f32) + swap(given).astype(f32)
+    given = lax.dynamic_slice_in_dim(kv_grad, jnp.where(ctx == 0, rows, rows - near), near)
+    got = swap(given)
+    got = jnp.where(
+        ctx == 0, jnp.pad(got, ((rows - near, 0), (0, 0))), jnp.pad(got, ((0, rows - near), (0, 0)))
+    )
+    kv_grad = kept.astype(f32) + got.astype(f32)
     kv_grad, last = after(kv_grad, shard_grads[3])
     there.append(swap(last))
     query_grad = (query_grad * HD**-0.5).transpose(1, 0, 2).reshape(rows, q_width)
@@ -862,7 +871,7 @@
         tokens_own, hidden_grad, lin_grad, qkv_w, gain_one[None], small_grads, shards
     )
     input_grad = input_grad.reshape(rows, width)
-    hidden, small_grads = after(hidden, small_grads)
+    hidden, small_grads, there[-1] = after(hidden, small_grads, there[-1])
     mixed = lax.psum_scatter(combined, ("ctx", "tp"), scatter_dimension=0, tiled=True)
     block_out = lax.all_gather((hidden + mixed.astype(f32)).astype(bf16), "tp", axis=0, tiled=True)
 

time: 763 us -> 750 us (0.983)
  waiting for transfers between devices: 86.5 us -> 64 us
  Pallas kernels: 445 us -> 457 us
    ppermute x9, waiting for transfers between devices: 49.8 us -> 14.3 us  [swap(): return lax.ppermute(x, 'ctx', [(0, 1), (1, 0)])]
    reduce_scatter x4, waiting for transfers between devices: 0.08 us -> 26 us  [per_device(): lax.psum_scatter(grads, 'fsdp', scatter_dimension=0, tiled=False)]
    all_gather x1 -> x2, waiting for transfers between devices: 35.7 us -> 21 us  [the longest x1 21 us: per_device(): front = lax.all_gather(front, 'fsdp', axis=0)]
    pallas_call x1, Pallas kernels: 54.5 us -> 67.7 us  [tail(): pl.pallas_call(functools.partial(tail_body, shards=shards), in_specs=[WHO...]
    unnamed x134 -> x131, local copies, waits for them, and re-layouts: 29.1 us -> 30.2 us
  transfers between devices with their start and end apart: 21 -> 22, of which waited for: 5 -> 4; matrix products, arithmetic and copies ran while one was open for 24% -> 24% of each run, Pallas kernels for 59% -> 62%
where the time goes in v4:
time: 750 us; the launch traced here: 740 us
  Pallas kernels  457 us (61%)
  local copies, waits for them, and re-layouts  111 us (15%)
  waiting for transfers between devices  64 us (9%)
  other arithmetic  59.8 us (8%)
  matrix products  21.5 us (3%)
  between operations  15.2 us (2%)
  starting transfers between devices  11.8 us (2%)
    pallas_call x4, Pallas kernels, moe_main(): pl.pallas_call(moe_body, grid=(count // PAIR,), in_specs=[SMEMS, one(x.sh...  146 us
    pallas_call x1, Pallas kernels, mid(): pl.pallas_call(functools.partial(mid_body, share=heads // kv, length=leng...  94.6 us
    pallas_call x1, Pallas kernels, turn(): pl.pallas_call(functools.partial(turn_body, count=count, kinds=kinds, fir...  74.6 us
    pallas_call x1, Pallas kernels, tail(): pl.pallas_call(functools.partial(tail_body, shards=shards), in_specs=[WHO...  67.7 us
    pallas_call x1, Pallas kernels, flash_bwd(): pl.pallas_call(functools.partial(flash_bwd_body, share=heads // kv, lengt...  55.7 us
    unnamed x131, local copies, waits for them, and re-layouts  30.2 us
    reduce_scatter x4, waiting for transfers between devices, per_device(): lax.psum_scatter(grads, 'fsdp', scatter_dimension=0, tiled=False)  26 us
    all_gather x1, waiting for transfers between devices, per_device(): front = lax.all_gather(front, 'fsdp', axis=0)  21 us
  transfers between devices with their start and end apart: 22, of which 4 were waited for; matrix products, arithmetic and copies ran while one was open for 24% of the time, Pallas kernels for 62%

profile of v4, /device:TPU:0, one launch (start us, length us, event | category | flops | bytes accessed | tf_op | source)
XLA Modules:
  0.0 740.3 jit_solution(15154274053169690989)
XLA Ops:
  7.9 1.7 fusion.22
  12.8 2.5 dynamic-slice_bitcast_fusion
  18.2 2.2 pad_maximum_fusion.13
  20.4 21.0 %all-gather.16.cloned.1.call-done = bf16[1056,512]{1,0:T(8,128)(2,1)} async-done(((bf16[264,512]{1,0:T(8,128)(2,1)}), bf16[1056,512]{1,0:T(8,128)(2,1)}) %all-gather.16.cloned.1.call-update) | async-done | bytes 1081360 | tf_op jit(solution)/shard_map/all_gather | solution.py:753
  43.4 1.5 collective-permute-start.2
  58.0 1.8 copy.278
  64.8 1.9 copy.330
  66.7 1.8 fusion.12
  69.1 2.3 fusion.15
  72.6 2.0 copy.323
  74.6 3.1 copy.324
  78.0 3.5 subtract_convert_fusion
  81.5 2.1 fusion.4.q_ref
  83.7 1.6 broadcast_select_fusion.9
  85.4 1.7 copy.285
  87.1 3.1 copy.286
  90.2 2.0 fusion.31
  92.2 3.2 copy.291
  95.4 1.6 collective-permute-start.1
  100.3 94.6 %mid.1 = (bf16[1536,256]{1,0:T(8,128)(2,1)}, f32[384,1024]{1,0:T(8,128)}, bf16[8,384,1024]{2,1,0:T(8,128)(2,1)}) custom-call(bf16[384,1024]{1,0:T(8,128)(2,1)} %constant_dynamic-slice_fusion.7.tok_ref, bf16[4,1536,64]{2,1,0:T(8,128)(2,1)} %fusion.4.q_ref, bf16[2,3072,64]{2,1,0:T(8,128)(2,1)} %get-tuple-element.197.k_ref, ...), custom_call_target="tpu_custom_call" | custom-call | flops 99999997952 | bytes 1048576 | tf_op jit(solution)/shard_map/mid/pallas_call | solution.py:434
  194.9 8.7 %copy.318 = bf16[3072,1024]{0,1:T(8,128)(2,1)} copy(bf16[3072,1024]{1,0:T(8,128)(2,1)} %bitcast.144) | data formatting | bytes 12582912 | tf_op jit(solution)/shard_map/reshape | solution.py:805
  203.6 5.0 fusion.35
  209.5 2.6 fusion.5.gates_ref
  212.1 2.3 broadcast_select_fusion.1
  214.4 5.1 fusion.29
  219.4 8.7 %copy.297.g_ref = bf16[3072,1024]{1,0:T(8,128)(2,1)} copy(bf16[3072,1024]{0,1:T(8,128)(2,1)} %get-tuple-element.193) | data formatting | bytes 12582912 | tf_op jit(solution)/shard_map/concatenate | solution.py:756
  229.4 36.3 %moe_main.4 = (bf16[3072,512]{1,0:T(8,128)(2,1)}, bf16[3072,1024]{1,0:T(8,128)(2,1)}, bf16[4,3,4,256,128]{4,3,2,1,0:T(8,128)(2,1)}, f32[3072,32]{1,0:T(8,128)}) custom-call(s32[1]{0:T(128)} %bitcast.29.base_ref, bf16[3072,1024]{1,0:T(8,128)(2,1)} %bitcast.146, bf16[3072,1024]{1,0:T(8,128)(2,1)} %copy.297.g_ref, ...), custom_call_target="tpu_custom_call", output_to_operand_aliasing={{3}: (6, {})} | custom-call | flops 19327352832 | bytes 31457280 | tf_op jit(solution)/shard_map/moe_main/pallas_call | solution.py:189
  266.0 37.0 %moe_main.5 = (bf16[3072,512]{1,0:T(8,128)(2,1)}, bf16[3072,1024]{1,0:T(8,128)(2,1)}, bf16[4,3,4,256,128]{4,3,2,1,0:T(8,128)(2,1)}, f32[3072,32]{1,0:T(8,128)}) custom-call(s32[1]{0:T(128)} %bitcast.34.base_ref, bf16[3072,1024]{1,0:T(8,128)(2,1)} %bitcast.147, bf16[3072,1024]{1,0:T(8,128)(2,1)} %copy.297.g_ref, ...), custom_call_target="tpu_custom_call", output_to_operand_aliasing={{3}: (6, {})} | custom-call | flops 19327352832 | bytes 31457280 | tf_op jit(solution)/shard_map/moe_main/pallas_call | solution.py:189
  303.0 36.4 %moe_main.6 = (bf16[3072,512]{1,0:T(8,128)(2,1)}, bf16[3072,1024]{1,0:T(8,128)(2,1)}, bf16[4,3,4,256,128]{4,3,2,1,0:T(8,128)(2,1)}, f32[3072,32]{1,0:T(8,128)}) custom-call(s32[1]{0:T(128)} %bitcast.36.base_ref, bf16[3072,1024]{1,0:T(8,128)(2,1)} %bitcast.148, bf16[3072,1024]{1,0:T(8,128)(2,1)} %copy.297.g_ref, ...), custom_call_target="tpu_custom_call", output_to_operand_aliasing={{3}: (6, {})} | custom-call | flops 19327352832 | bytes 31457280 | tf_op jit(solution)/shard_map/moe_main/pallas_call | solution.py:189
  340.5 36.4 %moe_main.7 = (bf16[3072,512]{1,0:T(8,128)(2,1)}, bf16[3072,1024]{1,0:T(8,128)(2,1)}, bf16[4,3,4,256,128]{4,3,2,1,0:T(8,128)(2,1)}, f32[3072,32]{1,0:T(8,128)}) custom-call(s32[1]{0:T(128)} %bitcast.38.base_ref, bf16[3072,1024]{1,0:T(8,128)(2,1)} %bitcast.149, bf16[3072,1024]{1,0:T(8,128)(2,1)} %copy.297.g_ref, ...), custom_call_target="tpu_custom_call", output_to_operand_aliasing={{3}: (6, {})} | custom-call | flops 19327352832 | bytes 31457280 | tf_op jit(solution)/shard_map/moe_main/pallas_call | solution.py:189
  378.8 1.7 copy.305.dock_ref
  380.5 1.7 copy.306.blkk_ref
  382.7 2.1 constant_dynamic-slice_fusion.2.refs_11_
  386.2 3.6 fusion.30
  389.8 2.1 subtract_convert_fusion.1.refs_8_
  392.0 1.9 fusion.36
  393.9 18.8 %moe_out.1 = bf16[3072,1024]{1,0:T(8,128)(2,1)} custom-call(bf16[3072,512]{1,0:T(8,128)(2,1)} %get-tuple-element.105.refs_0_, bf16[3072,512]{1,0:T(8,128)(2,1)} %get-tuple-element.106.refs_1_, bf16[3072,512]{1,0:T(8,128)(2,1)} %get-tuple-element.107.refs_2_, bf16[3072,512]{1,0:T(8,128)(2,1)} %get-tuple-element.108.refs_3_, ...), custom_call_target="tpu_custom_call" | custom-call | flops 12884901888 | bytes 12582912 | tf_op jit(solution)/shard_map/moe_out/pallas_call | solution.py:239
  413.2 74.6 %turn.1 = (bf16[4,384,1024]{2,1,0:T(8,128)(2,1)}, f32[384,1024]{1,0:T(8,128)}, f32[1,1024]{1,0:T(1,128)}) custom-call(bf16[3072,1024]{1,0:T(8,128)(2,1)} %get-tuple-element.71.refs_0_, bf16[3072,1024]{1,0:T(8,128)(2,1)} %get-tuple-element.74.refs_1_, bf16[3072,1024]{1,0:T(8,128)(2,1)} %get-tuple-element.77.refs_2_, ...), custom_call_target="tpu_custom_call" | custom-call | flops 74999996416 | bytes 1048576 | tf_op jit(solution)/shard_map/turn/pallas_call | solution.py:665
  487.8 25.9 %reduce-scatter.9.cloned.1.call-done = bf16[1,3,4,256,128]{4,3,2,1,0:T(8,128)(2,1)} async-done(((bf16[4,3,4,256,128]{4,3,2,1,0:T(8,128)(2,1)}), bf16[1,3,4,256,128]{4,3,2,1,0:T(8,128)(2,1)}) %reduce-scatter.9.cloned.1.call-update) | async-done | bytes 786448 | tf_op jit(solution)/shard_map/reduce_scatter | solution.py:823
  513.8 3.8 convolution_convert_fusion
  517.6 2.8 copy.304
  520.4 1.5 collective-permute-start.3
  522.4 1.5 collective-permute-start.5
  523.9 55.7 %flash_bwd.1 = (f32[4,1536,64]{2,1,0:T(8,128)}, f32[2,3072,64]{2,1,0:T(8,128)}, f32[2,3072,64]{2,1,0:T(8,128)}) custom-call(s32[1]{0:T(128)} %bitcast.41.base_ref, bf16[4,1536,64]{2,1,0:T(8,128)(2,1)} %fusion.4.q_ref, bf16[4,1536,64]{2,1,0:T(8,128)(2,1)} %bitcast.173, bf16[2,3072,64]{2,1,0:T(8,128)(2,1)} %get-tuple-element.197.k_ref, ...), custom_call_target="tpu_custom_call" | custom-call | flops 54999998464 | bytes 1048576 | tf_op jit(solution)/shard_map/flash_bwd/pallas_call | solution.py:97
  580.3 4.0 convolution_convert_fusion.2
  587.5 2.6 copy.308
  594.5 2.2 multiply_bitcast_fusion
  596.7 2.0 copy.307
  598.7 6.5 collective-permute-done.6
  605.2 1.7 convert_add_fusion
  611.8 2.7 copy.312
  614.5 1.5 collective-permute-start.7
  616.0 3.3 convolution_convert_fusion.1
  622.4 67.7 %tail.1 = (bf16[4,384,1024]{2,1,0:T(8,128)(2,1)}, f32[40,256]{1,0:T(8,128)}) custom-call(bf16[384,1024]{1,0:T(8,128)(2,1)} %constant_dynamic-slice_fusion.7.tok_ref, f32[384,1024]{1,0:T(8,128)} %get-tuple-element.84.hg_ref, bf16[1536,512]{1,0:T(8,128)(2,1)} %pad_maximum_fusion.3.lin_ref, bf16[1024,512]{1,0:T(8,128)(2,1)} %bitcast.178, f32[1,1024]{1,0:T(1,128)} %bitcast.200, ...), custom_call_target="tpu_custom_call" | custom-call | flops 49999998976 | bytes 1048576 | tf_op jit(solution)/shard_map/tail/pallas_call | solution.py:521
  690.2 2.3 add_convert_fusion.1
  696.3 1.9 slice_bitcast_fusion.12
  699.1 1.9 slice_bitcast_fusion.10
  701.3 2.3 convert_bitcast_fusion
  703.6 5.9 copy.316
  709.8 2.3 maximum_convert_fusion.1
  713.8 2.3 maximum_convert_fusion
  716.7 7.8 %collective-permute-done.8 = bf16[256,768]{0,1:T(8,128)(2,1)S(1)} collective-permute-done((bf16[256,768]{0,1:T(8,128)(2,1)}, bf16[256,768]{0,1:T(8,128)(2,1)S(1)}, u32[]{:S(2)}, u32[]{:S(2)}) %collective-permute-start.8) | collective-permute-done | bytes 393248 | tf_op jit(solution)/shard_map/ppermute | solution.py:716
  727.7 4.0 copy.340
  731.7 1.7 copy.341
  (245 shorter events, 67.4 us)
Async XLA Ops:
  7.2 34.2 %all-gather.16.cloned.1.call-start = ((), (), s32[]{:S(2)}) async-start(), calls=%async_computation.13 | async-start | bytes 1351680 | tf_op jit(solution)/shard_map/all_gather | solution.py:753
  9.6 2.2 copy-start.52
  9.6 2.3 copy-start.45
  9.6 87.3 %all-gather.18.cloned.1.call-start = ((), (), s32[]{:S(2)}) async-start(), calls=%async_computation.14 | async-start | bytes 1351680 | tf_op jit(solution)/shard_map/all_gather | solution.py:765
  18.2 26.7 %copy-start.6 = (bf16[1536,1024]{1,0:T(8,128)(2,1)S(1)}, bf16[1536,1024]{1,0:T(8,128)(2,1)}, u32[]{:S(2)}) copy-start(bf16[1536,1024]{1,0:T(8,128)(2,1)} %param.15) | copy-start | bytes 9437188
  41.4 186.7 %all-gather.20.cloned.1.call-start = ((), (), s32[]{:S(2)}) async-start(), calls=%async_computation.15 | async-start | bytes 3932160 | tf_op jit(solution)/shard_map/all_gather | solution.py:772
  42.2 223.8 %all-gather.22.cloned.1.call-start = ((), (), s32[]{:S(2)}) async-start(), calls=%async_computation.16 | async-start | bytes 3932160 | tf_op jit(solution)/shard_map/all_gather | solution.py:772
  42.7 260.3 %all-gather.24.cloned.1.call-start = ((), (), s32[]{:S(2)}) async-start(), calls=%async_computation.17 | async-start | bytes 3932160 | tf_op jit(solution)/shard_map/all_gather | solution.py:772
  43.3 297.1 %all-gather.26.cloned.1.call-start = ((), (), s32[]{:S(2)}) async-start(), calls=%async_computation.18 | async-start | bytes 3932160 | tf_op jit(solution)/shard_map/all_gather | solution.py:772
  43.4 12.0 %collective-permute-start.2 = (s32[1536,8]{0,1:T(8,128)}, s32[1536,8]{0,1:T(8,128)}, u32[]{:S(2)}, u32[]{:S(2)}) collective-permute-start(s32[1536,8]{0,1:T(8,128)} %param.19), channel_id=1, source_target_pairs={{0,4},{4,0},{1,5},{5,1},{2,6},{6,2},{3,7},{7,3},{8,12},{12,8},{9,1... | collective-permute-start | bytes 147464 | tf_op jit(solution)/shard_map/ppermute | solution.py:716
  45.6 5.3 copy-start.41
  47.7 15.0 %copy-start.15 = (f32[1536,32]{0,1:T(8,128)}, f32[1536,32]{0,1:T(8,128)S(1)}, u32[]{:S(2)}) copy-start(f32[1536,32]{0,1:T(8,128)S(1)} %get-tuple-element.260) | copy-start | bytes 589828
  55.3 4.5 copy-start.9
  56.8 3.8 copy-start.47
  60.6 8.5 %copy-start.50 = (f32[1,2,4,128]{3,1,2,0:T(2,128)}, f32[1,2,4,128]{3,1,2,0:T(2,128)S(1)}, u32[]{:S(2)}) copy-start(f32[1,2,4,128]{3,1,2,0:T(2,128)S(1)} %copy.331) | copy-start | bytes 12292
  68.5 15.1 %collective-permute-start = (bf16[1024,256]{1,0:T(8,128)(2,1)}, bf16[1024,256]{1,0:T(8,128)(2,1)}, u32[]{:S(2)}, u32[]{:S(2)}) collective-permute-start(bf16[1024,256]{1,0:T(8,128)(2,1)} %fusion.12), channel_id=1, source_target_pairs={{0,4},{4,0},{1,5},{5,1},{2,6},{6,2},{3,7},{7,3},{8,12},{12,8},{9,1... | collective-permute-start | bytes 1572872 | tf_op jit(solution)/shard_map/ppermute | solution.py:716
  77.7 335.4 %reduce-scatter.7.cloned.1.call-start = ((), (), s32[]{:S(2)}) async-start(), calls=%async_computation.6 | async-start | bytes 3932160 | tf_op jit(solution)/shard_map/reduce_scatter | solution.py:823
  95.4 116.7 %collective-permute-start.1 = (bf16[1536,1024]{0,1:T(8,128)(2,1)S(1)}, bf16[1536,1024]{0,1:T(8,128)(2,1)}, u32[]{:S(2)}, u32[]{:S(2)}) collective-permute-start(bf16[1536,1024]{0,1:T(8,128)(2,1)S(1)} %copy.291), channel_id=1, source_target_pairs={{0,4},{4,0},{1,5},{5,1},{2,6},{6,2},{3,7},{7,3},{8,12},{12,8},{9,1... | collective-permute-start | bytes 9437192 | tf_op jit(solution)/shard_map/ppermute | solution.py:716
  194.8 8.7 %copy-start.18 = (pred[3072,32]{1,0:T(32,128)(4,1)S(1)}, pred[3072,32]{1,0:T(32,128)(4,1)}, u32[]{:S(2)}) copy-start(pred[3072,32]{1,0:T(32,128)(4,1)} %copy.293) | copy-start | bytes 294916
  208.5 3.5 copy-start
  265.7 222.1 %reduce-scatter.11.cloned.1.call-start = ((), (), s32[]{:S(2)}) async-start(), calls=%async_computation.8 | async-start | bytes 3932160 | tf_op jit(solution)/shard_map/reduce_scatter | solution.py:823
  339.4 174.3 %reduce-scatter.9.cloned.1.call-start = ((), (), s32[]{:S(2)}) async-start(), calls=%async_computation.7 | async-start | bytes 3932160 | tf_op jit(solution)/shard_map/reduce_scatter | solution.py:823
  340.2 266.7 %reduce-scatter.13.cloned.1.call-start = ((), (), s32[]{:S(2)}) async-start(), calls=%async_computation.9 | async-start | bytes 3932160 | tf_op jit(solution)/shard_map/reduce_scatter | solution.py:823
  376.9 3.6 copy-start.43
  376.9 313.2 %reduce-scatter.15.cloned.1.call-start = ((), (), s32[]{:S(2)}) async-start(), calls=%async_computation.10 | async-start | bytes 7077888 | tf_op jit(solution)/shard_map/reduce_scatter | solution.py:875
  378.8 6.1 copy-start.46
  378.8 6.7 copy-start.4
  378.8 13.2 %slice-start = ((s8[6291456]{0:T(1024)(128)(4,1)}), s8[2097152]{0:T(1024)(128)(4,1)S(1)}, s32[]{:S(2)}) async-start(s8[6291456]{0:T(1024)(128)(4,1)} %bitcast.150), calls=%async_computation.19 | async-start | bytes 4194304
  382.1 4.0 copy-start.1
  386.2 5.8 slice-start.1
  412.7 300.3 %reduce-scatter.17.cloned.1.call-start = ((), (), s32[]{:S(2)}) async-start(), calls=%async_computation.12 | async-start | bytes 1966080 | tf_op jit(solution)/shard_map/reduce_scatter | solution.py:879
  517.6 2.8 copy-start.25
  517.6 4.3 copy-start.28
  517.6 4.8 copy-start.27
  520.4 64.0 %collective-permute-start.3 = (bf16[3,4,256,128]{3,2,1,0:T(8,128)(2,1)S(1)}, bf16[3,4,256,128]{3,2,1,0:T(8,128)(2,1)}, u32[]{:S(2)}, u32[]{:S(2)}) collective-permute-start(bf16[3,4,256,128]{3,2,1,0:T(8,128)(2,1)S(1)} %bitcast.184), channel_id=1, source_target_pairs={{0,4},{4,0},{1,5},{5,1},{2,6},{6,2},{3,7},{7,3},{8,12},{12,8},{9,1... | collective-permute-start | bytes 2359304 | tf_op jit(solution)/shard_map/ppermute | solution.py:716
  521.8 62.6 %collective-permute-start.4 = (bf16[3,4,256,128]{3,2,1,0:T(8,128)(2,1)S(1)}, bf16[3,4,256,128]{3,2,1,0:T(8,128)(2,1)}, u32[]{:S(2)}, u32[]{:S(2)}) collective-permute-start(bf16[3,4,256,128]{3,2,1,0:T(8,128)(2,1)S(1)} %bitcast.187), channel_id=1, source_target_pairs={{0,4},{4,0},{1,5},{5,1},{2,6},{6,2},{3,7},{7,3},{8,12},{12,8},{9,1... | collective-permute-start | bytes 2359304 | tf_op jit(solution)/shard_map/ppermute | solution.py:716
  522.4 62.0 %collective-permute-start.5 = (bf16[3,4,256,128]{3,2,1,0:T(8,128)(2,1)S(1)}, bf16[3,4,256,128]{3,2,1,0:T(8,128)(2,1)S(1)}, u32[]{:S(2)}, u32[]{:S(2)}) collective-permute-start(bf16[3,4,256,128]{3,2,1,0:T(8,128)(2,1)S(1)} %bitcast.186), channel_id=1, source_target_pairs={{0,4},{4,0},{1,5},{5,1},{2,6},{6,2},{3,7},{7,3},{8,12},{12,8},{9,1... | collective-permute-start | bytes 2359304 | tf_op jit(solution)/shard_map/ppermute | solution.py:716
  523.9 55.7 %copy-start.33 = (f32[32,1024]{1,0:T(8,128)S(1)}, f32[32,1024]{1,0:T(8,128)}, u32[]{:S(2)}) copy-start(f32[32,1024]{1,0:T(8,128)} %fusion.36) | copy-start | bytes 393220
  523.9 55.7 %copy-start.49 = (f32[1,1024]{1,0:T(1,128)S(1)}, f32[1,1024]{1,0:T(1,128)}, u32[]{:S(2)}) copy-start(f32[1,1024]{1,0:T(1,128)} %get-tuple-element.101) | copy-start | bytes 12292
  523.9 55.7 %copy-start.53 = (f32[40]{0:T(128)S(1)}, f32[40]{0:T(128)}, u32[]{:S(2)}) copy-start(f32[40]{0:T(128)} %pad.62.clone) | copy-start | bytes 484
  580.3 4.1 copy-start.13
  584.4 2.2 copy-start.12
  590.1 3.1 copy-start.5
  592.4 12.8 %collective-permute-start.6 = (bf16[1024,256]{1,0:T(8,128)(2,1)}, bf16[1024,256]{1,0:T(8,128)(2,1)}, u32[]{:S(2)}, u32[]{:S(2)}) collective-permute-start(bf16[1024,256]{1,0:T(8,128)(2,1)} %copy.326), channel_id=1, source_target_pairs={{0,4},{4,0},{1,5},{5,1},{2,6},{6,2},{3,7},{7,3},{8,12},{12,8},{9,1... | collective-permute-start | bytes 1572872 | tf_op jit(solution)/shard_map/ppermute | solution.py:716
  606.9 2.4 copy-start.2
  610.7 5.3 copy-start.7
  610.7 5.3 copy-start.48
  610.7 5.3 copy-start.51
  614.5 4.8 copy-start.34
  614.5 75.6 %collective-permute-start.7 = (bf16[3,4,256,128]{3,2,1,0:T(8,128)(2,1)}, bf16[3,4,256,128]{3,2,1,0:T(8,128)(2,1)}, u32[]{:S(2)}, u32[]{:S(2)}) collective-permute-start(bf16[3,4,256,128]{3,2,1,0:T(8,128)(2,1)} %bitcast.188), channel_id=1, source_target_pairs={{0,4},{4,0},{1,5},{5,1},{2,6},{6,2},{3,7},{7,3},{8,12},{12,8},{9,1... | collective-permute-start | bytes 2359304 | tf_op jit(solution)/shard_map/ppermute | solution.py:716
  622.4 105.3 %all-gather.14.cloned.1.call-start = ((), (), s32[]{:S(2)}) async-start(), calls=%async_computation.11 | async-start | bytes 3932160 | tf_op jit(solution)/shard_map/all_gather | solution.py:876
  622.4 67.8 %copy-start.17 = (f32[384,1024]{1,0:T(8,128)S(1)}, f32[384,1024]{1,0:T(8,128)}, u32[]{:S(2)}) copy-start(f32[384,1024]{1,0:T(8,128)} %get-tuple-element.104.refs_10_) | copy-start | bytes 4718596
  690.1 2.4 copy-start.26
  692.6 2.5 copy-start.29
  695.0 3.2 copy-start.31
  703.6 5.9 copy-start.23
  703.6 5.9 copy-start.24
  709.7 2.3 copy-start.44
  709.8 2.9 copy-start.20
  709.8 2.9 copy-start.21
  709.8 2.9 copy-start.22
  713.0 11.5 %collective-permute-start.8 = (bf16[256,768]{0,1:T(8,128)(2,1)}, bf16[256,768]{0,1:T(8,128)(2,1)S(1)}, u32[]{:S(2)}, u32[]{:S(2)}) collective-permute-start(bf16[256,768]{0,1:T(8,128)(2,1)} %reduce-scatter.17.cloned.1.call-done), channel_id=1, source_target_pairs={{0,4},{4,0},{1,5},{5,1},{2,6},{6,2},{3,7},{7,3},{8,12},{12,8},{9,1... | collective-permute-start | bytes 1179656 | tf_op jit(solution)/shard_map/ppermute | solution.py:716
  713.8 10.7 %copy-start.35 = (bf16[256,768]{0,1:T(8,128)(2,1)S(1)}, bf16[256,768]{0,1:T(8,128)(2,1)}, u32[]{:S(2)}) copy-start(bf16[256,768]{0,1:T(8,128)(2,1)} %reduce-scatter.17.cloned.1.call-done) | copy-start | bytes 1179652
  727.7 4.0 copy-start.11
  (14 other events, 18.9 us)
Sparse Core Ops, SparseCore 0:
  10.1 31.2 all-gather.15
  43.0 27.8 all-gather.17
  72.5 62.8 all-gather.19
  136.7 62.0 all-gather.21
  200.3 62.0 all-gather.23
  263.8 62.0 all-gather.25
  328.8 59.0 reduce-scatter.6
  390.2 60.3 reduce-scatter.10
  453.4 60.3 reduce-scatter.8
  515.9 60.3 reduce-scatter.12
  579.7 76.2 reduce-scatter.14
  658.7 38.0 reduce-scatter.16
  698.9 27.3 all-gather.13

commit v5 on v4

--- a/solution.py
+++ b/solution.py
@@ -396,9 +396,16 @@
 
 
 def mid_body(tok_ref, q_ref, k_ref, v_ref, docq_ref, blkq_ref, dock_ref, blkk_ref, w_ref, gain_ref,
-             mix_ref, hid_ref, all_ref, send, pair_in, far_in, own, sems, *, share, length):
+             mix_ref, hid_ref, all_ref, whole_ref, send, pair_in, far_in, own, sems, w_sems, *, share, length):
     place = Place()
-    place.meet((place.pair, place.far, place.side))
+    shards, part, _ = whole_ref.shape
+    z = lax.axis_index("fsdp")
+    others = [{"fsdp": lax.rem(z + d, shards)} for d in range(1, shards)]
+    place.meet((place.pair, place.far, place.side, *others))
+    spread = [push(w_ref, whole_ref.at[z], w_sems, d, device) for d, device in enumerate(others)]
+    for copy in spread:
+        copy.start()
+    whole_ref[z] = w_ref[...]
     heads, rows, _ = q_ref.shape
     block = rows // 4
     band = min(DOC + block + BLK, length)
@@ -418,27 +425,39 @@
             outs.append(nn(p.astype(jnp.bfloat16), v_ref[head // share, keys, :]).astype(jnp.bfloat16))
         mix = jnp.concatenate(outs, axis=1)
         mix_ref[here, :] = mix
-        send[j] = nt(mix, w_ref[...]).astype(jnp.bfloat16)
+
+        @pl.when(j == 0)
+        def _():
+            for copy in spread:
+                copy.wait_recv()
+
+        for n in range(shards):
+            send[j, :, n * part : (n + 1) * part] = nt(mix, whole_ref[n]).astype(jnp.bfloat16)
 
     reduce_four(place, produce, send, pair_in, far_in, own, sems, 0)
     hidden = tok_ref[...].astype(jnp.float32) + own[...]
     hid_ref[...] = hidden
     all_ref[place.ctx * 4 + place.tp] = (normalize(hidden)[1] * gain_ref[...]).astype(jnp.bfloat16)
     gather_eight(place, all_ref, sems, 3)
+    for copy in spread:
+        copy.wait_send()
 
 
 def mid(tok, q, k, v, docq, blkq, dock, blkk, out_w, gain):
     heads, rows, _ = q.shape
     kv, length, _ = k.shape
     own, width = tok.shape
+    part = out_w.shape[0]
+    shards = width // part
     return pl.pallas_call(
         functools.partial(mid_body, share=heads // kv, length=length),
         in_specs=[WHOLE] * 10,
-        out_specs=[WHOLE] * 3,
+        out_specs=[WHOLE] * 4,
         out_shape=[
             jax.ShapeDtypeStruct((rows, heads * HD), jnp.bfloat16),
             jax.ShapeDtypeStruct((own, width), jnp.float32),
             jax.ShapeDtypeStruct((8, own, width), jnp.bfloat16),
+            jax.ShapeDtypeStruct((shards, *out_w.shape), jnp.bfloat16),
         ],
         scratch_shapes=[
             pltpu.VMEM((4, own, width), jnp.bfloat16),
@@ -446,6 +465,7 @@
             pltpu.VMEM((own, width), jnp.bfloat16),
             pltpu.VMEM((own, width), jnp.float32),
             pltpu.SemaphoreType.DMA((2, 12)),
+            pltpu.SemaphoreType.DMA((2, shards - 1)),
         ],
         compiler_params=pltpu.CompilerParams(vmem_limit_bytes=VL, collective_id=0, has_side_effects=True),
         cost_estimate=busy(100),
@@ -746,13 +766,12 @@
     each = mine // CHUNKS
     ff = w_gate.shape[2]
 
-    front = jnp.concatenate(
-        [jnp.concatenate([w_query, w_key, w_value], axis=1),
-         jnp.pad(norm1_gain[None], ((0, 7), (0, q_width + 2 * kv_width - part)))], axis=0
-    )
+    columns = q_width + 2 * kv_width
+    extra = jnp.concatenate([norm1_gain, norm2_gain, w_router.reshape(-1)])
+    extra_rows = -(-extra.shape[0] // (8 * columns)) * 8
+    extra = jnp.pad(extra, (0, extra_rows * columns - extra.shape[0])).reshape(extra_rows, columns)
+    front = jnp.concatenate([jnp.concatenate([w_query, w_key, w_value], axis=1), extra], axis=0)
     front = lax.all_gather(front, "fsdp", axis=0)
-    packed = jnp.concatenate([w_out.T, w_router, norm2_gain[:, None]], axis=1)
-    packed = jnp.pad(packed, ((0, 8), (0, 2 * q_width - packed.shape[1])))
     ordered = lambda here, there, axis=0: jnp.concatenate(
         [jnp.where(ctx == 0, here, there), jnp.where(ctx == 0, there, here)], axis=axis
     )
@@ -761,13 +780,12 @@
         first = ctx * mine + chunk * each
         pick = lambda w: lax.dynamic_slice_in_dim(w, first, each, 0)
         shard_list.append(jnp.stack([pick(w_gate), pick(w_up), pick(w_down).transpose(0, 2, 1)]))
-    front, packed, *shard_list = after(front, packed, *shard_list)
-    packed = lax.all_gather(packed, "fsdp", axis=0)[:, :part].reshape(width, 2 * q_width)
-    qkv_w = front[:, :part].reshape(width, q_width + 2 * kv_width)
-    gain_one = front[:, part, :part].reshape(width).astype(f32)
-    out_w = packed[:, :q_width]
-    router_w = packed[:, q_width : q_width + experts]
-    gain_two = packed[:, q_width + experts].astype(f32)
+    front, *shard_list = after(front, *shard_list)
+    qkv_w = front[:, :part].reshape(width, columns)
+    extra = front[:, part:].reshape(shards, extra_rows * columns)
+    gain_one = extra[:, :part].reshape(width).astype(f32)
+    gain_two = extra[:, part : 2 * part].reshape(width).astype(f32)
+    router_w = extra[:, 2 * part : (2 + experts) * part].reshape(width, experts)
 
     stacked = [lax.all_gather(shard, "fsdp", axis=0) for shard in shard_list]
     ids_all = ordered(expert_ids, swap(expert_ids))
@@ -798,10 +816,11 @@
     base = start.astype(jnp.int32).reshape(1)
     tokens_own = lax.dynamic_slice_in_dim(tokens, tp * own, own)
     grad_own = lax.dynamic_slice_in_dim(out_grad, tp * own, own)
-    attn_mix, hidden, normed_two = mid(
+    attn_mix, hidden, normed_two, out_w = mid(
         tokens_own, queries, keys, values, query_doc[:, None], query_block[:, None], doc_ids[None],
-        block_ids[None], out_w, gain_two[None],
-    )
+        block_ids[None], w_out.T, gain_two[None],
+    )
+    out_w = out_w.reshape(width, q_width)
     normed_two = normed_two.reshape(ctx_size * rows, width)
 
     logits = jnp.dot(normed_two, router_w, preferred_element_type=f32)

time: 750 us -> 727 us (0.969)
  waiting for transfers between devices: 64 us -> 45.8 us
    reduce_scatter x4, waiting for transfers between devices: 26 us -> 0.08 us  [per_device(): lax.psum_scatter(grads, 'fsdp', scatter_dimension=0, tiled=False)]
    pallas_call x1, Pallas kernels: 67.7 us -> 59.8 us  [tail(): pl.pallas_call(functools.partial(tail_body, shards=shards), in_specs=[WHO...]
    unnamed x131 -> x126, local copies, waits for them, and re-layouts: 30.2 us -> 34.1 us
  transfers between devices with their start and end apart: 22 -> 21, of which waited for: 4 -> 3; matrix products, arithmetic and copies ran while one was open for 24% -> 25% of each run, Pallas kernels for 62% -> 63%
where the time goes in v5:
time: 727 us; the launch traced here: 718 us
  Pallas kernels  453 us (62%)
  local copies, waits for them, and re-layouts  112 us (15%)
  other arithmetic  58.9 us (8%)
  waiting for transfers between devices  45.8 us (6%)
  matrix products  20.5 us (3%)
  between operations  15.5 us (2%)
  starting transfers between devices  12.8 us (2%)
    pallas_call x4, Pallas kernels, moe_main(): pl.pallas_call(moe_body, grid=(count // PAIR,), in_specs=[SMEMS, one(x.sh...  146 us
    pallas_call x1, Pallas kernels, mid(): pl.pallas_call(functools.partial(mid_body, share=heads // kv, length=leng...  98.6 us
    pallas_call x1, Pallas kernels, turn(): pl.pallas_call(functools.partial(turn_body, count=count, kinds=kinds, fir...  74.5 us
    pallas_call x1, Pallas kernels, tail(): pl.pallas_call(functools.partial(tail_body, shards=shards), in_specs=[WHO...  59.8 us
    pallas_call x1, Pallas kernels, flash_bwd(): pl.pallas_call(functools.partial(flash_bwd_body, share=heads // kv, lengt...  55.8 us
    unnamed x126, local copies, waits for them, and re-layouts  34.1 us
    all_gather x1, waiting for transfers between devices, per_device(): front = lax.all_gather(front, 'fsdp', axis=0)  22.8 us
    ppermute x9, waiting for transfers between devices, swap(): return lax.ppermute(x, 'ctx', [(0, 1), (1, 0)])  21.2 us
  transfers between devices with their start and end apart: 21, of which 3 were waited for; matrix products, arithmetic and copies ran while one was open for 25% of the time, Pallas kernels for 63%

profile of v5, /device:TPU:0, one launch (start us, length us, event | category | flops | bytes accessed | tf_op | source)
XLA Modules:
  0.0 718.2 jit_solution(3853791373713110170)
XLA Ops:
  8.9 1.7 pad_maximum_fusion.18
  12.7 2.5 dynamic-slice_bitcast_fusion
  18.1 2.1 pad_maximum_fusion.13
  20.3 22.8 %all-gather.14.cloned.1.call-done = bf16[1120,512]{1,0:T(8,128)(2,1)} async-done(((bf16[280,512]{1,0:T(8,128)(2,1)}), bf16[1120,512]{1,0:T(8,128)(2,1)}) %all-gather.14.cloned.1.call-update) | async-done | bytes 1146896 | tf_op jit(solution)/shard_map/all_gather | solution.py:774
  43.9 1.5 collective-permute-start.2
  56.6 1.7 copy.223
  68.7 1.9 copy.267
  70.6 1.8 fusion.7
  73.0 2.3 fusion.10
  76.5 2.0 copy.260
  78.5 3.1 copy.261
  82.2 1.7 reshape.244.refs_9_
  84.2 3.1 subtract_convert_fusion
  87.4 2.1 fusion.4.q_ref
  89.5 1.6 broadcast_select_fusion.9
  91.2 1.7 copy.221
  93.0 3.1 copy.222
  96.1 2.0 fusion.23
  98.0 3.2 copy.228
  101.2 1.5 collective-permute-start.1
  102.7 98.6 %mid.1 = (bf16[1536,256]{1,0:T(8,128)(2,1)}, f32[384,1024]{1,0:T(8,128)}, bf16[8,384,1024]{2,1,0:T(8,128)(2,1)}, bf16[4,256,256]{2,1,0:T(8,128)(2,1)}) custom-call(bf16[384,1024]{1,0:T(8,128)(2,1)} %constant_dynamic-slice_fusion.7.tok_ref, bf16[4,1536,64]{2,1,0:T(8,128)(2,1)} %fusion.4.q_ref, bf16[2,3072,64]{2,1,0:T(8,128)(2,1)} %get-tuple-element.185.k_ref, ...), custom_call_target="tpu_custom_call" | custom-call | flops 99999997952 | bytes 1048576 | tf_op jit(solution)/shard_map/mid/pallas_call | solution.py:452
  201.4 8.7 %copy.255 = bf16[3072,1024]{0,1:T(8,128)(2,1)} copy(bf16[3072,1024]{1,0:T(8,128)(2,1)} %bitcast.150) | data formatting | bytes 12582912 | tf_op jit(solution)/shard_map/reshape | solution.py:824
  210.1 4.7 fusion.27
  215.8 2.6 fusion.5.gates_ref
  218.3 2.3 broadcast_select_fusion.1
  220.7 5.1 fusion.21
  225.7 8.6 %copy.234.g_ref = bf16[3072,1024]{1,0:T(8,128)(2,1)} copy(bf16[3072,1024]{0,1:T(8,128)(2,1)} %get-tuple-element.181) | data formatting | bytes 12582912 | tf_op jit(solution)/shard_map/concatenate | solution.py:775
  235.6 37.0 %moe_main.4 = (bf16[3072,512]{1,0:T(8,128)(2,1)}, bf16[3072,1024]{1,0:T(8,128)(2,1)}, bf16[4,3,4,256,128]{4,3,2,1,0:T(8,128)(2,1)}, f32[3072,32]{1,0:T(8,128)}) custom-call(s32[1]{0:T(128)} %bitcast.27.base_ref, bf16[3072,1024]{1,0:T(8,128)(2,1)} %bitcast.152, bf16[3072,1024]{1,0:T(8,128)(2,1)} %copy.234.g_ref, ...), custom_call_target="tpu_custom_call", output_to_operand_aliasing={{3}: (6, {})} | custom-call | flops 19327352832 | bytes 31457280 | tf_op jit(solution)/shard_map/moe_main/pallas_call | solution.py:189
  272.9 36.4 %moe_main.5 = (bf16[3072,512]{1,0:T(8,128)(2,1)}, bf16[3072,1024]{1,0:T(8,128)(2,1)}, bf16[4,3,4,256,128]{4,3,2,1,0:T(8,128)(2,1)}, f32[3072,32]{1,0:T(8,128)}) custom-call(s32[1]{0:T(128)} %bitcast.32.base_ref, bf16[3072,1024]{1,0:T(8,128)(2,1)} %bitcast.153, bf16[3072,1024]{1,0:T(8,128)(2,1)} %copy.234.g_ref, ...), custom_call_target="tpu_custom_call", output_to_operand_aliasing={{3}: (6, {})} | custom-call | flops 19327352832 | bytes 31457280 | tf_op jit(solution)/shard_map/moe_main/pallas_call | solution.py:189
  309.3 36.3 %moe_main.6 = (bf16[3072,512]{1,0:T(8,128)(2,1)}, bf16[3072,1024]{1,0:T(8,128)(2,1)}, bf16[4,3,4,256,128]{4,3,2,1,0:T(8,128)(2,1)}, f32[3072,32]{1,0:T(8,128)}) custom-call(s32[1]{0:T(128)} %bitcast.34.base_ref, bf16[3072,1024]{1,0:T(8,128)(2,1)} %bitcast.154, bf16[3072,1024]{1,0:T(8,128)(2,1)} %copy.234.g_ref, ...), custom_call_target="tpu_custom_call", output_to_operand_aliasing={{3}: (6, {})} | custom-call | flops 19327352832 | bytes 31457280 | tf_op jit(solution)/shard_map/moe_main/pallas_call | solution.py:189
  346.7 36.4 %moe_main.7 = (bf16[3072,512]{1,0:T(8,128)(2,1)}, bf16[3072,1024]{1,0:T(8,128)(2,1)}, bf16[4,3,4,256,128]{4,3,2,1,0:T(8,128)(2,1)}, f32[3072,32]{1,0:T(8,128)}) custom-call(s32[1]{0:T(128)} %bitcast.36.base_ref, bf16[3072,1024]{1,0:T(8,128)(2,1)} %bitcast.155, bf16[3072,1024]{1,0:T(8,128)(2,1)} %copy.234.g_ref, ...), custom_call_target="tpu_custom_call", output_to_operand_aliasing={{3}: (6, {})} | custom-call | flops 19327352832 | bytes 31457280 | tf_op jit(solution)/shard_map/moe_main/pallas_call | solution.py:189
  385.1 1.7 copy.242.dock_ref
  386.8 1.7 copy.243.blkk_ref
  389.0 2.0 constant_dynamic-slice_fusion.2.refs_11_
  391.7 3.6 fusion.22
  395.3 2.1 subtract_convert_fusion.1.refs_8_
  397.5 1.9 fusion.28
  399.3 18.2 %moe_out.1 = bf16[3072,1024]{1,0:T(8,128)(2,1)} custom-call(bf16[3072,512]{1,0:T(8,128)(2,1)} %get-tuple-element.105.refs_0_, bf16[3072,512]{1,0:T(8,128)(2,1)} %get-tuple-element.106.refs_1_, bf16[3072,512]{1,0:T(8,128)(2,1)} %get-tuple-element.107.refs_2_, bf16[3072,512]{1,0:T(8,128)(2,1)} %get-tuple-element.108.refs_3_, ...), custom_call_target="tpu_custom_call" | custom-call | flops 12884901888 | bytes 12582912 | tf_op jit(solution)/shard_map/moe_out/pallas_call | solution.py:239
  418.1 74.5 %turn.1 = (bf16[4,384,1024]{2,1,0:T(8,128)(2,1)}, f32[384,1024]{1,0:T(8,128)}, f32[1,1024]{1,0:T(1,128)}) custom-call(bf16[3072,1024]{1,0:T(8,128)(2,1)} %get-tuple-element.70.refs_0_, bf16[3072,1024]{1,0:T(8,128)(2,1)} %get-tuple-element.73.refs_1_, bf16[3072,1024]{1,0:T(8,128)(2,1)} %get-tuple-element.76.refs_2_, ...), custom_call_target="tpu_custom_call" | custom-call | flops 74999996416 | bytes 1048576 | tf_op jit(solution)/shard_map/turn/pallas_call | solution.py:685
  492.7 3.0 convolution_convert_fusion
  495.7 1.7 copy.241
  500.9 55.8 %flash_bwd.1 = (f32[4,1536,64]{2,1,0:T(8,128)}, f32[2,3072,64]{2,1,0:T(8,128)}, f32[2,3072,64]{2,1,0:T(8,128)}) custom-call(s32[1]{0:T(128)} %bitcast.39.base_ref, bf16[4,1536,64]{2,1,0:T(8,128)(2,1)} %fusion.4.q_ref, bf16[4,1536,64]{2,1,0:T(8,128)(2,1)} %bitcast.172, bf16[2,3072,64]{2,1,0:T(8,128)(2,1)} %get-tuple-element.185.k_ref, ...), custom_call_target="tpu_custom_call" | custom-call | flops 54999998464 | bytes 1048576 | tf_op jit(solution)/shard_map/flash_bwd/pallas_call | solution.py:97
  557.5 4.1 convolution_convert_fusion.2
  562.5 1.8 copy-done.9
  565.1 2.6 copy.245
  572.2 2.1 multiply_bitcast_fusion
  574.3 2.0 copy.244
  576.3 14.4 %collective-permute-done.6 = bf16[1024,256]{1,0:T(8,128)(2,1)} collective-permute-done((bf16[1024,256]{1,0:T(8,128)(2,1)}, bf16[1024,256]{1,0:T(8,128)(2,1)}, u32[]{:S(2)}, u32[]{:S(2)}) %collective-permute-start.6) | collective-permute-done | bytes 524320 | tf_op jit(solution)/shard_map/ppermute | solution.py:736
  590.7 1.7 convert_add_fusion
  597.4 2.7 copy.249
  600.1 1.5 collective-permute-start.7
  601.6 3.3 convolution_convert_fusion.1
  608.1 59.8 %tail.1 = (bf16[4,384,1024]{2,1,0:T(8,128)(2,1)}, f32[40,256]{1,0:T(8,128)}) custom-call(bf16[384,1024]{1,0:T(8,128)(2,1)} %constant_dynamic-slice_fusion.7.tok_ref, f32[384,1024]{1,0:T(8,128)} %get-tuple-element.83.hg_ref, bf16[1536,512]{1,0:T(8,128)(2,1)} %pad_maximum_fusion.3.lin_ref, bf16[1024,512]{1,0:T(8,128)(2,1)} %bitcast.179, f32[1,1024]{1,0:T(1,128)} %bitcast.202, ...), custom_call_target="tpu_custom_call" | custom-call | flops 49999998976 | bytes 1048576 | tf_op jit(solution)/shard_map/tail/pallas_call | solution.py:541
  668.0 2.3 add_convert_fusion.1
  674.1 1.9 slice_bitcast_fusion.12
  676.8 2.0 slice_bitcast_fusion.10
  679.1 2.3 convert_bitcast_fusion
  681.4 5.7 copy.253
  687.4 2.3 maximum_convert_fusion.1
  690.6 1.7 collective-permute-start.8
  692.3 2.3 maximum_convert_fusion
  695.2 6.8 collective-permute-done.8
  705.2 4.0 copy.279
  709.3 1.7 copy.280
  (234 shorter events, 67.1 us)
Async XLA Ops:
  7.2 35.9 %all-gather.14.cloned.1.call-start = ((), (), s32[]{:S(2)}) async-start(), calls=%async_computation.13 | async-start | bytes 1433600 | tf_op jit(solution)/shard_map/all_gather | solution.py:774
  10.6 223.7 %all-gather.16.cloned.1.call-start = ((), (), s32[]{:S(2)}) async-start(), calls=%async_computation.14 | async-start | bytes 3932160 | tf_op jit(solution)/shard_map/all_gather | solution.py:790
  18.1 28.0 %copy-start.4 = (bf16[1536,1024]{1,0:T(8,128)(2,1)S(1)}, bf16[1536,1024]{1,0:T(8,128)(2,1)}, u32[]{:S(2)}) copy-start(bf16[1536,1024]{1,0:T(8,128)(2,1)} %param.15) | copy-start | bytes 9437188
  43.1 229.8 %all-gather.18.cloned.1.call-start = ((), (), s32[]{:S(2)}) async-start(), calls=%async_computation.15 | async-start | bytes 3932160 | tf_op jit(solution)/shard_map/all_gather | solution.py:790
  43.9 265.4 %all-gather.20.cloned.1.call-start = ((), (), s32[]{:S(2)}) async-start(), calls=%async_computation.16 | async-start | bytes 3932160 | tf_op jit(solution)/shard_map/all_gather | solution.py:790
  43.9 14.3 %collective-permute-start.2 = (s32[1536,8]{0,1:T(8,128)}, s32[1536,8]{0,1:T(8,128)}, u32[]{:S(2)}, u32[]{:S(2)}) collective-permute-start(s32[1536,8]{0,1:T(8,128)} %param.19), channel_id=1, source_target_pairs={{0,4},{4,0},{1,5},{5,1},{2,6},{6,2},{3,7},{7,3},{8,12},{12,8},{9,1... | collective-permute-start | bytes 147464 | tf_op jit(solution)/shard_map/ppermute | solution.py:736
  46.1 300.6 %all-gather.22.cloned.1.call-start = ((), (), s32[]{:S(2)}) async-start(), calls=%async_computation.17 | async-start | bytes 3932160 | tf_op jit(solution)/shard_map/all_gather | solution.py:790
  46.9 5.3 copy-start.37
  48.9 17.7 %copy-start.12 = (f32[1536,32]{0,1:T(8,128)}, f32[1536,32]{0,1:T(8,128)S(1)}, u32[]{:S(2)}) copy-start(f32[1536,32]{0,1:T(8,128)S(1)} %get-tuple-element.249) | copy-start | bytes 589828
  54.0 9.8 %copy-start.43 = (f32[1536]{0:T(1024)S(1)}, f32[1536]{0:T(1024)}, u32[]{:S(2)}) copy-start(f32[1536]{0:T(1024)} %add_rsqrt_fusion) | copy-start | bytes 18436
  62.1 3.0 copy-start.16
  63.8 9.2 %copy-start.46 = (f32[1,2,4,128]{3,1,2,0:T(2,128)}, f32[1,2,4,128]{3,1,2,0:T(2,128)S(1)}, u32[]{:S(2)}) copy-start(f32[1,2,4,128]{3,1,2,0:T(2,128)S(1)} %copy.269) | copy-start | bytes 12292
  72.4 17.1 %collective-permute-start = (bf16[1024,256]{1,0:T(8,128)(2,1)}, bf16[1024,256]{1,0:T(8,128)(2,1)}, u32[]{:S(2)}, u32[]{:S(2)}) collective-permute-start(bf16[1024,256]{1,0:T(8,128)(2,1)} %fusion.7), channel_id=1, source_target_pairs={{0,4},{4,0},{1,5},{5,1},{2,6},{6,2},{3,7},{7,3},{8,12},{12,8},{9,1... | collective-permute-start | bytes 1572872 | tf_op jit(solution)/shard_map/ppermute | solution.py:736
  84.0 334.1 %reduce-scatter.7.cloned.1.call-start = ((), (), s32[]{:S(2)}) async-start(), calls=%async_computation.6 | async-start | bytes 3932160 | tf_op jit(solution)/shard_map/reduce_scatter | solution.py:842
  87.4 2.2 copy-start.7
  101.2 117.1 %collective-permute-start.1 = (bf16[1536,1024]{0,1:T(8,128)(2,1)S(1)}, bf16[1536,1024]{0,1:T(8,128)(2,1)}, u32[]{:S(2)}, u32[]{:S(2)}) collective-permute-start(bf16[1536,1024]{0,1:T(8,128)(2,1)S(1)} %copy.228), channel_id=1, source_target_pairs={{0,4},{4,0},{1,5},{5,1},{2,6},{6,2},{3,7},{7,3},{8,12},{12,8},{9,1... | collective-permute-start | bytes 9437192 | tf_op jit(solution)/shard_map/ppermute | solution.py:736
  201.4 8.7 %copy-start.15 = (pred[3072,32]{1,0:T(32,128)(4,1)S(1)}, pred[3072,32]{1,0:T(32,128)(4,1)}, u32[]{:S(2)}) copy-start(pred[3072,32]{1,0:T(32,128)(4,1)} %copy.230) | copy-start | bytes 294916
  214.8 3.5 copy-start
  272.7 220.0 %reduce-scatter.11.cloned.1.call-start = ((), (), s32[]{:S(2)}) async-start(), calls=%async_computation.8 | async-start | bytes 3932160 | tf_op jit(solution)/shard_map/reduce_scatter | solution.py:842
  345.7 147.0 %reduce-scatter.9.cloned.1.call-start = ((), (), s32[]{:S(2)}) async-start(), calls=%async_computation.7 | async-start | bytes 3932160 | tf_op jit(solution)/shard_map/reduce_scatter | solution.py:842
  346.4 246.0 %reduce-scatter.13.cloned.1.call-start = ((), (), s32[]{:S(2)}) async-start(), calls=%async_computation.9 | async-start | bytes 3932160 | tf_op jit(solution)/shard_map/reduce_scatter | solution.py:842
  383.2 1.9 copy-start.38
  383.2 3.6 copy-start.39
  383.2 284.7 %reduce-scatter.15.cloned.1.call-start = ((), (), s32[]{:S(2)}) async-start(), calls=%async_computation.10 | async-start | bytes 7077888 | tf_op jit(solution)/shard_map/reduce_scatter | solution.py:894
  385.0 6.0 copy-start.42
  385.1 12.4 %slice-start = ((s8[6291456]{0:T(1024)(128)(4,1)}), s8[2097152]{0:T(1024)(128)(4,1)S(1)}, s32[]{:S(2)}) async-start(s8[6291456]{0:T(1024)(128)(4,1)} %bitcast.156), calls=%async_computation.18 | async-start | bytes 4194304
  388.4 3.2 copy-start.1
  391.7 5.8 slice-start.1
  397.5 1.9 copy-start.11
  417.6 273.0 %reduce-scatter.17.cloned.1.call-start = ((), (), s32[]{:S(2)}) async-start(), calls=%async_computation.12 | async-start | bytes 1966080 | tf_op jit(solution)/shard_map/reduce_scatter | solution.py:898
  418.1 74.6 %copy-start.49 = (bf16[4,256,256]{2,1,0:T(8,128)(2,1)S(1)}, bf16[4,256,256]{2,1,0:T(8,128)(2,1)}, u32[]{:S(2)}) copy-start(bf16[4,256,256]{2,1,0:T(8,128)(2,1)} %get-tuple-element.89) | copy-start | bytes 1572868
  495.7 3.1 copy-start.25
  495.7 3.8 copy-start.24
  497.5 64.1 %collective-permute-start.3 = (bf16[3,4,256,128]{3,2,1,0:T(8,128)(2,1)S(1)}, bf16[3,4,256,128]{3,2,1,0:T(8,128)(2,1)}, u32[]{:S(2)}, u32[]{:S(2)}) collective-permute-start(bf16[3,4,256,128]{3,2,1,0:T(8,128)(2,1)S(1)} %bitcast.184), channel_id=1, source_target_pairs={{0,4},{4,0},{1,5},{5,1},{2,6},{6,2},{3,7},{7,3},{8,12},{12,8},{9,1... | collective-permute-start | bytes 2359304 | tf_op jit(solution)/shard_map/ppermute | solution.py:736
  498.9 62.7 %collective-permute-start.4 = (bf16[3,4,256,128]{3,2,1,0:T(8,128)(2,1)S(1)}, bf16[3,4,256,128]{3,2,1,0:T(8,128)(2,1)}, u32[]{:S(2)}, u32[]{:S(2)}) collective-permute-start(bf16[3,4,256,128]{3,2,1,0:T(8,128)(2,1)S(1)} %bitcast.187), channel_id=1, source_target_pairs={{0,4},{4,0},{1,5},{5,1},{2,6},{6,2},{3,7},{7,3},{8,12},{12,8},{9,1... | collective-permute-start | bytes 2359304 | tf_op jit(solution)/shard_map/ppermute | solution.py:736
  499.5 62.1 %collective-permute-start.5 = (bf16[3,4,256,128]{3,2,1,0:T(8,128)(2,1)S(1)}, bf16[3,4,256,128]{3,2,1,0:T(8,128)(2,1)S(1)}, u32[]{:S(2)}, u32[]{:S(2)}) collective-permute-start(bf16[3,4,256,128]{3,2,1,0:T(8,128)(2,1)S(1)} %bitcast.186), channel_id=1, source_target_pairs={{0,4},{4,0},{1,5},{5,1},{2,6},{6,2},{3,7},{7,3},{8,12},{12,8},{9,1... | collective-permute-start | bytes 2359304 | tf_op jit(solution)/shard_map/ppermute | solution.py:736
  500.9 55.8 %copy-start.30 = (f32[32,1024]{1,0:T(8,128)S(1)}, f32[32,1024]{1,0:T(8,128)}, u32[]{:S(2)}) copy-start(f32[32,1024]{1,0:T(8,128)} %fusion.28) | copy-start | bytes 393220
  500.9 55.8 %copy-start.45 = (f32[1,1024]{1,0:T(1,128)S(1)}, f32[1,1024]{1,0:T(1,128)}, u32[]{:S(2)}) copy-start(f32[1,1024]{1,0:T(1,128)} %get-tuple-element.101) | copy-start | bytes 12292
  500.9 55.8 %copy-start.48 = (f32[40]{0:T(128)S(1)}, f32[40]{0:T(128)}, u32[]{:S(2)}) copy-start(f32[40]{0:T(128)} %pad.57.clone) | copy-start | bytes 484
  557.5 4.2 copy-start.10
  561.6 2.6 copy-start.9
  567.7 3.3 copy-start.3
  569.9 20.8 %collective-permute-start.6 = (bf16[1024,256]{1,0:T(8,128)(2,1)}, bf16[1024,256]{1,0:T(8,128)(2,1)}, u32[]{:S(2)}, u32[]{:S(2)}) collective-permute-start(bf16[1024,256]{1,0:T(8,128)(2,1)} %copy.263), channel_id=1, source_target_pairs={{0,4},{4,0},{1,5},{5,1},{2,6},{6,2},{3,7},{7,3},{8,12},{12,8},{9,1... | collective-permute-start | bytes 1572872 | tf_op jit(solution)/shard_map/ppermute | solution.py:736
  592.4 2.5 copy-start.2
  596.2 5.3 copy-start.5
  596.3 5.3 copy-start.44
  596.3 5.3 copy-start.47
  600.1 4.8 copy-start.31
  600.1 67.8 %collective-permute-start.7 = (bf16[3,4,256,128]{3,2,1,0:T(8,128)(2,1)}, bf16[3,4,256,128]{3,2,1,0:T(8,128)(2,1)}, u32[]{:S(2)}, u32[]{:S(2)}) collective-permute-start(bf16[3,4,256,128]{3,2,1,0:T(8,128)(2,1)} %bitcast.188), channel_id=1, source_target_pairs={{0,4},{4,0},{1,5},{5,1},{2,6},{6,2},{3,7},{7,3},{8,12},{12,8},{9,1... | collective-permute-start | bytes 2359304 | tf_op jit(solution)/shard_map/ppermute | solution.py:736
  604.9 1.8 copy-start.6
  608.0 97.2 %all-gather.12.cloned.1.call-start = ((), (), s32[]{:S(2)}) async-start(), calls=%async_computation.11 | async-start | bytes 3932160 | tf_op jit(solution)/shard_map/all_gather | solution.py:895
  608.1 59.9 %copy-start.14 = (f32[384,1024]{1,0:T(8,128)S(1)}, f32[384,1024]{1,0:T(8,128)}, u32[]{:S(2)}) copy-start(f32[384,1024]{1,0:T(8,128)} %get-tuple-element.104.refs_10_) | copy-start | bytes 4718596
  667.9 2.4 copy-start.23
  670.3 2.5 copy-start.26
  672.8 3.2 copy-start.28
  681.4 5.7 copy-start.20
  681.4 5.7 copy-start.21
  687.4 2.3 copy-start.41
  687.4 2.9 copy-start.17
  687.4 2.9 copy-start.18
  687.4 2.9 copy-start.19
  690.6 11.4 %collective-permute-start.8 = (bf16[256,768]{0,1:T(8,128)(2,1)}, bf16[256,768]{0,1:T(8,128)(2,1)S(1)}, u32[]{:S(2)}, u32[]{:S(2)}) collective-permute-start(bf16[256,768]{0,1:T(8,128)(2,1)} %reduce-scatter.17.cloned.1.call-done), channel_id=1, source_target_pairs={{0,4},{4,0},{1,5},{5,1},{2,6},{6,2},{3,7},{7,3},{8,12},{12,8},{9,1... | collective-permute-start | bytes 1179656 | tf_op jit(solution)/shard_map/ppermute | solution.py:736
  692.3 9.8 %copy-start.32 = (bf16[256,768]{0,1:T(8,128)(2,1)S(1)}, bf16[256,768]{0,1:T(8,128)(2,1)}, u32[]{:S(2)}) copy-start(bf16[256,768]{0,1:T(8,128)(2,1)} %reduce-scatter.17.cloned.1.call-done) | copy-start | bytes 1179652
  705.2 4.0 copy-start.8
  (9 other events, 9.1 us)
Sparse Core Ops, SparseCore 0:
  10.8 32.3 all-gather.13
  44.7 62.7 all-gather.15
  109.1 62.4 all-gather.17
  173.0 62.0 all-gather.19
  236.5 62.0 all-gather.21
  301.4 59.0 reduce-scatter.6
  362.7 60.2 reduce-scatter.10
  426.0 60.2 reduce-scatter.8
  488.6 60.3 reduce-scatter.12
  552.2 74.3 reduce-scatter.14
  629.4 36.2 reduce-scatter.16
  670.5 28.7 all-gather.11

commit v6 on v5

--- a/solution.py
+++ b/solution.py
@@ -713,6 +713,35 @@
     )(*gus, *ws, logit_grad, router_w, hidden, grad_own, gain)
 
 
+def place_body(ctx_ref, *refs, chunks, turned):
+    own_refs, other_refs, outs = refs[:chunks], refs[chunks : 2 * chunks], refs[2 * chunks :]
+    ctx = ctx_ref[0]
+    for chunk in range(chunks):
+        for half, piece in ((ctx, own_refs[chunk]), (1 - ctx, other_refs[chunk])):
+            for kind in range(3):
+                value = piece[kind, 0].astype(jnp.float32)
+                outs[kind][half, chunk, 0] = value.T if kind == 2 and turned else value
+
+
+def place_shards(ctx, own, other):
+    _, each, part, ff = own[0].shape
+    chunks = len(own)
+    turned = part % 128 == 0
+    shapes = [(part, ff), (part, ff), (ff, part) if turned else (part, ff)]
+    outs = pl.pallas_call(
+        functools.partial(place_body, chunks=chunks, turned=turned),
+        grid=(each,),
+        in_specs=[SMEMS] + [pl.BlockSpec((3, 1, part, ff), lambda e: (0, e, 0, 0))] * (2 * chunks),
+        out_specs=[pl.BlockSpec((2, chunks, 1, *shape), lambda e: (0, 0, e, 0, 0)) for shape in shapes],
+        out_shape=[jax.ShapeDtypeStruct((2, chunks, each, *shape), jnp.float32) for shape in shapes],
+        compiler_params=pltpu.CompilerParams(vmem_limit_bytes=VL),
+        cost_estimate=busy(8),
+        name="place_shards",
+    )(ctx.astype(jnp.int32).reshape(1), *own, *other)
+    gate, up, down = [out.reshape(2 * chunks * each, *out.shape[3:]) for out in outs]
+    return gate, up, down if turned else down.transpose(0, 2, 1)
+
+
 from jax.sharding import PartitionSpec as P
 
 rope_base = 10000.0
@@ -897,13 +926,7 @@
     big = jnp.concatenate([qkv_grad, out_w_grad], axis=1).astype(bf16)
     big = lax.psum_scatter(big, "fsdp", scatter_dimension=0, tiled=True)
     big = big.astype(f32) + swap(big).astype(f32)
-    gate_s, up_s, down_s = [
-        ordered(
-            jnp.concatenate([piece[kind] for piece in shard_grads]),
-            jnp.concatenate([piece[kind] for piece in there]),
-        ).astype(f32)
-        for kind in range(3)
-    ]
+    gate_s, up_s, down_s = place_shards(ctx, shard_grads, there)
     at = q_width + 2 * kv_width
     return (
         block_out,
@@ -917,7 +940,7 @@
         small_grads[:experts].T,
         gate_s,
         up_s,
-        down_s.transpose(0, 2, 1),
+        down_s,
     )
 
 

time: 727 us -> 720 us (level)
  local copies, waits for them, and re-layouts: 112 us -> 96.6 us
  Pallas kernels: 453 us -> 464 us
    unnamed x126 -> x105, local copies, waits for them, and re-layouts: 34.1 us -> 25.6 us
    squeeze x8 -> x0, local copies, waits for them, and re-layouts: 8.44 us -> none  [per_device(): piece[kind]]
    pallas_call x0 -> x1, Pallas kernels: none -> 8.27 us  [place_shards(): pl.pallas_call(functools.partial(place_body, chunks=chunks, turned=turned...]
  transfers between devices with their start and end apart: 21 -> 21, of which waited for: 3 -> 4; matrix products, arithmetic and copies ran while one was open for 25% -> 22% of each run, Pallas kernels for 63% -> 65%
where the time goes in v6:
time: 720 us; the launch traced here: 711 us
  Pallas kernels  464 us (64%)
  local copies, waits for them, and re-layouts  96.6 us (13%)
  other arithmetic  52.7 us (7%)
  waiting for transfers between devices  50.2 us (7%)
  matrix products  20.5 us (3%)
  between operations  15.4 us (2%)
  starting transfers between devices  12.2 us (2%)
    pallas_call x4, Pallas kernels, moe_main(): pl.pallas_call(moe_body, grid=(count // PAIR,), in_specs=[SMEMS, one(x.sh...  146 us
    pallas_call x1, Pallas kernels, mid(): pl.pallas_call(functools.partial(mid_body, share=heads // kv, length=leng...  98.9 us
    pallas_call x1, Pallas kernels, turn(): pl.pallas_call(functools.partial(turn_body, count=count, kinds=kinds, fir...  74.2 us
    pallas_call x1, Pallas kernels, tail(): pl.pallas_call(functools.partial(tail_body, shards=shards), in_specs=[WHO...  62 us
    pallas_call x1, Pallas kernels, flash_bwd(): pl.pallas_call(functools.partial(flash_bwd_body, share=heads // kv, lengt...  55.8 us
    unnamed x105, local copies, waits for them, and re-layouts  25.6 us
    all_gather x1, waiting for transfers between devices, per_device(): front = lax.all_gather(front, 'fsdp', axis=0)  22.9 us
    ppermute x9, waiting for transfers between devices, swap(): return lax.ppermute(x, 'ctx', [(0, 1), (1, 0)])  21 us
  transfers between devices with their start and end apart: 21, of which 4 were waited for; matrix products, arithmetic and copies ran while one was open for 22% of the time, Pallas kernels for 65%

profile of v6, /device:TPU:0, one launch (start us, length us, event | category | flops | bytes accessed | tf_op | source)
XLA Modules:
  0.0 711.3 jit_solution(11115114116287403220)
XLA Ops:
  8.9 1.7 pad_maximum_fusion.12
  10.7 1.3 constant_dynamic-slice_fusion.3
  12.7 2.5 dynamic-slice_bitcast_fusion
  18.1 2.2 pad_maximum_fusion.9
  20.2 22.9 %all-gather.14.cloned.1.call-done = bf16[1120,512]{1,0:T(8,128)(2,1)} async-done(((bf16[280,512]{1,0:T(8,128)(2,1)}), bf16[1120,512]{1,0:T(8,128)(2,1)}) %all-gather.14.cloned.1.call-update) | async-done | bytes 1146896 | tf_op jit(solution)/shard_map/all_gather | solution.py:803
  43.9 1.5 collective-permute-start.2
  46.9 1.4 fusion.12
  50.9 1.7 copy.219
  59.9 1.3 slice.82
  68.6 1.3 subtract_convert_fusion.3
  70.7 1.9 copy.216
  72.6 1.8 fusion.7
  75.0 2.3 fusion.10
  78.5 2.0 copy.256
  80.5 3.1 copy.255
  83.9 3.2 subtract_convert_fusion
  87.1 2.2 fusion.4.q_ref
  89.3 1.6 broadcast_select_fusion.3
  91.0 1.7 copy.217
  92.8 3.1 copy.218
  95.8 1.9 fusion.23
  97.7 3.2 copy.224
  100.9 1.6 collective-permute-start.1
  102.5 98.9 %mid.1 = (bf16[1536,256]{1,0:T(8,128)(2,1)}, f32[384,1024]{1,0:T(8,128)}, bf16[8,384,1024]{2,1,0:T(8,128)(2,1)}, bf16[4,256,256]{2,1,0:T(8,128)(2,1)}) custom-call(bf16[384,1024]{1,0:T(8,128)(2,1)} %constant_dynamic-slice_fusion.7.tok_ref, bf16[4,1536,64]{2,1,0:T(8,128)(2,1)} %fusion.4.q_ref, bf16[2,3072,64]{2,1,0:T(8,128)(2,1)} %get-tuple-element.191.k_ref, ...), custom_call_target="tpu_custom_call" | custom-call | flops 99999997952 | bytes 1048576 | tf_op jit(solution)/shard_map/mid/pallas_call | solution.py:452
  201.4 8.8 %copy.250 = bf16[3072,1024]{0,1:T(8,128)(2,1)} copy(bf16[3072,1024]{1,0:T(8,128)(2,1)} %bitcast.104) | data formatting | bytes 12582912 | tf_op jit(solution)/shard_map/reshape | solution.py:853
  210.2 4.7 fusion.27
  215.9 2.6 fusion.5.gates_ref
  218.5 2.3 broadcast_select_fusion.1
  220.8 5.1 fusion.21
  225.9 8.7 %copy.230.g_ref = bf16[3072,1024]{1,0:T(8,128)(2,1)} copy(bf16[3072,1024]{0,1:T(8,128)(2,1)} %get-tuple-element.187) | data formatting | bytes 12582912 | tf_op jit(solution)/shard_map/concatenate | solution.py:804
  235.9 37.0 %moe_main.4 = (bf16[3072,512]{1,0:T(8,128)(2,1)}, bf16[3072,1024]{1,0:T(8,128)(2,1)}, bf16[4,3,4,256,128]{4,3,2,1,0:T(8,128)(2,1)}, f32[3072,32]{1,0:T(8,128)}) custom-call(s32[1]{0:T(128)} %bitcast.27.base_ref, bf16[3072,1024]{1,0:T(8,128)(2,1)} %bitcast.106, bf16[3072,1024]{1,0:T(8,128)(2,1)} %copy.230.g_ref, ...), custom_call_target="tpu_custom_call", output_to_operand_aliasing={{3}: (6, {})} | custom-call | flops 19327352832 | bytes 31457280 | tf_op jit(solution)/shard_map/moe_main/pallas_call | solution.py:189
  273.2 36.4 %moe_main.5 = (bf16[3072,512]{1,0:T(8,128)(2,1)}, bf16[3072,1024]{1,0:T(8,128)(2,1)}, bf16[4,3,4,256,128]{4,3,2,1,0:T(8,128)(2,1)}, f32[3072,32]{1,0:T(8,128)}) custom-call(s32[1]{0:T(128)} %bitcast.32.base_ref, bf16[3072,1024]{1,0:T(8,128)(2,1)} %bitcast.107, bf16[3072,1024]{1,0:T(8,128)(2,1)} %copy.230.g_ref, ...), custom_call_target="tpu_custom_call", output_to_operand_aliasing={{3}: (6, {})} | custom-call | flops 19327352832 | bytes 31457280 | tf_op jit(solution)/shard_map/moe_main/pallas_call | solution.py:189
  309.6 36.4 %moe_main.6 = (bf16[3072,512]{1,0:T(8,128)(2,1)}, bf16[3072,1024]{1,0:T(8,128)(2,1)}, bf16[4,3,4,256,128]{4,3,2,1,0:T(8,128)(2,1)}, f32[3072,32]{1,0:T(8,128)}) custom-call(s32[1]{0:T(128)} %bitcast.34.base_ref, bf16[3072,1024]{1,0:T(8,128)(2,1)} %bitcast.108, bf16[3072,1024]{1,0:T(8,128)(2,1)} %copy.230.g_ref, ...), custom_call_target="tpu_custom_call", output_to_operand_aliasing={{3}: (6, {})} | custom-call | flops 19327352832 | bytes 31457280 | tf_op jit(solution)/shard_map/moe_main/pallas_call | solution.py:189
  346.4 36.4 %moe_main.7 = (bf16[3072,512]{1,0:T(8,128)(2,1)}, bf16[3072,1024]{1,0:T(8,128)(2,1)}, bf16[4,3,4,256,128]{4,3,2,1,0:T(8,128)(2,1)}, f32[3072,32]{1,0:T(8,128)}) custom-call(s32[1]{0:T(128)} %bitcast.36.base_ref, bf16[3072,1024]{1,0:T(8,128)(2,1)} %bitcast.109, bf16[3072,1024]{1,0:T(8,128)(2,1)} %copy.230.g_ref, ...), custom_call_target="tpu_custom_call", output_to_operand_aliasing={{3}: (6, {})} | custom-call | flops 19327352832 | bytes 31457280 | tf_op jit(solution)/shard_map/moe_main/pallas_call | solution.py:189
  384.7 1.7 copy.239.blkk_ref
  386.4 1.7 copy.238.dock_ref
  388.7 2.1 constant_dynamic-slice_fusion.2.refs_11_
  391.4 3.6 fusion.22
  395.0 2.1 subtract_convert_fusion.1.refs_8_
  397.2 1.9 fusion.28
  399.0 18.3 %moe_out.1 = bf16[3072,1024]{1,0:T(8,128)(2,1)} custom-call(bf16[3072,512]{1,0:T(8,128)(2,1)} %get-tuple-element.108.refs_0_, bf16[3072,512]{1,0:T(8,128)(2,1)} %get-tuple-element.109.refs_1_, bf16[3072,512]{1,0:T(8,128)(2,1)} %get-tuple-element.110.refs_2_, bf16[3072,512]{1,0:T(8,128)(2,1)} %get-tuple-element.111.refs_3_, ...), custom_call_target="tpu_custom_call" | custom-call | flops 12884901888 | bytes 12582912 | tf_op jit(solution)/shard_map/moe_out/pallas_call | solution.py:239
  417.9 74.2 %turn.1 = (bf16[4,384,1024]{2,1,0:T(8,128)(2,1)}, f32[384,1024]{1,0:T(8,128)}, f32[1,1024]{1,0:T(1,128)}) custom-call(bf16[3072,1024]{1,0:T(8,128)(2,1)} %get-tuple-element.73.refs_0_, bf16[3072,1024]{1,0:T(8,128)(2,1)} %get-tuple-element.76.refs_1_, bf16[3072,1024]{1,0:T(8,128)(2,1)} %get-tuple-element.79.refs_2_, ...), custom_call_target="tpu_custom_call" | custom-call | flops 74999996416 | bytes 1048576 | tf_op jit(solution)/shard_map/turn/pallas_call | solution.py:685
  492.1 2.9 convolution_convert_fusion
  495.1 1.7 copy.237
  500.1 55.8 %flash_bwd.1 = (f32[4,1536,64]{2,1,0:T(8,128)}, f32[2,3072,64]{2,1,0:T(8,128)}, f32[2,3072,64]{2,1,0:T(8,128)}) custom-call(s32[1]{0:T(128)} %bitcast.39.base_ref, bf16[4,1536,64]{2,1,0:T(8,128)(2,1)} %fusion.4.q_ref, bf16[4,1536,64]{2,1,0:T(8,128)(2,1)} %bitcast.126, bf16[2,3072,64]{2,1,0:T(8,128)(2,1)} %get-tuple-element.191.k_ref, ...), custom_call_target="tpu_custom_call" | custom-call | flops 54999998464 | bytes 1048576 | tf_op jit(solution)/shard_map/flash_bwd/pallas_call | solution.py:97
  556.6 4.2 convolution_convert_fusion.2
  561.7 1.7 copy-done.8
  564.3 2.4 copy.241
  569.9 2.1 multiply_bitcast_fusion
  572.0 2.3 copy.240
  575.7 13.1 %collective-permute-done.6 = bf16[1024,256]{1,0:T(8,128)(2,1)} collective-permute-done((bf16[1024,256]{1,0:T(8,128)(2,1)}, bf16[1024,256]{1,0:T(8,128)(2,1)}, u32[]{:S(2)}, u32[]{:S(2)}) %collective-permute-start.6) | collective-permute-done | bytes 524320 | tf_op jit(solution)/shard_map/ppermute | solution.py:765
  588.8 1.4 convert_add_fusion
  591.3 1.4 copy.244
  595.2 2.6 copy.245
  599.1 3.3 convolution_convert_fusion.1
  604.1 1.3 pad_maximum_fusion.3.lin_ref
  605.5 62.0 %tail.1 = (bf16[4,384,1024]{2,1,0:T(8,128)(2,1)}, f32[40,256]{1,0:T(8,128)}) custom-call(bf16[384,1024]{1,0:T(8,128)(2,1)} %constant_dynamic-slice_fusion.7.tok_ref, f32[384,1024]{1,0:T(8,128)} %get-tuple-element.86.hg_ref, bf16[1536,512]{1,0:T(8,128)(2,1)} %pad_maximum_fusion.3.lin_ref, bf16[1024,512]{1,0:T(8,128)(2,1)} %bitcast.133, f32[1,1024]{1,0:T(1,128)} %bitcast.151, ...), custom_call_target="tpu_custom_call" | custom-call | flops 49999998976 | bytes 1048576 | tf_op jit(solution)/shard_map/tail/pallas_call | solution.py:541
  667.6 2.3 add_convert_fusion.1
  669.9 8.3 %place_shards.1 = (f32[2,4,4,256,128]{4,3,2,1,0:T(8,128)}, f32[2,4,4,256,128]{4,3,2,1,0:T(8,128)}, f32[2,4,4,128,256]{4,3,2,1,0:T(8,128)}) custom-call(s32[1]{0:T(128)} %bitcast.60.ctx_ref, bf16[3,4,256,128]{3,2,1,0:T(8,128)(2,1)} %bitcast.166, bf16[3,4,256,128]{3,2,1,0:T(8,128)(2,1)} %bitcast.168, bf16[3,4,256,128]{3,2,1,0:T(8,128)(2,1)} %bitcast.170, ...), custom_call_target="tpu_custom_call" | custom-call | flops 8000000000 | bytes 1048576 | tf_op jit(solution)/shard_map/place_shards/pallas_call | solution.py:731
  678.2 1.5 collective-permute-start.8
  680.9 7.9 %collective-permute-done.8 = bf16[256,768]{0,1:T(8,128)(2,1)S(1)} collective-permute-done((bf16[256,768]{0,1:T(8,128)(2,1)}, bf16[256,768]{0,1:T(8,128)(2,1)S(1)}, u32[]{:S(2)}, u32[]{:S(2)}) %collective-permute-start.8) | collective-permute-done | bytes 393248 | tf_op jit(solution)/shard_map/ppermute | solution.py:765
  693.0 5.3 all-gather.12.cloned.1.call-done
  698.3 4.0 copy.274
  702.4 1.7 copy.275
  (200 shorter events, 56.5 us)
Async XLA Ops:
  7.2 35.9 %all-gather.14.cloned.1.call-start = ((), (), s32[]{:S(2)}) async-start(), calls=%async_computation.13 | async-start | bytes 1433600 | tf_op jit(solution)/shard_map/all_gather | solution.py:803
  10.6 224.0 %all-gather.16.cloned.1.call-start = ((), (), s32[]{:S(2)}) async-start(), calls=%async_computation.14 | async-start | bytes 3932160 | tf_op jit(solution)/shard_map/all_gather | solution.py:819
  18.0 27.5 %copy-start.3 = (bf16[1536,1024]{1,0:T(8,128)(2,1)S(1)}, bf16[1536,1024]{1,0:T(8,128)(2,1)}, u32[]{:S(2)}) copy-start(bf16[1536,1024]{1,0:T(8,128)(2,1)} %param.15) | copy-start | bytes 9437188
  43.1 230.0 %all-gather.18.cloned.1.call-start = ((), (), s32[]{:S(2)}) async-start(), calls=%async_computation.15 | async-start | bytes 3932160 | tf_op jit(solution)/shard_map/all_gather | solution.py:819
  43.9 265.8 %all-gather.20.cloned.1.call-start = ((), (), s32[]{:S(2)}) async-start(), calls=%async_computation.16 | async-start | bytes 3932160 | tf_op jit(solution)/shard_map/all_gather | solution.py:819
  43.9 13.4 %collective-permute-start.2 = (s32[1536,8]{0,1:T(8,128)}, s32[1536,8]{0,1:T(8,128)}, u32[]{:S(2)}, u32[]{:S(2)}) collective-permute-start(s32[1536,8]{0,1:T(8,128)} %param.19), channel_id=1, source_target_pairs={{0,4},{4,0},{1,5},{5,1},{2,6},{6,2},{3,7},{7,3},{8,12},{12,8},{9,1... | collective-permute-start | bytes 147464 | tf_op jit(solution)/shard_map/ppermute | solution.py:765
  45.5 300.9 %all-gather.22.cloned.1.call-start = ((), (), s32[]{:S(2)}) async-start(), calls=%async_computation.17 | async-start | bytes 3932160 | tf_op jit(solution)/shard_map/all_gather | solution.py:819
  48.3 9.0 %copy-start.11 = (f32[1536,32]{0,1:T(8,128)}, f32[1536,32]{0,1:T(8,128)S(1)}, u32[]{:S(2)}) copy-start(f32[1536,32]{0,1:T(8,128)S(1)} %get-tuple-element.225) | copy-start | bytes 589828
  48.3 9.0 %copy-start.13 = (f32[1536,32]{0,1:T(8,128)}, f32[1536,32]{0,1:T(8,128)S(1)}, u32[]{:S(2)}) copy-start(f32[1536,32]{0,1:T(8,128)S(1)} %get-tuple-element.224) | copy-start | bytes 589828
  50.1 9.8 %copy-start.22 = (s32[1536]{0:T(1024)}, s32[1536]{0:T(1024)S(1)}, u32[]{:S(2)}) copy-start(s32[1536]{0:T(1024)S(1)} %dynamic_slice.71) | copy-start | bytes 18436
  50.9 9.0 %copy-start.20 = (s32[1536]{0:T(1024)}, s32[1536]{0:T(1024)S(1)}, u32[]{:S(2)}) copy-start(s32[1536]{0:T(1024)S(1)} %dynamic_slice.72) | copy-start | bytes 18436
  57.3 5.6 copy-start.28
  61.2 3.0 copy-start.16
  62.9 12.1 %copy-start.32 = (f32[1,2,4,128]{3,1,2,0:T(2,128)}, f32[1,2,4,128]{3,1,2,0:T(2,128)S(1)}, u32[]{:S(2)}) copy-start(f32[1,2,4,128]{3,1,2,0:T(2,128)S(1)} %copy.264) | copy-start | bytes 12292
  68.6 6.4 copy-start.29
  74.5 14.8 %collective-permute-start = (bf16[1024,256]{1,0:T(8,128)(2,1)}, bf16[1024,256]{1,0:T(8,128)(2,1)}, u32[]{:S(2)}, u32[]{:S(2)}) collective-permute-start(bf16[1024,256]{1,0:T(8,128)(2,1)} %fusion.7), channel_id=1, source_target_pairs={{0,4},{4,0},{1,5},{5,1},{2,6},{6,2},{3,7},{7,3},{8,12},{12,8},{9,1... | collective-permute-start | bytes 1572872 | tf_op jit(solution)/shard_map/ppermute | solution.py:765
  83.7 334.2 %reduce-scatter.7.cloned.1.call-start = ((), (), s32[]{:S(2)}) async-start(), calls=%async_computation.6 | async-start | bytes 3932160 | tf_op jit(solution)/shard_map/reduce_scatter | solution.py:871
  87.1 2.2 copy-start.6
  100.9 117.5 %collective-permute-start.1 = (bf16[1536,1024]{0,1:T(8,128)(2,1)S(1)}, bf16[1536,1024]{0,1:T(8,128)(2,1)}, u32[]{:S(2)}, u32[]{:S(2)}) collective-permute-start(bf16[1536,1024]{0,1:T(8,128)(2,1)S(1)} %copy.224), channel_id=1, source_target_pairs={{0,4},{4,0},{1,5},{5,1},{2,6},{6,2},{3,7},{7,3},{8,12},{12,8},{9,1... | collective-permute-start | bytes 9437192 | tf_op jit(solution)/shard_map/ppermute | solution.py:765
  201.4 8.8 %copy-start.15 = (pred[3072,32]{1,0:T(32,128)(4,1)S(1)}, pred[3072,32]{1,0:T(32,128)(4,1)}, u32[]{:S(2)}) copy-start(pred[3072,32]{1,0:T(32,128)(4,1)} %copy.226) | copy-start | bytes 294916
  215.0 3.5 copy-start
  272.9 219.1 %reduce-scatter.9.cloned.1.call-start = ((), (), s32[]{:S(2)}) async-start(), calls=%async_computation.7 | async-start | bytes 3932160 | tf_op jit(solution)/shard_map/reduce_scatter | solution.py:871
  309.6 182.5 %reduce-scatter.11.cloned.1.call-start = ((), (), s32[]{:S(2)}) async-start(), calls=%async_computation.8 | async-start | bytes 3932160 | tf_op jit(solution)/shard_map/reduce_scatter | solution.py:871
  346.1 244.2 %reduce-scatter.13.cloned.1.call-start = ((), (), s32[]{:S(2)}) async-start(), calls=%async_computation.9 | async-start | bytes 3932160 | tf_op jit(solution)/shard_map/reduce_scatter | solution.py:871
  382.8 0.7 copy-start.23
  382.8 1.3 copy-start.21
  382.8 1.9 copy-start.24
  382.9 3.6 copy-start.25
  382.9 284.7 %reduce-scatter.15.cloned.1.call-start = ((), (), s32[]{:S(2)}) async-start(), calls=%async_computation.10 | async-start | bytes 7077888 | tf_op jit(solution)/shard_map/reduce_scatter | solution.py:923
  384.7 6.0 copy-start.27
  384.7 12.4 %slice-start = ((s8[6291456]{0:T(1024)(128)(4,1)}), s8[2097152]{0:T(1024)(128)(4,1)S(1)}, s32[]{:S(2)}) async-start(s8[6291456]{0:T(1024)(128)(4,1)} %bitcast.110), calls=%async_computation.18 | async-start | bytes 4194304
  388.1 3.3 copy-start.1
  391.4 5.8 slice-start.1
  397.1 1.9 copy-start.10
  417.4 260.8 %reduce-scatter.17.cloned.1.call-start = ((), (), s32[]{:S(2)}) async-start(), calls=%async_computation.12 | async-start | bytes 1966080 | tf_op jit(solution)/shard_map/reduce_scatter | solution.py:927
  417.9 74.3 %copy-start.39 = (bf16[4,256,256]{2,1,0:T(8,128)(2,1)S(1)}, bf16[4,256,256]{2,1,0:T(8,128)(2,1)}, u32[]{:S(2)}) copy-start(bf16[4,256,256]{2,1,0:T(8,128)(2,1)} %get-tuple-element.92) | copy-start | bytes 1572868
  495.0 1.8 copy-start.35
  495.0 3.0 copy-start.36
  495.1 3.8 copy-start.37
  496.8 64.0 %collective-permute-start.3 = (bf16[3,4,256,128]{3,2,1,0:T(8,128)(2,1)S(1)}, bf16[3,4,256,128]{3,2,1,0:T(8,128)(2,1)S(1)}, u32[]{:S(2)}, u32[]{:S(2)}) collective-permute-start(bf16[3,4,256,128]{3,2,1,0:T(8,128)(2,1)S(1)} %bitcast.167), channel_id=1, source_target_pairs={{0,4},{4,0},{1,5},{5,1},{2,6},{6,2},{3,7},{7,3},{8,12},{12,8},{9,1... | collective-permute-start | bytes 2359304 | tf_op jit(solution)/shard_map/ppermute | solution.py:765
  498.1 62.8 %collective-permute-start.4 = (bf16[3,4,256,128]{3,2,1,0:T(8,128)(2,1)S(1)}, bf16[3,4,256,128]{3,2,1,0:T(8,128)(2,1)}, u32[]{:S(2)}, u32[]{:S(2)}) collective-permute-start(bf16[3,4,256,128]{3,2,1,0:T(8,128)(2,1)S(1)} %bitcast.169), channel_id=1, source_target_pairs={{0,4},{4,0},{1,5},{5,1},{2,6},{6,2},{3,7},{7,3},{8,12},{12,8},{9,1... | collective-permute-start | bytes 2359304 | tf_op jit(solution)/shard_map/ppermute | solution.py:765
  498.8 62.0 %collective-permute-start.5 = (bf16[3,4,256,128]{3,2,1,0:T(8,128)(2,1)S(1)}, bf16[3,4,256,128]{3,2,1,0:T(8,128)(2,1)}, u32[]{:S(2)}, u32[]{:S(2)}) collective-permute-start(bf16[3,4,256,128]{3,2,1,0:T(8,128)(2,1)S(1)} %bitcast.171), channel_id=1, source_target_pairs={{0,4},{4,0},{1,5},{5,1},{2,6},{6,2},{3,7},{7,3},{8,12},{12,8},{9,1... | collective-permute-start | bytes 2359304 | tf_op jit(solution)/shard_map/ppermute | solution.py:765
  500.1 55.8 %copy-start.18 = (f32[32,1024]{1,0:T(8,128)S(1)}, f32[32,1024]{1,0:T(8,128)}, u32[]{:S(2)}) copy-start(f32[32,1024]{1,0:T(8,128)} %fusion.28) | copy-start | bytes 393220
  500.1 55.8 %copy-start.31 = (f32[1,1024]{1,0:T(1,128)S(1)}, f32[1,1024]{1,0:T(1,128)}, u32[]{:S(2)}) copy-start(f32[1,1024]{1,0:T(1,128)} %get-tuple-element.104) | copy-start | bytes 12292
  500.1 55.8 %copy-start.34 = (f32[40]{0:T(128)S(1)}, f32[40]{0:T(128)}, u32[]{:S(2)}) copy-start(f32[40]{0:T(128)} %pad.27.clone) | copy-start | bytes 484
  556.6 4.2 copy-start.9
  560.8 0.9 copy-start.38
  560.9 2.6 copy-start.8
  568.8 20.0 %collective-permute-start.6 = (bf16[1024,256]{1,0:T(8,128)(2,1)}, bf16[1024,256]{1,0:T(8,128)(2,1)}, u32[]{:S(2)}, u32[]{:S(2)}) collective-permute-start(bf16[1024,256]{1,0:T(8,128)(2,1)} %copy.258), channel_id=1, source_target_pairs={{0,4},{4,0},{1,5},{5,1},{2,6},{6,2},{3,7},{7,3},{8,12},{12,8},{9,1... | collective-permute-start | bytes 1572872 | tf_op jit(solution)/shard_map/ppermute | solution.py:765
  590.2 2.4 copy-start.2
  592.7 0.9 copy-start.12
  592.7 1.0 copy-start.17
  594.1 5.0 copy-start.4
  594.1 5.0 copy-start.30
  594.1 4.9 copy-start.33
  597.9 4.5 copy-start.19
  597.9 69.7 %collective-permute-start.7 = (bf16[3,4,256,128]{3,2,1,0:T(8,128)(2,1)}, bf16[3,4,256,128]{3,2,1,0:T(8,128)(2,1)}, u32[]{:S(2)}, u32[]{:S(2)}) collective-permute-start(bf16[3,4,256,128]{3,2,1,0:T(8,128)(2,1)} %bitcast.172), channel_id=1, source_target_pairs={{0,4},{4,0},{1,5},{5,1},{2,6},{6,2},{3,7},{7,3},{8,12},{12,8},{9,1... | collective-permute-start | bytes 2359304 | tf_op jit(solution)/shard_map/ppermute | solution.py:765
  602.4 1.8 copy-start.5
  605.5 92.9 %all-gather.12.cloned.1.call-start = ((), (), s32[]{:S(2)}) async-start(), calls=%async_computation.11 | async-start | bytes 3932160 | tf_op jit(solution)/shard_map/all_gather | solution.py:924
  605.5 62.1 %copy-start.14 = (f32[384,1024]{1,0:T(8,128)S(1)}, f32[384,1024]{1,0:T(8,128)}, u32[]{:S(2)}) copy-start(f32[384,1024]{1,0:T(8,128)} %get-tuple-element.107.refs_10_) | copy-start | bytes 4718596
  669.9 9.8 %copy-start.26 = (f32[40,256]{1,0:T(8,128)S(1)}, f32[40,256]{1,0:T(8,128)}, u32[]{:S(2)}) copy-start(f32[40,256]{1,0:T(8,128)} %get-tuple-element.113) | copy-start | bytes 122884
  678.2 10.6 %collective-permute-start.8 = (bf16[256,768]{0,1:T(8,128)(2,1)}, bf16[256,768]{0,1:T(8,128)(2,1)S(1)}, u32[]{:S(2)}, u32[]{:S(2)}) collective-permute-start(bf16[256,768]{0,1:T(8,128)(2,1)} %reduce-scatter.17.cloned.1.call-done), channel_id=1, source_target_pairs={{0,4},{4,0},{1,5},{5,1},{2,6},{6,2},{3,7},{7,3},{8,12},{12,8},{9,1... | collective-permute-start | bytes 1179656 | tf_op jit(solution)/shard_map/ppermute | solution.py:765
  698.3 4.0 copy-start.7
Sparse Core Ops, SparseCore 0:
  10.8 32.3 all-gather.13
  44.7 62.8 all-gather.15
  109.1 62.1 all-gather.17
  172.7 62.0 all-gather.19
  236.2 62.0 all-gather.21
  301.1 59.0 reduce-scatter.6
  363.1 60.3 reduce-scatter.8
  425.7 60.2 reduce-scatter.10
  488.4 60.3 reduce-scatter.12
  551.9 74.2 reduce-scatter.14
  629.1 35.9 reduce-scatter.16
  670.0 28.2 all-gather.11
